TPU v7x, 32 devices: a whole 2x2x4 slice. The times are simulated.
32 devices in a mesh: ctx: 8 (over z, y), wa: 4 (over x, core).
Axes of the slice: x: 2, y: 2, z: 4, core: 2. Of those that a mesh axis runs over, the one named last changes fastest.
Arguments:
- tokens: bfloat16 [4, 8, 2, 128, 1536], P('wa', 'ctx'), may hold values from -6 to 6
- doc_starts: int32 [4, 8], P('wa'), may hold values from 0 to 2047, as said below
- routes: int32 [4, 8, 2, 128, 6], P('wa', 'ctx'), may hold values from 0 to 15, all different within a row; in each aligned block of 256 rows (0 to 255, 256 to 511, ..., all dimensions but the last counted through in order) at most 192 rows name the same one
- norm_gain_1: bfloat16 [1536], P('wa'), may hold values from 0.5 to 1.5
- query_weight: bfloat16 [1536, 1536], P('wa'), may hold values from -0.21875 to 0.21875
- key_matrix: bfloat16 [1536, 512], P('wa'), may hold values from -0.21875 to 0.21875
- value_matrix: bfloat16 [1536, 512], P('wa'), may hold values from -0.15625 to 0.15625
- out_weight: bfloat16 [1536, 1536], P(None, 'wa'), may hold values from -2 to 2
- norm_gain_2: bfloat16 [1536], P('wa'), may hold values from 0.5 to 1.5
- router_weight: bfloat16 [1536, 16], P('wa'), may hold values from -0.078125 to 0.078125
- shared_gate: bfloat16 [1536, 1024], P('wa'), may hold values from -0.15625 to 0.15625
- shared_up: bfloat16 [1536, 1024], P('wa'), may hold values from -0.15625 to 0.15625
- shared_down: bfloat16 [1024, 1536], P(None, 'wa'), may hold values from -0.375 to 0.375
- expert_gate: bfloat16 [16, 1536, 512], P('wa'), may hold values from -0.15625 to 0.15625
- expert_up: bfloat16 [16, 1536, 512], P('wa'), may hold values from -0.15625 to 0.15625
- expert_down: bfloat16 [16, 512, 1536], P('wa'), may hold values from -0.75 to 0.75
- out_grad: bfloat16 [4, 8, 2, 128, 1536], P('wa', 'ctx'), may hold values from -6 to 6
Outputs:
- block_out: bfloat16 [4, 8, 2, 128, 1536], P('wa', 'ctx')
- tokens_grad: bfloat16 [4, 8, 2, 128, 1536], P('wa', 'ctx')
- norm_gain_1_grad: float32 [1536], P(('ctx', 'wa'))
- query_weight_grad: float32 [1536, 1536], P(('ctx', 'wa'))
- key_weight_grad: float32 [1536, 512], P(('ctx', 'wa'))
- value_weight_grad: float32 [1536, 512], P(('ctx', 'wa'))
- out_weight_grad: float32 [1536, 1536], P(None, ('ctx', 'wa'))
- norm_gain_2_grad: float32 [1536], P(('ctx', 'wa'))
- router_weight_grad: float32 [1536, 16], P(('ctx', 'wa'))
- shared_gate_grad: float32 [1536, 1024], P(('ctx', 'wa'))
- shared_up_grad: float32 [1536, 1024], P(('ctx', 'wa'))
- shared_down_grad: float32 [1024, 1536], P(None, ('ctx', 'wa'))
- expert_gate_grad: float32 [16, 1536, 512], P('wa', 'ctx')
- expert_up_grad: float32 [16, 1536, 512], P('wa', 'ctx')
- expert_down_grad: float32 [16, 512, 1536], P('wa', None, 'ctx')
Inputs may be any that keep to these rules, and one draw needn't show every extreme that they name: doc_starts[s, 0] is 0 and each row rises strictly; the 8 documents of a stream (the last one ending at the stream's end) have 1 to 1024 tokens, and one of them has exactly 1024. `routes`: the 6 experts of a token are different; among the 256 tokens of one device no expert is chosen more than 192 times, and in every draw some device chooses some expert exactly 192 times.
All inputs are finite; a program needn't handle non-finite values.
Results may differ from a plain program's by a relative error of at most 0.018.
The roundings to bfloat16 on the way count: a program that leaves them out, or rounds other values in their place, can miss the bound.
Values may be sent and summed in bfloat16 or wider, within the bound.
No kernel may reach another device: no remote copies, remote signals or barrier semaphores. Data moves between devices by JAX's collectives and lax.ppermute only.
A program may use at most 320 MiB of HBM per device.

v0:
```python
import jax
import jax.numpy as jnp
from jax import lax
from jax.sharding import PartitionSpec as P

QUERY_HEADS = 12
KEY_VALUE_HEADS = 4
HEAD_DIM = 128
TOP = 6
EXPERTS = 16
MOST = 192


epsilon = 1e-05
large_negative = -1e30
highest = lax.Precision.HIGHEST


def silu_parts(values):
    sigmoid_of = jax.nn.sigmoid(values)
    return (values * sigmoid_of, sigmoid_of * (1.0 + values * (1.0 - sigmoid_of)))


def device_positions(device_index, half_rows, stream_rows):
    offsets = jnp.arange(half_rows, dtype=jnp.int32)
    return jnp.concatenate(
        [device_index * half_rows + offsets, stream_rows - (device_index + 1) * half_rows + offsets]
    )


def segment_of(positions, starts):
    return jnp.sum((starts[1:][None, :] <= positions[:, None]).astype(jnp.int32), axis=1)


def heads_first(square_matrix, heads_ratio):
    nearby_rows = square_matrix.shape[0]
    return (
        square_matrix.reshape(nearby_rows, KEY_VALUE_HEADS, heads_ratio, HEAD_DIM)
        .transpose(1, 2, 0, 3)
        .reshape(KEY_VALUE_HEADS, heads_ratio * nearby_rows, HEAD_DIM)
    )


def rows_first(square_matrix, heads_ratio):
    nearby_rows = square_matrix.shape[1] // heads_ratio
    return (
        square_matrix.reshape(KEY_VALUE_HEADS, heads_ratio, nearby_rows, HEAD_DIM)
        .transpose(2, 0, 1, 3)
        .reshape(nearby_rows, KEY_VALUE_HEADS * heads_ratio * HEAD_DIM)
    )


def rms_back(grad_normed, normed, inverse, gain_values):
    scaled = grad_normed * gain_values
    return (
        jnp.sum(grad_normed * normed, axis=0),
        inverse * (scaled - normed * jnp.mean(scaled * normed, axis=-1, keepdims=True)),
    )


def shards(
    tokens,
    doc_starts,
    routes,
    norm_gain_1,
    query_weight,
    key_matrix,
    value_matrix,
    out_weight,
    norm_gain_2,
    router_weight,
    shared_gate,
    shared_up,
    shared_down,
    expert_gate,
    expert_up,
    expert_down,
    out_grad,
):
    context_count = lax.axis_size("ctx")
    wa_count = lax.axis_size("wa")
    device_index = lax.axis_index("ctx")
    half_rows = tokens.shape[3]
    model_width = tokens.shape[4]
    nearby_rows = 2 * half_rows
    stream_rows = context_count * nearby_rows
    heads_ratio = QUERY_HEADS // KEY_VALUE_HEADS
    score_scale = HEAD_DIM ** (-0.5)
    expert_local = expert_gate.shape[0]
    inputs = tokens.reshape(nearby_rows, model_width).astype(jnp.float32)
    starts = doc_starts[0]
    query_pos = device_positions(device_index, half_rows, stream_rows)
    row_pos = jnp.tile(query_pos, heads_ratio)
    row_seg = jnp.tile(segment_of(query_pos, starts), heads_ratio)
    all_pos = jax.vmap(lambda peer_index: device_positions(peer_index, half_rows, stream_rows))(
        jnp.arange(context_count, dtype=jnp.int32)
    )
    key_pos = all_pos.reshape(context_count // 2, 2 * nearby_rows)
    key_seg = segment_of(all_pos.reshape(-1), starts).reshape(context_count // 2, 2 * nearby_rows)
    (
        gain_one,
        query_full,
        key_full,
        value_full,
        out_full,
        gain_two,
        router_full,
        gate_full,
        up_full,
        down_full,
    ) = (
        lax.all_gather(norm_gain_1, "wa", axis=0, tiled=True),
        lax.all_gather(query_weight, "wa", axis=0, tiled=True),
        lax.all_gather(key_matrix, "wa", axis=0, tiled=True),
        lax.all_gather(value_matrix, "wa", axis=0, tiled=True),
        lax.all_gather(out_weight, "wa", axis=1, tiled=True),
        lax.all_gather(norm_gain_2, "wa", axis=0, tiled=True),
        lax.all_gather(router_weight, "wa", axis=0, tiled=True),
        lax.all_gather(shared_gate, "wa", axis=0, tiled=True),
        lax.all_gather(shared_up, "wa", axis=0, tiled=True),
        lax.all_gather(shared_down, "wa", axis=1, tiled=True),
    )
    gain_one = gain_one.astype(jnp.float32)
    gain_two = gain_two.astype(jnp.float32)
    inverse_one = lax.rsqrt(jnp.mean(inputs * inputs, axis=-1, keepdims=True) + epsilon)
    normed_one = inputs * inverse_one
    normed_low = (normed_one * gain_one).astype(jnp.bfloat16)
    query_projected = jnp.dot(normed_low, query_full, preferred_element_type=jnp.float32).astype(
        jnp.bfloat16
    )
    key_projected = jnp.dot(normed_low, key_full, preferred_element_type=jnp.float32).astype(
        jnp.bfloat16
    )
    value_projected = jnp.dot(normed_low, value_full, preferred_element_type=jnp.float32).astype(
        jnp.bfloat16
    )
    every_key, every_value = (
        lax.all_gather(key_projected[None], "ctx", axis=0, tiled=True),
        lax.all_gather(value_projected[None], "ctx", axis=0, tiled=True),
    )
    grouped_keys = every_key.reshape(context_count // 2, 2 * nearby_rows, KEY_VALUE_HEADS, HEAD_DIM)
    grouped_values = every_value.reshape(
        context_count // 2, 2 * nearby_rows, KEY_VALUE_HEADS, HEAD_DIM
    )
    query_heads = heads_first(query_projected, heads_ratio)

    def scores_of(key_block, pos_block, seg_block):
        scores = (
            jnp.einsum("grd,kgd->grk", query_heads, key_block, preferred_element_type=jnp.float32)
            * score_scale
        )
        allowed = (pos_block[None, :] <= row_pos[:, None]) & (
            seg_block[None, :] == row_seg[:, None]
        )
        return (jnp.where(allowed[None], scores, large_negative), allowed)

    def stats_step(carry, block_items):
        running_max, running_sum = carry
        key_block, pos_block, seg_block = block_items
        scores, allowed = scores_of(key_block, pos_block, seg_block)
        new_max = jnp.maximum(running_max, jnp.max(scores, axis=-1))
        expo = jnp.where(allowed[None], jnp.exp(scores - new_max[..., None]), 0.0)
        return (
            (new_max, running_sum * jnp.exp(running_max - new_max) + jnp.sum(expo, axis=-1)),
            None,
        )

    stats_init = (
        jnp.full((KEY_VALUE_HEADS, heads_ratio * nearby_rows), large_negative, jnp.float32),
        jnp.zeros((KEY_VALUE_HEADS, heads_ratio * nearby_rows), jnp.float32),
    )
    (row_max, row_sum), _ = lax.scan(stats_step, stats_init, (grouped_keys, key_pos, key_seg))

    def probs_of(scores, allowed):
        return (
            jnp.where(allowed[None], jnp.exp(scores - row_max[..., None]), 0.0) / row_sum[..., None]
        )

    def value_step(accum, block_items):
        key_block, value_block, pos_block, seg_block = block_items
        scores, allowed = scores_of(key_block, pos_block, seg_block)
        weights_low = probs_of(scores, allowed).astype(jnp.bfloat16)
        return (
            accum
            + jnp.einsum(
                "grk,kgd->grd", weights_low, value_block, preferred_element_type=jnp.float32
            ),
            None,
        )

    attended_rows, _ = lax.scan(
        value_step,
        jnp.zeros((KEY_VALUE_HEADS, heads_ratio * nearby_rows, HEAD_DIM), jnp.float32),
        (grouped_keys, grouped_values, key_pos, key_seg),
    )
    attended_low = rows_first(attended_rows, heads_ratio).astype(jnp.bfloat16)
    residual = inputs + jnp.dot(attended_low, out_full, preferred_element_type=jnp.float32)
    inverse_two = lax.rsqrt(jnp.mean(residual * residual, axis=-1, keepdims=True) + epsilon)
    normed_two = residual * inverse_two
    second_low = (normed_two * gain_two).astype(jnp.bfloat16)
    logits = jnp.dot(second_low, router_full, preferred_element_type=jnp.float32)
    route_rows = routes.reshape(nearby_rows, TOP)
    choose_table = (route_rows[..., None] == jnp.arange(EXPERTS, dtype=jnp.int32)).astype(
        jnp.float32
    )
    chosen = jnp.einsum("te,tke->tk", logits, choose_table, precision=highest)
    gate_expo = jnp.exp(chosen - jnp.max(chosen, axis=-1, keepdims=True))
    gates = gate_expo / jnp.sum(gate_expo, axis=-1, keepdims=True)
    shared_gate_pre = jnp.dot(second_low, gate_full, preferred_element_type=jnp.float32)
    shared_up_pre = jnp.dot(second_low, up_full, preferred_element_type=jnp.float32)
    shared_silu, shared_slope = silu_parts(shared_gate_pre)
    shared_hidden = (shared_silu * shared_up_pre).astype(jnp.bfloat16)
    shared_out = jnp.dot(shared_hidden, down_full, preferred_element_type=jnp.float32)
    flat_ids = route_rows.reshape(-1)
    one_hot = (flat_ids[:, None] == jnp.arange(EXPERTS, dtype=jnp.int32)[None, :]).astype(jnp.int32)
    rank_in_expert = jnp.sum((jnp.cumsum(one_hot, axis=0) - 1) * one_hot, axis=1)
    slot_index = flat_ids * MOST + rank_in_expert
    owner_rows = jnp.arange(nearby_rows * TOP, dtype=jnp.int32) // TOP

    def to_slots(slot_values):
        return (
            jnp.zeros((EXPERTS * MOST, model_width), jnp.bfloat16)
            .at[slot_index]
            .set(slot_values)
            .reshape(wa_count, expert_local, MOST, model_width)
        )

    arrived = lax.all_to_all(
        to_slots(second_low[owner_rows]), "wa", split_axis=0, concat_axis=0, tiled=True
    )
    gate_pre = jnp.einsum(
        "semd,edf->semf", arrived, expert_gate, preferred_element_type=jnp.float32
    )
    up_pre = jnp.einsum("semd,edf->semf", arrived, expert_up, preferred_element_type=jnp.float32)
    expert_silu, expert_slope = silu_parts(gate_pre)
    expert_hidden = (expert_silu * up_pre).astype(jnp.bfloat16)
    produced = jnp.einsum(
        "semf,efd->semd", expert_hidden, expert_down, preferred_element_type=jnp.float32
    ).astype(jnp.bfloat16)
    returned = lax.all_to_all(produced, "wa", split_axis=0, concat_axis=0, tiled=True).reshape(
        EXPERTS * MOST, model_width
    )
    picked = returned[slot_index].reshape(nearby_rows, TOP, model_width)
    mixture = jnp.sum(gates[:, :, None] * picked, axis=1)
    block_out = (residual + shared_out + mixture).astype(jnp.bfloat16).reshape(tokens.shape)
    grad_low = out_grad.reshape(nearby_rows, model_width)
    grad_rows = grad_low.astype(jnp.float32)
    gate_grad = jnp.sum(grad_rows[:, None, :] * picked, axis=-1)
    slot_grad = (
        (gates[:, :, None] * grad_rows[:, None, :])
        .astype(jnp.bfloat16)
        .reshape(nearby_rows * TOP, model_width)
    )
    sent_grad = lax.all_to_all(to_slots(slot_grad), "wa", split_axis=0, concat_axis=0, tiled=True)
    hidden_grad = jnp.einsum(
        "semd,efd->semf", sent_grad, expert_down, preferred_element_type=jnp.float32
    )
    gate_low = (hidden_grad * up_pre * expert_slope).astype(jnp.bfloat16)
    up_low = (hidden_grad * expert_silu).astype(jnp.bfloat16)
    down_term = jnp.einsum(
        "semf,semd->efd", expert_hidden, sent_grad, preferred_element_type=jnp.float32
    )
    gate_term = jnp.einsum("semd,semf->edf", arrived, gate_low, preferred_element_type=jnp.float32)
    up_term = jnp.einsum("semd,semf->edf", arrived, up_low, preferred_element_type=jnp.float32)
    input_slots = (
        jnp.einsum("semf,edf->semd", gate_low, expert_gate, preferred_element_type=jnp.float32)
        + jnp.einsum("semf,edf->semd", up_low, expert_up, preferred_element_type=jnp.float32)
    ).astype(jnp.bfloat16)
    back_slots = lax.all_to_all(input_slots, "wa", split_axis=0, concat_axis=0, tiled=True).reshape(
        EXPERTS * MOST, model_width
    )
    expert_input_grad = jnp.sum(
        back_slots[slot_index].reshape(nearby_rows, TOP, model_width).astype(jnp.float32), axis=1
    )
    expert_gate_grad, expert_up_grad, expert_down_grad = (
        lax.psum_scatter(
            gate_term.astype(jnp.bfloat16), "ctx", scatter_dimension=1, tiled=True
        ).astype(jnp.float32),
        lax.psum_scatter(
            up_term.astype(jnp.bfloat16), "ctx", scatter_dimension=1, tiled=True
        ).astype(jnp.float32),
        lax.psum_scatter(
            down_term.astype(jnp.bfloat16), "ctx", scatter_dimension=2, tiled=True
        ).astype(jnp.float32),
    )
    chosen_grad = gates * (gate_grad - jnp.sum(gates * gate_grad, axis=-1, keepdims=True))
    logit_grad = jnp.einsum("tk,tke->te", chosen_grad, choose_table, precision=highest)
    shared_hidden_grad = jnp.dot(grad_low, down_full.T, preferred_element_type=jnp.float32)
    shared_gate_low = (shared_hidden_grad * shared_up_pre * shared_slope).astype(jnp.bfloat16)
    shared_up_low = (shared_hidden_grad * shared_silu).astype(jnp.bfloat16)
    shared_down_term = jnp.dot(shared_hidden.T, grad_low, preferred_element_type=jnp.float32)
    shared_gate_term = jnp.dot(second_low.T, shared_gate_low, preferred_element_type=jnp.float32)
    shared_up_term = jnp.dot(second_low.T, shared_up_low, preferred_element_type=jnp.float32)
    router_term = jnp.dot(second_low.astype(jnp.float32).T, logit_grad, precision=highest)
    second_grad = (
        jnp.dot(shared_gate_low, gate_full.T, preferred_element_type=jnp.float32)
        + jnp.dot(shared_up_low, up_full.T, preferred_element_type=jnp.float32)
        + expert_input_grad
        + jnp.dot(logit_grad, router_full.astype(jnp.float32).T, precision=highest)
    )
    gain_two_term, residual_back = rms_back(second_grad, normed_two, inverse_two, gain_two)
    residual_grad = grad_rows + residual_back
    norm_gain_2_grad, router_weight_grad, shared_gate_grad, shared_up_grad, shared_down_grad = (
        lax.psum_scatter(gain_two_term, ("ctx", "wa"), scatter_dimension=0, tiled=True),
        lax.psum_scatter(router_term, ("ctx", "wa"), scatter_dimension=0, tiled=True),
        lax.psum_scatter(shared_gate_term, ("ctx", "wa"), scatter_dimension=0, tiled=True),
        lax.psum_scatter(shared_up_term, ("ctx", "wa"), scatter_dimension=0, tiled=True),
        lax.psum_scatter(shared_down_term, ("ctx", "wa"), scatter_dimension=1, tiled=True),
    )
    mix_low = residual_grad.astype(jnp.bfloat16)
    out_term = jnp.dot(attended_low.T, mix_low, preferred_element_type=jnp.float32)
    attended_grad = jnp.dot(mix_low, out_full.T, preferred_element_type=jnp.float32).astype(
        jnp.bfloat16
    )
    dout_heads = heads_first(attended_grad, heads_ratio)
    delta = jnp.sum(dout_heads.astype(jnp.float32) * attended_rows, axis=-1)

    def back_step(query_grad, block_items):
        key_block, value_block, pos_block, seg_block = block_items
        scores, allowed = scores_of(key_block, pos_block, seg_block)
        probs = probs_of(scores, allowed)
        probs_low = probs.astype(jnp.bfloat16)
        probs_grad = jnp.einsum(
            "grd,kgd->grk", dout_heads, value_block, preferred_element_type=jnp.float32
        )
        score_low = (probs * (probs_grad - delta[..., None])).astype(jnp.bfloat16)
        query_grad = (
            query_grad
            + jnp.einsum("grk,kgd->grd", score_low, key_block, preferred_element_type=jnp.float32)
            * score_scale
        )
        key_part = (
            jnp.einsum("grk,grd->kgd", score_low, query_heads, preferred_element_type=jnp.float32)
            * score_scale
        )
        value_part = jnp.einsum(
            "grk,grd->kgd", probs_low, dout_heads, preferred_element_type=jnp.float32
        )
        return (query_grad, (key_part, value_part))

    query_grad, (key_sections, value_sections) = lax.scan(
        back_step,
        jnp.zeros((KEY_VALUE_HEADS, heads_ratio * nearby_rows, HEAD_DIM), jnp.float32),
        (grouped_keys, grouped_values, key_pos, key_seg),
    )
    key_grad, value_grad = (
        lax.psum_scatter(
            key_sections.reshape(context_count, nearby_rows, KEY_VALUE_HEADS * HEAD_DIM).astype(
                jnp.bfloat16
            ),
            "ctx",
            scatter_dimension=0,
            tiled=True,
        ).astype(jnp.float32),
        lax.psum_scatter(
            value_sections.reshape(context_count, nearby_rows, KEY_VALUE_HEADS * HEAD_DIM).astype(
                jnp.bfloat16
            ),
            "ctx",
            scatter_dimension=0,
            tiled=True,
        ).astype(jnp.float32),
    )
    key_low = key_grad[0].astype(jnp.bfloat16)
    value_low = value_grad[0].astype(jnp.bfloat16)
    query_low = rows_first(query_grad, heads_ratio).astype(jnp.bfloat16)
    query_term = jnp.dot(normed_low.T, query_low, preferred_element_type=jnp.float32)
    key_term = jnp.dot(normed_low.T, key_low, preferred_element_type=jnp.float32)
    value_term = jnp.dot(normed_low.T, value_low, preferred_element_type=jnp.float32)
    first_grad = (
        jnp.dot(query_low, query_full.T, preferred_element_type=jnp.float32)
        + jnp.dot(key_low, key_full.T, preferred_element_type=jnp.float32)
        + jnp.dot(value_low, value_full.T, preferred_element_type=jnp.float32)
    )
    gain_one_term, input_back = rms_back(first_grad, normed_one, inverse_one, gain_one)
    tokens_grad = (residual_grad + input_back).astype(jnp.bfloat16).reshape(tokens.shape)
    norm_gain_1_grad, query_weight_grad, key_weight_grad, value_weight_grad, out_weight_grad = (
        lax.psum_scatter(gain_one_term, ("ctx", "wa"), scatter_dimension=0, tiled=True),
        lax.psum_scatter(query_term, ("ctx", "wa"), scatter_dimension=0, tiled=True),
        lax.psum_scatter(key_term, ("ctx", "wa"), scatter_dimension=0, tiled=True),
        lax.psum_scatter(value_term, ("ctx", "wa"), scatter_dimension=0, tiled=True),
        lax.psum_scatter(out_term, ("ctx", "wa"), scatter_dimension=1, tiled=True),
    )
    return (
        block_out,
        tokens_grad,
        norm_gain_1_grad,
        query_weight_grad,
        key_weight_grad,
        value_weight_grad,
        out_weight_grad,
        norm_gain_2_grad,
        router_weight_grad,
        shared_gate_grad,
        shared_up_grad,
        shared_down_grad,
        expert_gate_grad,
        expert_up_grad,
        expert_down_grad,
    )


def solution(mesh):
    return jax.shard_map(
        shards,
        mesh=mesh,
        in_specs=(
            P("wa", "ctx", None, None, None),
            P("wa", None),
            P("wa", "ctx", None, None, None),
            P("wa"),
            P("wa", None),
            P("wa", None),
            P("wa", None),
            P(None, "wa"),
            P("wa"),
            P("wa", None),
            P("wa", None),
            P("wa", None),
            P(None, "wa"),
            P("wa", None, None),
            P("wa", None, None),
            P("wa", None, None),
            P("wa", "ctx", None, None, None),
        ),
        out_specs=(
            P("wa", "ctx", None, None, None),
            P("wa", "ctx", None, None, None),
            P(("ctx", "wa")),
            P(("ctx", "wa"), None),
            P(("ctx", "wa"), None),
            P(("ctx", "wa"), None),
            P(None, ("ctx", "wa")),
            P(("ctx", "wa")),
            P(("ctx", "wa"), None),
            P(("ctx", "wa"), None),
            P(("ctx", "wa"), None),
            P(None, ("ctx", "wa")),
            P("wa", "ctx", None),
            P("wa", "ctx", None),
            P("wa", None, "ctx"),
        ),
        check_vma=False,
    )
```

profile of v0, /device:TPU:10, one launch (start us, length us, event | category | flops | bytes accessed | tf_op | source)
XLA Modules:
  0.0 2439.0 jit_solution(3972686669096609254)
XLA Ops:
  70.0 33.9 %all-gather.28.cloned.1.call-done = bf16[2048,512]{1,0:T(8,128)(2,1)} async-done(((bf16[256,512]{1,0:T(8,128)(2,1)}), bf16[2048,512]{1,0:T(8,128)(2,1)}) %all-gather.28.cloned.1.call-update) | async-done | bytes 2097168 | tf_op jit(solution)/shard_map/all_gather | solution.py:138
  108.1 46.1 %all-gather.30.cloned.1.call-done = bf16[2048,512]{1,0:T(8,128)(2,1)} async-done(((bf16[256,512]{1,0:T(8,128)(2,1)}), bf16[2048,512]{1,0:T(8,128)(2,1)}) %all-gather.30.cloned.1.call-update) | async-done | bytes 2097168 | tf_op jit(solution)/shard_map/all_gather | solution.py:139
  158.5 32.2 %all-gather.16.cloned.1.call-done = bf16[1536,1536]{1,0:T(8,128)(2,1)} async-done(((bf16[384,1536]{1,0:T(8,128)(2,1)}), bf16[1536,1536]{1,0:T(8,128)(2,1)}) %all-gather.16.cloned.1.call-update) | async-done | bytes 4718608 | tf_op jit(solution)/shard_map/all_gather | solution.py:113
  195.1 47.8 %while.39 = (s32[]{:T(128)}, f32[4,768]{1,0:T(4,128)S(1)}, f32[4,768]{1,0:T(4,128)}, s32[4,512]{1,0:T(4,128)}, s32[4,512]{1,0:T(4,128)}, /*index=5*/bf16[4,512,4...) while((s32[]{:T(128)}, f32[4,768]{1,0:T(4,128)S(1)}, ...), condition=%wide.region_6.7_spmd.clone, body=%wide.region_3.6_spmd.clone.sunk | while | flops 416431104 | bytes 15370932 | solution.py:172
  278.0 29.3 %scatter_custom_fusion = bf16[3072,1536]{1,0:T(8,128)(2,1)} fusion(s32[1536]{0:T(1024)S(1)} %copy-done.54, bf16[256,1536]{1,0:T(8,128)(2,1)S(1)} %multiply_convert_fusion.3, s32[2048]{0:T(1024)} %pad_clamp_fusion.1, bf16[]{:T(256)} %constant.108.clone.1), kind=kCustom, calls=%fused_computation.111 | custom fusion | bytes 9437696 | tf_op jit(solution)/shard_map/scatter | solution.py:224
  332.4 85.8 %all_gather.47 = bf16[1536,16]{0,1:T(8,128)(2,1)S(1)} all-gather(bf16[384,16]{0,1:T(8,128)(2,1)S(1)} %copy-done.60), channel_id=1, replica_groups=mesh['ctx'=8,'wa'=4] {'wa'}, dimensions={0}, use_global_device_ids=true | all-gather | bytes 61440 | tf_op jit(solution)/shard_map/all_gather | solution.py:118
  466.3 95.8 %all-to-all-done.2 = bf16[4,4,192,1536]{3,2,1,0:T(8,128)(2,1)} async-done(((bf16[4,4,192,1536]{3,2,1,0:T(8,128)(2,1)}), bf16[4,4,192,1536]{3,2,1,0:T(8,128)(2,1)}, u32[]{:S(2)}, u32[]{:S(2)}) %all-to-all-start.2) | async-done | bytes 9437216 | tf_op jit(solution)/shard_map/all_to_all | solution.py:254
  638.9 84.3 %all-to-all-done.1 = bf16[4,4,192,1536]{3,2,1,0:T(8,128)(2,1)} async-done(((bf16[4,4,192,1536]{3,2,1,0:T(8,128)(2,1)}), bf16[4,4,192,1536]{3,2,1,0:T(8,128)(2,1)}, u32[]{:S(2)}, u32[]{:S(2)}) %all-to-all-start.1) | async-done | bytes 9437216 | tf_op jit(solution)/shard_map/all_to_all | solution.py:240
  739.5 39.0 %all-gather.26.cloned.1.call-done = bf16[1024,1536]{1,0:T(8,128)(2,1)} async-done(((bf16[1024,384]{1,0:T(8,128)(2,1)}), bf16[1024,1536]{1,0:T(8,128)(2,1)}) %all-gather.26.cloned.1.call-update) | async-done | bytes 3145744 | tf_op jit(solution)/shard_map/all_gather | solution.py:121
  820.1 30.2 %all-to-all-done.3 = bf16[4,4,192,1536]{3,2,1,0:T(8,128)(2,1)} async-done(((bf16[4,4,192,1536]{3,2,1,0:T(8,128)(2,1)}), bf16[4,4,192,1536]{3,2,1,0:T(8,128)(2,1)}, u32[]{:S(2)}, u32[]{:S(2)}) %all-to-all-start.3) | async-done | bytes 9437216 | tf_op jit(solution)/shard_map/all_to_all | solution.py:269
  896.0 70.9 %while.41 = (s32[]{:T(128)}, f32[4,768,128]{2,1,0:T(8,128)}, bf16[4,512,4,128]{3,1,2,0:T(8,128)(2,1)}, bf16[4,512,4,128]{3,1,2,0:T(8,128)(2,1)}, s32[4,512]{1,0:...) while((s32[]{:T(128)}, f32[4,768,128]{2,1,0:T(8,128)}, ...), condition=%wide.region_24.25_spmd.clone, body=%wide.region_23.24_spmd.clone.sunk | while | flops 2030043136 | bytes 98906944 | solution.py:341
  1044.1 67.1 %reduce-scatter.18.cloned.1.call-done = bf16[1,256,512]{2,1,0:T(8,128)(2,1)} async-done(((bf16[8,256,512]{2,1,0:T(8,128)(2,1)}), bf16[1,256,512]{2,1,0:T(8,128)(2,1)}) %reduce-scatter.18.cloned.1.call-update) | async-done | bytes 262160 | tf_op jit(solution)/shard_map/reduce_scatter | solution.py:355
  1140.6 70.6 %reduce-scatter.40.cloned.1.call-done = f32[48,16]{1,0:T(8,128)} async-done(((f32[1536,16]{1,0:T(8,128)}), f32[48,16]{1,0:T(8,128)}) %reduce-scatter.40.cloned.1.call-update) | async-done | bytes 3088
  1216.8 43.9 %all-reduce.2 = (f32[1536]{0:T(1024)S(1)}, f32[1536]{0:T(1024)S(1)}) all-reduce(f32[1536]{0:T(1024)S(1)} %get-tuple-element.516, f32[1536]{0:T(1024)S(1)} %copy-done.53), channel_id=6, replica_groups=mesh['ctx'=8,'wa'=4] {'ctx','wa'}, use_global_device_ids=true, to_apply=%region_29.30.clone | all-reduce | flops 3072 | bytes 24576
  1264.6 67.8 %reduce-scatter.38.cloned.1.call-done = bf16[4,512,192]{1,2,0:T(8,128)(2,1)} async-done(((bf16[4,512,1536]{1,2,0:T(8,128)(2,1)}), bf16[4,512,192]{1,2,0:T(8,128)(2,1)}) %reduce-scatter.38.cloned.1.call-update) | async-done | bytes 786448 | tf_op jit(solution)/shard_map/reduce_scatter | solution.py:282
  1334.8 118.1 %reduce-scatter.34.cloned.1.call-done = bf16[4,192,512]{2,1,0:T(8,128)(2,1)} async-done(((bf16[4,1536,512]{2,1,0:T(8,128)(2,1)}), bf16[4,192,512]{2,1,0:T(8,128)(2,1)}) %reduce-scatter.34.cloned.1.call-update) | async-done | bytes 786448 | tf_op jit(solution)/shard_map/reduce_scatter | solution.py:276
  1455.4 118.0 %reduce-scatter.36.cloned.1.call-done = bf16[4,192,512]{2,1,0:T(8,128)(2,1)} async-done(((bf16[4,1536,512]{2,1,0:T(8,128)(2,1)}), bf16[4,192,512]{2,1,0:T(8,128)(2,1)}) %reduce-scatter.36.cloned.1.call-update) | async-done | bytes 786448 | tf_op jit(solution)/shard_map/reduce_scatter | solution.py:279
  1576.0 117.8 %reduce-scatter.28.cloned.1.call-done = f32[48,1024]{1,0:T(8,128)} async-done(((f32[1536,1024]{1,0:T(8,128)}), f32[48,1024]{1,0:T(8,128)}) %reduce-scatter.28.cloned.1.call-update) | async-done | bytes 196624 | tf_op jit(solution)/shard_map/reduce_scatter | solution.py:306
  1693.8 120.6 %reduce-scatter.30.cloned.1.call-done = f32[48,1024]{1,0:T(8,128)} async-done(((f32[1536,1024]{1,0:T(8,128)}), f32[48,1024]{1,0:T(8,128)}) %reduce-scatter.30.cloned.1.call-update) | async-done | bytes 196624 | tf_op jit(solution)/shard_map/reduce_scatter | solution.py:307
  1814.4 119.7 %reduce-scatter.32.cloned.1.call-done = f32[1024,48]{0,1:T(8,128)} async-done(((f32[1024,1536]{0,1:T(8,128)}), f32[1024,48]{0,1:T(8,128)}) %reduce-scatter.32.cloned.1.call-update) | async-done | bytes 196624 | tf_op jit(solution)/shard_map/reduce_scatter | solution.py:308
  1934.1 107.5 %reduce-scatter.22.cloned.1.call-done = f32[48,512]{1,0:T(8,128)} async-done(((f32[1536,512]{1,0:T(8,128)}), f32[48,512]{1,0:T(8,128)}) %reduce-scatter.22.cloned.1.call-update) | async-done | bytes 98320 | tf_op jit(solution)/shard_map/reduce_scatter | solution.py:380
  2041.5 107.3 %reduce-scatter.24.cloned.1.call-done = f32[48,512]{1,0:T(8,128)} async-done(((f32[1536,512]{1,0:T(8,128)}), f32[48,512]{1,0:T(8,128)}) %reduce-scatter.24.cloned.1.call-update) | async-done | bytes 98320 | tf_op jit(solution)/shard_map/reduce_scatter | solution.py:381
  2148.8 142.1 %reduce-scatter.26.cloned.1.call-done = f32[1536,48]{0,1:T(8,128)} async-done(((f32[1536,1536]{0,1:T(8,128)}), f32[1536,48]{0,1:T(8,128)}) %reduce-scatter.26.cloned.1.call-update) | async-done | bytes 294928 | tf_op jit(solution)/shard_map/reduce_scatter | solution.py:382
  2290.9 141.0 %reduce-scatter.20.cloned.1.call-done = f32[48,1536]{1,0:T(8,128)} async-done(((f32[1536,1536]{1,0:T(8,128)}), f32[48,1536]{1,0:T(8,128)}) %reduce-scatter.20.cloned.1.call-update) | async-done | bytes 294928 | tf_op jit(solution)/shard_map/reduce_scatter | solution.py:379
  (475 shorter events, 630.5 us)
Async XLA Ops:
  8.7 95.2 %all-gather.28.cloned.1.call-start = ((), (), s32[]{:S(2)}) async-start(), calls=%async_computation.36 | async-start | bytes 2359296 | tf_op jit(solution)/shard_map/all_gather | solution.py:138
  32.2 122.1 %all-gather.30.cloned.1.call-start = ((), (), s32[]{:S(2)}) async-start(), calls=%async_computation.37 | async-start | bytes 2359296 | tf_op jit(solution)/shard_map/all_gather | solution.py:139
  53.5 137.3 %all-gather.16.cloned.1.call-start = ((), (), s32[]{:S(2)}) async-start(), calls=%async_computation.18 | async-start | bytes 5898240 | tf_op jit(solution)/shard_map/all_gather | solution.py:113
  54.0 218.4 %all-gather.20.cloned.1.call-start = ((), (), s32[]{:S(2)}) async-start(), calls=%async_computation.20 | async-start | bytes 5898240 | tf_op jit(solution)/shard_map/all_gather | solution.py:116
  307.3 127.7 %all-to-all-start = ((bf16[4,4,192,1536]{3,2,1,0:T(8,128)(2,1)}), bf16[4,4,192,1536]{3,2,1,0:T(8,128)(2,1)}, u32[]{:S(2)}, u32[]{:S(2)}) async-start(bf16[4,4,192,1536]{3,2,1,0:T(8,128)(2,1)} %bitcast.346), calls=%async_computation | async-start | bytes 18874368 | tf_op jit(solution)/shard_map/all_to_all | solution.py:228
  435.0 127.1 %all-to-all-start.2 = ((bf16[4,4,192,1536]{3,2,1,0:T(8,128)(2,1)}), bf16[4,4,192,1536]{3,2,1,0:T(8,128)(2,1)}, u32[]{:S(2)}, u32[]{:S(2)}) async-start(bf16[4,4,192,1536]{3,2,1,0:T(8,128)(2,1)} %bitcast.345), calls=%async_computation.2 | async-start | bytes 18874368 | tf_op jit(solution)/shard_map/all_to_all | solution.py:254
  442.5 290.3 %all-gather.22.cloned.1.call-start = ((), (), s32[]{:S(2)}) async-start(), calls=%async_computation.21 | async-start | bytes 3932160 | tf_op jit(solution)/shard_map/all_gather | solution.py:119
  596.1 127.1 %all-to-all-start.1 = ((bf16[4,4,192,1536]{3,2,1,0:T(8,128)(2,1)}), bf16[4,4,192,1536]{3,2,1,0:T(8,128)(2,1)}, u32[]{:S(2)}, u32[]{:S(2)}) async-start(bf16[4,4,192,1536]{3,2,1,0:T(8,128)(2,1)} %copy.121), calls=%async_computation.1 | async-start | bytes 18874368 | tf_op jit(solution)/shard_map/all_to_all | solution.py:240
  603.5 132.1 %all-gather.24.cloned.1.call-start = ((), (), s32[]{:S(2)}) async-start(), calls=%async_computation.22 | async-start | bytes 3932160 | tf_op jit(solution)/shard_map/all_gather | solution.py:120
  723.2 127.1 %all-to-all-start.3 = ((bf16[4,4,192,1536]{3,2,1,0:T(8,128)(2,1)}), bf16[4,4,192,1536]{3,2,1,0:T(8,128)(2,1)}, u32[]{:S(2)}, u32[]{:S(2)}) async-start(bf16[4,4,192,1536]{3,2,1,0:T(8,128)(2,1)} %copy.123), calls=%async_computation.3 | async-start | bytes 18874368 | tf_op jit(solution)/shard_map/all_to_all | solution.py:269
  730.7 47.9 %all-gather.26.cloned.1.call-start = ((), (), s32[]{:S(2)}) async-start(), calls=%async_computation.23 | async-start | bytes 3932160 | tf_op jit(solution)/shard_map/all_gather | solution.py:121
  731.4 309.4 %reduce-scatter.16.cloned.1.call-start = ((), (), s32[]{:S(2)}) async-start(), calls=%async_computation.24 | async-start | bytes 2359296 | tf_op jit(solution)/shard_map/reduce_scatter | solution.py:347
  972.3 138.8 %reduce-scatter.18.cloned.1.call-start = ((), (), s32[]{:S(2)}) async-start(), calls=%async_computation.25 | async-start | bytes 2359296 | tf_op jit(solution)/shard_map/reduce_scatter | solution.py:355
  977.9 233.3 %reduce-scatter.40.cloned.1.call-start = ((), (), s32[]{:S(2)}) async-start(), calls=%async_computation.38 | async-start | bytes 811008
  979.8 352.5 %reduce-scatter.38.cloned.1.call-start = ((), (), s32[]{:S(2)}) async-start(), calls=%async_computation.35 | async-start | bytes 7077888 | tf_op jit(solution)/shard_map/reduce_scatter | solution.py:282
  992.9 460.0 %reduce-scatter.34.cloned.1.call-start = ((), (), s32[]{:S(2)}) async-start(), calls=%async_computation.33 | async-start | bytes 7077888 | tf_op jit(solution)/shard_map/reduce_scatter | solution.py:276
  1005.7 567.8 %reduce-scatter.36.cloned.1.call-start = ((), (), s32[]{:S(2)}) async-start(), calls=%async_computation.34 | async-start | bytes 7077888 | tf_op jit(solution)/shard_map/reduce_scatter | solution.py:279
  1018.4 675.4 %reduce-scatter.28.cloned.1.call-start = ((), (), s32[]{:S(2)}) async-start(), calls=%async_computation.30 | async-start | bytes 6488064 | tf_op jit(solution)/shard_map/reduce_scatter | solution.py:306
  1023.1 791.3 %reduce-scatter.30.cloned.1.call-start = ((), (), s32[]{:S(2)}) async-start(), calls=%async_computation.31 | async-start | bytes 6488064 | tf_op jit(solution)/shard_map/reduce_scatter | solution.py:307
  1027.7 906.3 %reduce-scatter.32.cloned.1.call-start = ((), (), s32[]{:S(2)}) async-start(), calls=%async_computation.32 | async-start | bytes 6488064 | tf_op jit(solution)/shard_map/reduce_scatter | solution.py:308
  1032.7 1008.9 %reduce-scatter.22.cloned.1.call-start = ((), (), s32[]{:S(2)}) async-start(), calls=%async_computation.27 | async-start | bytes 3244032 | tf_op jit(solution)/shard_map/reduce_scatter | solution.py:380
  1044.0 1104.8 %reduce-scatter.24.cloned.1.call-start = ((), (), s32[]{:S(2)}) async-start(), calls=%async_computation.28 | async-start | bytes 3244032 | tf_op jit(solution)/shard_map/reduce_scatter | solution.py:381
  1114.4 1176.5 %reduce-scatter.26.cloned.1.call-start = ((), (), s32[]{:S(2)}) async-start(), calls=%async_computation.29 | async-start | bytes 9732096 | tf_op jit(solution)/shard_map/reduce_scatter | solution.py:382
  1120.7 1311.2 %reduce-scatter.20.cloned.1.call-start = ((), (), s32[]{:S(2)}) async-start(), calls=%async_computation.26 | async-start | bytes 9732096 | tf_op jit(solution)/shard_map/reduce_scatter | solution.py:379
  (89 other events, 1599.7 us)
Sparse Core Ops, SparseCore 0:
  9.6 19.8 all-gather.13
  31.0 19.6 all-gather.17
  53.4 50.4 all-gather.27
  106.4 47.7 all-gather.29
  155.7 35.0 all-gather.15
  192.2 37.3 all-gather.19
  444.9 45.4 all-gather.21
  605.9 45.4 all-gather.23
  733.0 45.4 all-gather.25
  972.5 68.2 reduce-scatter.15
  1044.3 66.8 reduce-scatter.17
  1116.1 95.0 reduce-scatter.39
  1214.8 117.4 reduce-scatter.37
  1335.8 117.1 reduce-scatter.33
  1456.4 117.0 reduce-scatter.35
  1579.6 114.1 reduce-scatter.27
  1700.8 113.5 reduce-scatter.29
  1820.4 113.5 reduce-scatter.31
  1940.9 100.5 reduce-scatter.21
  2048.3 100.5 reduce-scatter.23
  2156.3 134.5 reduce-scatter.25
  2297.4 134.4 reduce-scatter.19
where the time goes:
time: 2450 us; the launch traced here: 2440 us
  waiting for transfers between devices  1700 us (69%)
  matrix products  297 us (12%)
  local copies, waits for them, and re-layouts  171 us (7%)
  blocking collectives  140 us (6%)
  other arithmetic  83.4 us (3%)
  starting transfers between devices  31.1 us (1%)
    reduce_scatter x1, waiting for transfers between devices, shards(): lax.psum_scatter(out_term, ('ctx', 'wa'), scatter_dimension=1, tiled=True)  142 us
    reduce_scatter x1, waiting for transfers between devices, shards(): lax.psum_scatter(query_term, ('ctx', 'wa'), scatter_dimension=0, tiled=True)  141 us
    reduce_scatter x1, waiting for transfers between devices, shards(): lax.psum_scatter(shared_up_term, ('ctx', 'wa'), scatter_dimension=0, tile...  121 us
    reduce_scatter x1, waiting for transfers between devices, shards(): lax.psum_scatter(shared_down_term, ('ctx', 'wa'), scatter_dimension=1, ti...  120 us
    reduce_scatter x1, waiting for transfers between devices, shards(): lax.psum_scatter(gate_term.astype(jnp.bfloat16), 'ctx', scatter_dimension...  118 us
    reduce_scatter x1, waiting for transfers between devices, shards(): lax.psum_scatter(up_term.astype(jnp.bfloat16), 'ctx', scatter_dimension=1...  118 us
    reduce_scatter x1, waiting for transfers between devices, shards(): lax.psum_scatter(shared_gate_term, ('ctx', 'wa'), scatter_dimension=0, ti...  118 us
    reduce_scatter x1, waiting for transfers between devices, shards(): lax.psum_scatter(key_term, ('ctx', 'wa'), scatter_dimension=0, tiled=True)  107 us
  transfers between devices with their start and end apart: 26, of which 22 were waited for; matrix products, arithmetic and copies ran while one was open for 16% of the time, Pallas kernels for 0%

commit v1 on v0

v1 whole, which is shorter than its diff:
```python
import jax
import jax.numpy as jnp
from jax import lax
from jax.experimental import pallas as pl
from jax.experimental.pallas import tpu as pltpu
from jax.sharding import PartitionSpec as P

QUERY_HEADS = 12
KEY_VALUE_HEADS = 4
HEAD_DIM = 128
TOP = 6
EXPERTS = 16

epsilon = 1e-05
large_negative = -1e30
highest = lax.Precision.HIGHEST
ORDER = (0, 2, 1, 3)


def dot32(left, right, dims=None):
    if dims is None:
        return jnp.dot(left, right, preferred_element_type=jnp.float32)
    return lax.dot_general(left, right, (dims, ((), ())), preferred_element_type=jnp.float32)


def flip(value, axis, bits):
    count = lax.axis_size(axis)
    return lax.ppermute(value, axis, [(i, i ^ bits) for i in range(count)])


def gather_rows(value):
    across = flip(value, "wa", 2)
    return jnp.concatenate([value, across, flip(value, "wa", 1), flip(across, "wa", 1)], axis=0)


def exchange(pieces, index):
    received = []
    for bits in ORDER:
        piece = lax.dynamic_index_in_dim(pieces, index ^ bits, 0, keepdims=False)
        received.append(piece if bits == 0 else flip(piece, "wa", bits))
    return jnp.concatenate(received, axis=0)


def reduce_rows(partial, kind):
    half = partial.shape[0] // 2
    near = partial[:half] + flip(partial[half:].astype(kind), "wa", 1).astype(jnp.float32)
    quarter = half // 2
    return near[:quarter] + flip(near[quarter:].astype(kind), "wa", 2).astype(jnp.float32)


def scatter_small(value):
    rows, width = value.shape
    contexts, members = lax.axis_size("ctx"), lax.axis_size("wa")
    each = width // (contexts * members)
    spread = value.reshape(rows, contexts, members, each).transpose(2, 0, 1, 3)
    spread = spread.reshape(members, rows, contexts * each)
    first = jnp.sum(lax.all_to_all(spread, "wa", 0, 0, tiled=True), axis=0)
    second = first.reshape(rows, contexts, each).transpose(1, 0, 2)
    return jnp.sum(lax.all_to_all(second, "ctx", 0, 0, tiled=True), axis=0)


def scatter_ctx(value):
    return lax.psum_scatter(value, "ctx", scatter_dimension=0, tiled=True)[0]


def silu_parts(values):
    sigmoid_of = jax.nn.sigmoid(values)
    return (values * sigmoid_of, sigmoid_of * (1.0 + values * (1.0 - sigmoid_of)))


def rms_back(grad_normed, normed, inverse, gain_values):
    scaled = grad_normed * gain_values
    return (
        jnp.sum(grad_normed * normed, axis=0),
        inverse * (scaled - normed * jnp.mean(scaled * normed, axis=-1, keepdims=True)),
    )


def attention_masks(starts_ref, block, half_rows, shape):
    rows = block * half_rows + lax.broadcasted_iota(jnp.int32, shape, 0) % half_rows
    first = jnp.zeros(shape, jnp.int32)
    for document in range(1, starts_ref.shape[0]):
        start = starts_ref[document]
        first = jnp.where(start <= rows, jnp.maximum(first, start), first)
    return first, rows


def block_bounds(starts_ref, block, half_rows):
    top = block * half_rows
    first = jnp.int32(0)
    for document in range(1, starts_ref.shape[0]):
        start = starts_ref[document]
        first = jnp.where(start <= top, jnp.maximum(first, start), first)
    return first // half_rows


def block_place(block, contexts):
    return jnp.where(block < contexts, 2 * block, 4 * contexts - 1 - 2 * block)


def attention_forward_kernel(starts_ref, own_ref, q_ref, k_ref, v_ref, o_ref, lse_ref, s_ref):
    blocks, half_rows, _ = k_ref.shape
    contexts = blocks // 2
    ratio = q_ref.shape[1] // HEAD_DIM
    rows = ratio * half_rows
    scale = HEAD_DIM ** (-0.5)
    for half in range(2):
        block = own_ref[0] if half == 0 else blocks - 1 - own_ref[0]
        queries = jnp.concatenate(
            [
                q_ref[half * half_rows : (half + 1) * half_rows, h * HEAD_DIM : (h + 1) * HEAD_DIM]
                for h in range(ratio)
            ],
            axis=0,
        )
        low = block_bounds(starts_ref, block, half_rows)
        first, position = attention_masks(starts_ref, block, half_rows, (rows, half_rows))
        column = lax.broadcasted_iota(jnp.int32, (rows, half_rows), 1)

        def score_step(step, running):
            keys = k_ref[block_place(step, contexts)]
            scores = dot32(queries, keys, ((1,), (1,))) * scale
            at = column + step * half_rows
            scores = jnp.where((at >= first) & (at <= position), scores, large_negative)
            s_ref[step - low] = scores
            return jnp.maximum(running, scores)

        running = lax.fori_loop(
            low, block + 1, score_step, jnp.full((rows, half_rows), large_negative, jnp.float32)
        )
        row_max = jnp.max(running, axis=1, keepdims=True)

        def sum_step(step, total):
            expo = jnp.exp(s_ref[step - low] - row_max)
            s_ref[step - low] = expo
            return total + expo

        total = lax.fori_loop(
            low, block + 1, sum_step, jnp.zeros((rows, half_rows), jnp.float32)
        )
        row_sum = jnp.sum(total, axis=1, keepdims=True)
        inverse = 1.0 / row_sum

        def value_step(step, accum):
            weights = (s_ref[step - low] * inverse).astype(jnp.bfloat16)
            return accum + dot32(weights, v_ref[block_place(step, contexts)])

        accum = lax.fori_loop(
            low, block + 1, value_step, jnp.zeros((rows, HEAD_DIM), jnp.float32)
        )
        log_sum = row_max + jnp.log(row_sum)
        lse_ref[0, half] = jnp.broadcast_to(log_sum, (rows, half_rows))
        for h in range(ratio):
            o_ref[half * half_rows : (half + 1) * half_rows, h * HEAD_DIM : (h + 1) * HEAD_DIM] = (
                accum[h * half_rows : (h + 1) * half_rows].astype(jnp.bfloat16)
            )


def attention_forward(starts, own, queries, keys, values):
    rows, width = queries.shape
    blocks, half_rows, _ = keys.shape
    ratio = QUERY_HEADS // KEY_VALUE_HEADS
    stacked = ratio * half_rows
    kv_spec = pl.BlockSpec((blocks, half_rows, HEAD_DIM), lambda g, *_: (0, 0, g))
    q_spec = pl.BlockSpec((rows, ratio * HEAD_DIM), lambda g, *_: (0, g))
    return pl.pallas_call(
        attention_forward_kernel,
        grid_spec=pltpu.PrefetchScalarGridSpec(
            num_scalar_prefetch=2,
            grid=(KEY_VALUE_HEADS,),
            in_specs=[q_spec, kv_spec, kv_spec],
            out_specs=[
                q_spec,
                pl.BlockSpec((1, 2, stacked, half_rows), lambda g, *_: (g, 0, 0, 0)),
            ],
            scratch_shapes=[pltpu.VMEM((blocks, stacked, half_rows), jnp.float32)],
        ),
        out_shape=(
            jax.ShapeDtypeStruct((rows, width), jnp.bfloat16),
            jax.ShapeDtypeStruct((KEY_VALUE_HEADS, 2, stacked, half_rows), jnp.float32),
        ),
        compiler_params=pltpu.CompilerParams(vmem_limit_bytes=48 << 20),
        cost_estimate=pl.CostEstimate(
            flops=2 * rows * width * blocks * half_rows * 2,
            bytes_accessed=4 * rows * width + 4 * blocks * half_rows * 512,
            transcendentals=rows * QUERY_HEADS * blocks * half_rows // 2,
        ),
        name="attention_forward",
    )(starts, own, queries, keys, values)


def attention_backward_kernel(
    starts_ref, own_ref, q_ref, do_ref, k_ref, v_ref, lse_ref, dq_ref, dk_ref, dv_ref, p_ref, dp_ref, dka_ref, dva_ref
):
    blocks, half_rows, _ = k_ref.shape
    contexts = blocks // 2
    ratio = q_ref.shape[1] // HEAD_DIM
    rows = ratio * half_rows
    scale = HEAD_DIM ** (-0.5)
    dka_ref[...] = jnp.zeros_like(dka_ref)
    dva_ref[...] = jnp.zeros_like(dva_ref)

    def stack(ref, half):
        return jnp.concatenate(
            [
                ref[half * half_rows : (half + 1) * half_rows, h * HEAD_DIM : (h + 1) * HEAD_DIM]
                for h in range(ratio)
            ],
            axis=0,
        )

    for half in range(2):
        block = own_ref[0] if half == 0 else blocks - 1 - own_ref[0]
        queries = stack(q_ref, half)
        grads = stack(do_ref, half)
        log_sum = lse_ref[0, half]
        low = block_bounds(starts_ref, block, half_rows)
        first, position = attention_masks(starts_ref, block, half_rows, (rows, half_rows))
        column = lax.broadcasted_iota(jnp.int32, (rows, half_rows), 1)

        def prob_step(step, running):
            place = block_place(step, contexts)
            scores = dot32(queries, k_ref[place], ((1,), (1,))) * scale
            at = column + step * half_rows
            probs = jnp.where(
                (at >= first) & (at <= position), jnp.exp(scores - log_sum), 0.0
            )
            prob_grads = dot32(grads, v_ref[place], ((1,), (1,)))
            p_ref[step - low] = probs
            dp_ref[step - low] = prob_grads
            return running + probs * prob_grads

        running = lax.fori_loop(
            low, block + 1, prob_step, jnp.zeros((rows, half_rows), jnp.float32)
        )
        delta = jnp.sum(running, axis=1, keepdims=True)

        def grad_step(step, query_grad):
            place = block_place(step, contexts)
            probs = p_ref[step - low]
            score_low = (probs * (dp_ref[step - low] - delta)).astype(jnp.bfloat16)
            dka_ref[place] += dot32(score_low, queries, ((0,), (0,)))
            dva_ref[place] += dot32(probs.astype(jnp.bfloat16), grads, ((0,), (0,)))
            return query_grad + dot32(score_low, k_ref[place])

        query_grad = lax.fori_loop(
            low, block + 1, grad_step, jnp.zeros((rows, HEAD_DIM), jnp.float32)
        )
        for h in range(ratio):
            dq_ref[half * half_rows : (half + 1) * half_rows, h * HEAD_DIM : (h + 1) * HEAD_DIM] = (
                query_grad[h * half_rows : (h + 1) * half_rows] * scale
            ).astype(jnp.bfloat16)
    dk_ref[...] = (dka_ref[...] * scale).astype(jnp.bfloat16)
    dv_ref[...] = dva_ref[...].astype(jnp.bfloat16)


def attention_backward(starts, own, queries, grads, keys, values, log_sums):
    rows, width = queries.shape
    blocks, half_rows, kv_width = keys.shape
    ratio = QUERY_HEADS // KEY_VALUE_HEADS
    stacked = ratio * half_rows
    kv_spec = pl.BlockSpec((blocks, half_rows, HEAD_DIM), lambda g, *_: (0, 0, g))
    q_spec = pl.BlockSpec((rows, ratio * HEAD_DIM), lambda g, *_: (0, g))
    return pl.pallas_call(
        attention_backward_kernel,
        grid_spec=pltpu.PrefetchScalarGridSpec(
            num_scalar_prefetch=2,
            grid=(KEY_VALUE_HEADS,),
            in_specs=[
                q_spec,
                q_spec,
                kv_spec,
                kv_spec,
                pl.BlockSpec((1, 2, stacked, half_rows), lambda g, *_: (g, 0, 0, 0)),
            ],
            out_specs=[q_spec, kv_spec, kv_spec],
            scratch_shapes=[
                pltpu.VMEM((blocks, stacked, half_rows), jnp.float32),
                pltpu.VMEM((blocks, stacked, half_rows), jnp.float32),
                pltpu.VMEM((blocks, half_rows, HEAD_DIM), jnp.float32),
                pltpu.VMEM((blocks, half_rows, HEAD_DIM), jnp.float32),
            ],
        ),
        out_shape=(
            jax.ShapeDtypeStruct((rows, width), jnp.bfloat16),
            jax.ShapeDtypeStruct((blocks, half_rows, kv_width), jnp.bfloat16),
            jax.ShapeDtypeStruct((blocks, half_rows, kv_width), jnp.bfloat16),
        ),
        compiler_params=pltpu.CompilerParams(vmem_limit_bytes=58 << 20),
        cost_estimate=pl.CostEstimate(
            flops=5 * rows * width * blocks * half_rows * 2,
            bytes_accessed=8 * rows * width + 8 * blocks * half_rows * kv_width,
            transcendentals=rows * QUERY_HEADS * blocks * half_rows // 2,
        ),
        name="attention_backward",
    )(starts, own, queries, grads, keys, values, log_sums)


def experts_kernel(
    base_ref, x_ref, dy_ref, xt_ref, dyt_ref, g_ref, gt_ref, wg_ref, wu_ref, wd_ref,
    out_ref, dx_ref, dg_ref, dw_ref, he_ref, da_ref, db_ref,
):
    local = pl.program_id(0)
    expert = base_ref[0] + local
    total_rows = x_ref.shape[0]
    step_rows = 256
    per = dw_ref.shape[3]
    tall = 384

    @pl.when(local == 0)
    def _():
        out_ref[...] = jnp.zeros_like(out_ref)
        dx_ref[...] = jnp.zeros_like(dx_ref)
        dg_ref[...] = jnp.zeros_like(dg_ref)

    @pl.loop(0, total_rows // step_rows)
    def _(step):
        rows = pl.ds(pl.multiple_of(step * step_rows, step_rows), step_rows)
        x = x_ref[rows, :]
        dy = dy_ref[rows, :].astype(jnp.float32)
        lane = lax.broadcasted_iota(jnp.int32, (step_rows, g_ref.shape[1]), 1)
        mine = lane == expert
        gate = jnp.sum(jnp.where(mine, g_ref[rows, :], 0.0), axis=1, keepdims=True)
        pre = dot32(x, wg_ref[0])
        up = dot32(x, wu_ref[0])
        silu, slope = silu_parts(pre)
        hidden = (silu * up).astype(jnp.bfloat16)
        he_ref[rows, :] = hidden
        made = dot32(hidden, wd_ref[0]).astype(jnp.bfloat16).astype(jnp.float32)
        out_ref[rows, :] += gate * made
        dg_ref[rows, :] += jnp.where(mine, jnp.sum(dy * made, axis=1, keepdims=True), 0.0)
        scaled = (gate * dy).astype(jnp.bfloat16)
        back = dot32(scaled, wd_ref[0], ((1,), (1,)))
        pre_low = (back * up * slope).astype(jnp.bfloat16)
        up_low = (back * silu).astype(jnp.bfloat16)
        da_ref[rows, :] = pre_low
        db_ref[rows, :] = up_low
        moved = dot32(pre_low, wg_ref[0], ((1,), (1,))) + dot32(up_low, wu_ref[0], ((1,), (1,)))
        dx_ref[rows, :] += moved.astype(jnp.bfloat16).astype(jnp.float32)

    gate_row = gt_ref[pl.ds(expert, 1), :]

    @pl.loop(0, xt_ref.shape[0] // tall)
    def _(step):
        rows = pl.ds(pl.multiple_of(step * tall, tall), tall)
        xt = xt_ref[rows, :]
        scaled = (dyt_ref[rows, :].astype(jnp.float32) * gate_row).astype(jnp.bfloat16)
        for number, term in enumerate(
            (dot32(xt, da_ref[...]), dot32(xt, db_ref[...]), dot32(scaled, he_ref[...]))
        ):
            low = term.astype(jnp.bfloat16)
            for part in range(tall // per):
                dw_ref[step * (tall // per) + part, 0, number] = low[part * per : (part + 1) * per]


def experts_call(base, x, dy, xt, dyt, gates, gates_t, gate_w, up_w, down_w, contexts):
    rows, width = x.shape
    count, _, hidden = gate_w.shape
    per = width // contexts
    once = pl.Buffered(1)
    whole = lambda shape: pl.BlockSpec(shape, lambda e, *_: (0,) * len(shape), pipeline_mode=once)
    weight = lambda shape: pl.BlockSpec((1,) + shape, lambda e, *_: (e, 0, 0))
    return pl.pallas_call(
        experts_kernel,
        grid_spec=pltpu.PrefetchScalarGridSpec(
            num_scalar_prefetch=1,
            grid=(count,),
            in_specs=[
                whole((rows, width)),
                whole((rows, width)),
                whole((width, rows)),
                whole((width, rows)),
                whole((rows, EXPERTS)),
                whole((EXPERTS, rows)),
                weight((width, hidden)),
                weight((width, hidden)),
                weight((hidden, width)),
            ],
            out_specs=[
                whole((rows, width)),
                whole((rows, width)),
                whole((rows, EXPERTS)),
                pl.BlockSpec((contexts, 1, 3, per, hidden), lambda e, *_: (0, e, 0, 0, 0)),
            ],
            scratch_shapes=[pltpu.VMEM((rows, hidden), jnp.bfloat16)] * 3,
        ),
        out_shape=(
            jax.ShapeDtypeStruct((rows, width), jnp.float32),
            jax.ShapeDtypeStruct((rows, width), jnp.float32),
            jax.ShapeDtypeStruct((rows, EXPERTS), jnp.float32),
            jax.ShapeDtypeStruct((contexts, count, 3, per, hidden), jnp.bfloat16),
        ),
        compiler_params=pltpu.CompilerParams(vmem_limit_bytes=60 << 20),
        cost_estimate=pl.CostEstimate(
            flops=18 * count * rows * width * hidden,
            bytes_accessed=16 * rows * width + 12 * count * width * hidden,
            transcendentals=count * rows * hidden,
        ),
        name="experts",
    )(base, x, dy, xt, dyt, gates, gates_t, gate_w, up_w, down_w)


def dense_gates(logits, routes):
    chosen = jnp.any(
        routes[:, :, None] == jnp.arange(EXPERTS, dtype=jnp.int32)[None, None, :], axis=1
    )
    top = jnp.max(jnp.where(chosen, logits, large_negative), axis=-1, keepdims=True)
    expo = jnp.where(chosen, jnp.exp(logits - top), 0.0)
    return expo / jnp.sum(expo, axis=-1, keepdims=True)


def shards(
    tokens, doc_starts, routes, norm_gain_1, query_weight, key_matrix, value_matrix, out_weight,
    norm_gain_2, router_weight, shared_gate, shared_up, shared_down, expert_gate, expert_up,
    expert_down, out_grad,
):
    contexts, members = lax.axis_size("ctx"), lax.axis_size("wa")
    context, member = lax.axis_index("ctx"), lax.axis_index("wa")
    half_rows, width = tokens.shape[3], tokens.shape[4]
    rows = 2 * half_rows
    share = width // members
    each = share // contexts
    kv_width = key_matrix.shape[1]
    blocks = 2 * contexts
    starts = doc_starts[0]
    own = context[None].astype(jnp.int32)
    inputs = tokens.reshape(rows, width).astype(jnp.float32)
    grad_low = out_grad.reshape(rows, width)
    grad_rows = grad_low.astype(jnp.float32)

    small = jnp.concatenate([norm_gain_1[:, None], norm_gain_2[:, None], router_weight], axis=1)
    small = lax.all_gather(small, "wa", axis=0, tiled=True)
    gain_one = small[:, 0].astype(jnp.float32)
    gain_two = small[:, 1].astype(jnp.float32)
    router_full = small[:, 2:]

    kv_full = lax.all_gather(
        jnp.concatenate([key_matrix, value_matrix], axis=1), "wa", axis=0, tiled=True
    )
    query_full = lax.all_gather(query_weight, "wa", axis=0, tiled=True)
    out_full = lax.all_gather(out_weight, "wa", axis=0, tiled=False)
    hidden_share = shared_gate.shape[1] // members
    pair = jnp.concatenate(
        [
            shared_gate.reshape(share, members, hidden_share),
            shared_up.reshape(share, members, hidden_share),
        ],
        axis=2,
    ).transpose(1, 0, 2)
    pair = lax.all_to_all(pair, "wa", 0, 0, tiled=True).reshape(width, 2 * hidden_share)
    down_share = lax.all_to_all(
        shared_down.reshape(members, hidden_share, share), "wa", 0, 0, tiled=True
    )
    down_share = down_share.transpose(1, 0, 2).reshape(hidden_share, width)

    inverse_one = lax.rsqrt(jnp.mean(inputs * inputs, axis=-1, keepdims=True) + epsilon)
    normed_one = inputs * inverse_one
    normed_low = (normed_one * gain_one).astype(jnp.bfloat16)
    kv_own = dot32(normed_low, kv_full).astype(jnp.bfloat16)
    kv_all = lax.all_gather(kv_own.reshape(2, half_rows, 2 * kv_width), "ctx", axis=0, tiled=True)
    keys, values = kv_all[:, :, :kv_width], kv_all[:, :, kv_width:]
    queries = dot32(normed_low, query_full).astype(jnp.bfloat16)
    by_share = lambda value: value.reshape(rows, contexts, members, each).transpose(2, 0, 1, 3).reshape(
        members, rows, share
    )
    normed_share = exchange(by_share(normed_low), member)
    routes_all = gather_rows(routes.reshape(rows, TOP))
    grad_all = gather_rows(grad_low)

    attended, log_sums = attention_forward(starts, own, queries, keys, values)
    attended_all = gather_rows(attended)
    mixed = jnp.concatenate([dot32(attended, out_full[m]) for m in range(members)], axis=1)
    residual = inputs + mixed
    inverse_two = lax.rsqrt(jnp.mean(residual * residual, axis=-1, keepdims=True) + epsilon)
    normed_two = residual * inverse_two
    second_low = (normed_two * gain_two).astype(jnp.bfloat16)

    second_all = gather_rows(second_low)
    gates_all = dense_gates(dot32(second_all, router_full), routes_all)
    out_part, dx_part, gate_back, expert_terms = experts_call(
        (member * expert_gate.shape[0])[None].astype(jnp.int32),
        second_all, grad_all, second_all.T, grad_all.T, gates_all, gates_all.T,
        expert_gate, expert_up, expert_down, contexts,
    )
    shared_pre = dot32(second_all, pair)
    shared_silu, shared_slope = silu_parts(shared_pre[:, :hidden_share])
    shared_up_pre = shared_pre[:, hidden_share:]
    shared_hidden = (shared_silu * shared_up_pre).astype(jnp.bfloat16)
    shared_back = dot32(grad_all, down_share, ((1,), (1,)))
    pair_low = jnp.concatenate(
        [
            (shared_back * shared_up_pre * shared_slope).astype(jnp.bfloat16),
            (shared_back * shared_silu).astype(jnp.bfloat16),
        ],
        axis=1,
    )
    out_part = out_part + dot32(shared_hidden, down_share)
    dx_part = dx_part + dot32(pair_low, pair, ((1,), (1,)))
    dx_own = reduce_rows(dx_part, jnp.bfloat16)
    out_own = reduce_rows(out_part, jnp.bfloat16)
    gate_back = reduce_rows(gate_back, jnp.float32)
    block_out = (residual + out_own).astype(jnp.bfloat16).reshape(tokens.shape)

    expert_sum = scatter_ctx(expert_terms).astype(jnp.float32)
    expert_gate_grad = expert_sum[:, 0]
    expert_up_grad = expert_sum[:, 1]
    expert_down_grad = expert_sum[:, 2].transpose(0, 2, 1)
    pair_term = dot32(second_all, pair_low, ((0,), (0,)))
    down_term = dot32(grad_all, shared_hidden, ((0,), (0,)))
    shared_term = jnp.concatenate([pair_term, down_term], axis=1).astype(jnp.bfloat16)
    shared_sum = scatter_ctx(shared_term.reshape(contexts, share // contexts * members, 3 * hidden_share))
    shared_sum = lax.all_to_all(
        shared_sum.reshape(members, each, 3 * hidden_share), "wa", 0, 0, tiled=True
    ).astype(jnp.float32)
    units = lambda part: (
        shared_sum[:, :, part * hidden_share : (part + 1) * hidden_share]
    )
    shared_gate_grad = units(0).transpose(1, 0, 2).reshape(each, members * hidden_share)
    shared_up_grad = units(1).transpose(1, 0, 2).reshape(each, members * hidden_share)
    shared_down_grad = units(2).transpose(0, 2, 1).reshape(members * hidden_share, each)

    gates = gates_all[:rows]
    logit_grad = gates * (gate_back - jnp.sum(gates * gate_back, axis=-1, keepdims=True))
    router_term = lax.dot_general(
        logit_grad, second_low.astype(jnp.float32), (((0,), (0,)), ((), ())), precision=highest
    )
    second_grad = dx_own + jnp.dot(logit_grad, router_full.astype(jnp.float32).T, precision=highest)
    gain_two_term, residual_back = rms_back(second_grad, normed_two, inverse_two, gain_two)
    residual_grad = grad_rows + residual_back
    mix_low = residual_grad.astype(jnp.bfloat16)

    mix_share = exchange(by_share(mix_low), member)
    attended_grad = sum(
        dot32(mix_low[:, m * share : (m + 1) * share], out_full[m], ((1,), (1,)))
        for m in range(members)
    ).astype(jnp.bfloat16)
    query_low, key_parts, value_parts = attention_backward(
        starts, own, queries, attended_grad, keys, values, log_sums
    )
    kv_parts = jnp.concatenate([key_parts, value_parts], axis=2)
    kv_low = scatter_ctx(kv_parts.reshape(contexts, rows, 2 * kv_width))
    out_term = dot32(mix_share, attended_all, ((0,), (0,))).astype(jnp.bfloat16)
    query_all = gather_rows(query_low)
    query_term = dot32(normed_share, query_all, ((0,), (0,))).astype(jnp.bfloat16)
    early = jnp.concatenate([out_term, query_term], axis=1).reshape(contexts, each, 2 * width)
    early = scatter_ctx(early).astype(jnp.float32)
    out_weight_grad = early[:, :width].T
    query_weight_grad = early[:, width:]
    kv_low_all = gather_rows(kv_low)
    kv_term = dot32(normed_share, kv_low_all, ((0,), (0,))).astype(jnp.bfloat16)
    late = scatter_ctx(kv_term.reshape(contexts, each, 2 * kv_width)).astype(jnp.float32)
    key_weight_grad = late[:, :kv_width]
    value_weight_grad = late[:, kv_width:]
    first_grad = dot32(query_low, query_full, ((1,), (1,))) + dot32(kv_low, kv_full, ((1,), (1,)))
    gain_one_term, input_back = rms_back(first_grad, normed_one, inverse_one, gain_one)
    tokens_grad = (residual_grad + input_back).astype(jnp.bfloat16).reshape(tokens.shape)

    tiny = scatter_small(jnp.concatenate([router_term, gain_two_term[None], gain_one_term[None]], axis=0))
    return (
        block_out,
        tokens_grad,
        tiny[EXPERTS + 1],
        query_weight_grad,
        key_weight_grad,
        value_weight_grad,
        out_weight_grad,
        tiny[EXPERTS],
        tiny[:EXPERTS].T,
        shared_gate_grad,
        shared_up_grad,
        shared_down_grad,
        expert_gate_grad,
        expert_up_grad,
        expert_down_grad,
    )


def solution(mesh):
    return jax.shard_map(
        shards,
        mesh=mesh,
        in_specs=(
            P("wa", "ctx", None, None, None),
            P("wa", None),
            P("wa", "ctx", None, None, None),
            P("wa"),
            P("wa", None),
            P("wa", None),
            P("wa", None),
            P(None, "wa"),
            P("wa"),
            P("wa", None),
            P("wa", None),
            P("wa", None),
            P(None, "wa"),
            P("wa", None, None),
            P("wa", None, None),
            P("wa", None, None),
            P("wa", "ctx", None, None, None),
        ),
        out_specs=(
            P("wa", "ctx", None, None, None),
            P("wa", "ctx", None, None, None),
            P(("ctx", "wa")),
            P(("ctx", "wa"), None),
            P(("ctx", "wa"), None),
            P(("ctx", "wa"), None),
            P(None, ("ctx", "wa")),
            P(("ctx", "wa")),
            P(("ctx", "wa"), None),
            P(("ctx", "wa"), None),
            P(("ctx", "wa"), None),
            P(None, ("ctx", "wa")),
            P("wa", "ctx", None),
            P("wa", "ctx", None),
            P("wa", None, "ctx"),
        ),
        check_vma=False,
    )
```

time: 2450 us -> 1110 us (0.45)
  waiting for transfers between devices: 1700 us -> 723 us
  matrix products: 297 us -> 60.3 us
  blocking collectives: 140 us -> 5.3 us
  Pallas kernels: 0 us -> 121 us
  local copies, waits for them, and re-layouts: 171 us -> 70 us
  other arithmetic: 83.4 us -> 42.9 us
    reduce_scatter x12 -> x5, waiting for transfers between devices: 1230 us -> 467 us  [scatter_ctx(): return lax.psum_scatter(value, 'ctx', scatter_dimension=0, tiled=True)[0]]
    dot_general x61 -> x23, matrix products: 293 us -> 56.7 us  [the longest x13 32 us: dot32(): lax.dot_general(left, right, (dims, ((), ())), preferred_element_type=jnp...]
    all_to_all x4 -> x5, waiting for transfers between devices: 210 us -> 3.15 us  [the longest x1 3.14 us: scatter_small(): first = jnp.sum(lax.all_to_all(spread, 'wa', 0, 0, tiled=True), axis=0)]
    pallas_call x0 -> x3, Pallas kernels: none -> 121 us  [the longest x1 84.4 us: experts_call(): pl.pallas_call(experts_kernel, grid_spec=pltpu.PrefetchScalarGridSpec(num...]
    ppermute x0 -> x30, waiting for transfers between devices: none -> 99.5 us  [flip(): return lax.ppermute(value, axis, [(i, i ^ bits) for i in range(count)])]
    all_gather x3 -> x1, blocking collectives: 96.1 us -> 5.3 us  [shards(): small = lax.all_gather(small, 'wa', axis=0, tiled=True)]
    unnamed x23 -> x9, waiting for transfers between devices: 74.9 us -> 2 us
    unnamed x1 -> x0, blocking collectives: 43.9 us -> none
  transfers between devices with their start and end apart: 26 -> 44, of which waited for: 22 -> 23; matrix products, arithmetic and copies ran while one was open for 16% -> 10% of each run, Pallas kernels for 0% -> 2%
where the time goes in v1:
time: 1110 us; the launch traced here: 1090 us
  waiting for transfers between devices  723 us (65%)
  Pallas kernels  121 us (11%)
  local copies, waits for them, and re-layouts  70 us (6%)
  matrix products  60.3 us (5%)
  starting transfers between devices  54.7 us (5%)
  other arithmetic  42.9 us (4%)
  between operations  15.1 us (1%)
    reduce_scatter x5, waiting for transfers between devices, scatter_ctx(): return lax.psum_scatter(value, 'ctx', scatter_dimension=0, tiled=True)[0]  467 us
    ppermute x30, waiting for transfers between devices, flip(): return lax.ppermute(value, axis, [(i, i ^ bits) for i in range(count)])  99.5 us
    pallas_call x1, Pallas kernels, experts_call(): pl.pallas_call(experts_kernel, grid_spec=pltpu.PrefetchScalarGridSpec(num...  84.4 us
    all_gather x1, waiting for transfers between devices, shards(): lax.all_gather(kv_own.reshape(2, half_rows, 2 * kv_width), 'ctx', axis=0,...  71.7 us
    all_gather x1, waiting for transfers between devices, shards(): query_full = lax.all_gather(query_weight, 'wa', axis=0, tiled=True)  45.8 us
    dot_general x13, matrix products, dot32(): lax.dot_general(left, right, (dims, ((), ())), preferred_element_type=jnp...  32 us
    ppermute x30, starting transfers between devices, flip(): return lax.ppermute(value, axis, [(i, i ^ bits) for i in range(count)])  30.6 us
    dot_general x9, matrix products, dot32(): return jnp.dot(left, right, preferred_element_type=jnp.float32)  23.5 us
  transfers between devices with their start and end apart: 44, of which 23 were waited for; matrix products, arithmetic and copies ran while one was open for 10% of the time, Pallas kernels for 2%

profile of v1, /device:TPU:10, one launch (start us, length us, event | category | flops | bytes accessed | tf_op | source)
XLA Modules:
  0.0 1092.6 jit_solution(13389343875384495308)
XLA Ops:
  13.6 5.3 all_gather.18
  19.8 19.2 %all-gather.8.cloned.1.call-done = bf16[1536,1024]{1,0:T(8,128)(2,1)} async-done(((bf16[384,1024]{1,0:T(8,128)(2,1)}), bf16[1536,1024]{1,0:T(8,128)(2,1)}) %all-gather.8.cloned.1.call-update) | async-done | bytes 3145744 | tf_op jit(solution)/shard_map/all_gather | solution.py:437
  54.4 45.8 %all-gather.6.cloned.1.call-done = bf16[1536,1536]{1,0:T(8,128)(2,1)} async-done(((bf16[384,1536]{1,0:T(8,128)(2,1)}), bf16[1536,1536]{1,0:T(8,128)(2,1)}) %all-gather.6.cloned.1.call-update) | async-done | bytes 4718608 | tf_op jit(solution)/shard_map/all_gather | solution.py:440
  105.0 71.7 %all-gather.10.cloned.1.call-done = bf16[16,128,1024]{2,1,0:T(8,128)(2,1)} async-done(((bf16[2,128,1024]{2,1,0:T(8,128)(2,1)}), bf16[16,128,1024]{2,1,0:T(8,128)(2,1)}) %all-gather.10.cloned.1.call-update) | async-done | bytes 4194320 | tf_op jit(solution)/shard_map/all_gather | solution.py:460
  180.7 16.8 %attention_forward.1 = (bf16[256,1536]{1,0:T(8,128)(2,1)S(1)}, f32[4,2,384,128]{3,2,1,0:T(8,128)S(1)}) custom-call(s32[8]{0:T(128)S(1)} %bitcast.145, s32[1]{0:T(128)} %bitcast.2.own_ref, bf16[256,1536]{1,0:T(8,128)(2,1)S(1)} %copy-done.2, bf16[16,128,512]{2,1,0:T(8,128)(2,1)S(1)} %get-tuple-element.135.k_ref, bf16[16,128,512]{2,1,0:T(8,128)(2,1)} %get-tuple-element.134.v_ref), custom_call_target="tpu_custom_call" | custom-call | flops 3221225472 | bytes 5767168 | tf_op jit(solution)/shard_map/attention_forward/pallas_call | solution.py:166
  198.7 14.9 %all-gather.12.cloned.1.call-done = bf16[6144,384]{1,0:T(8,128)(2,1)} async-done(((bf16[1536,384]{1,0:T(8,128)(2,1)}), bf16[6144,384]{1,0:T(8,128)(2,1)}) %all-gather.12.cloned.1.call-update) | async-done | bytes 4718608 | tf_op jit(solution)/shard_map/all_gather | solution.py:441
  222.4 5.8 all-to-all-start
  233.6 30.1 %collective-permute-done.6 = s32[256,6]{0,1:T(8,128)S(1)} collective-permute-done((s32[256,6]{0,1:T(8,128)S(1)}, s32[256,6]{0,1:T(8,128)S(1)}, u32[]{:S(2)}, u32[]{:S(2)}) %collective-permute-start.6) | collective-permute-done | bytes 6176 | tf_op jit(solution)/shard_map/ppermute | solution.py:28
  295.2 84.4 %experts.1 = (f32[1024,1536]{1,0:T(8,128)}, f32[1024,1536]{1,0:T(8,128)}, f32[1024,16]{1,0:T(8,128)}, bf16[8,4,3,192,512]{4,3,2,1,0:T(8,128)(2,1)}) custom-call(s32[1]{0:T(128)} %bitcast.5.base_ref, bf16[1024,1536]{1,0:T(8,128)(2,1)} %copy.180.x_ref, bf16[1024,1536]{1,0:T(8,128)(2,1)} %copy.181.dy_ref, bf16[1536,1024]{1,0:T(8,128)(2,1)} %fusion.112.xt_ref, ...), custom_call_target="tpu_custom_call" | custom-call | flops 57982058496 | bytes 62914560 | tf_op jit(solution)/shard_map/experts/pallas_call | solution.py:363
  379.6 6.9 copy.189
  406.9 15.6 %collective-permute-done.14 = f32[256,16]{0,1:T(8,128)S(1)} collective-permute-done((f32[256,16]{0,1:T(8,128)S(1)}, f32[256,16]{0,1:T(8,128)S(1)}, u32[]{:S(2)}, u32[]{:S(2)}) %collective-permute-start.14) | collective-permute-done | bytes 16416 | tf_op jit(solution)/shard_map/ppermute | solution.py:28
  433.4 20.2 %attention_backward.1 = (bf16[256,1536]{1,0:T(8,128)(2,1)}, bf16[16,128,512]{2,1,0:T(8,128)(2,1)}, bf16[16,128,512]{2,1,0:T(8,128)(2,1)}) custom-call(s32[8]{0:T(128)} %bitcast.144, s32[1]{0:T(128)} %bitcast.2.own_ref, bf16[256,1536]{1,0:T(8,128)(2,1)} %convolution_convert_fusion.2.q_ref, bf16[256,1536]{1,0:T(8,128)(2,1)} %fusion.22.do_ref, ...), custom_call_target="tpu_custom_call" | custom-call | flops 8053063680 | bytes 11534336 | tf_op jit(solution)/shard_map/attention_backward/pallas_call | solution.py:264
  453.6 4.9 pad_maximum_fusion
  465.5 8.0 collective-permute-start.18
  476.7 12.5 %collective-permute-done.18 = bf16[256,1536]{1,0:T(8,128)(2,1)} collective-permute-done((bf16[256,1536]{1,0:T(8,128)(2,1)S(1)}, bf16[256,1536]{1,0:T(8,128)(2,1)}, u32[]{:S(2)}, u32[]{:S(2)}) %collective-permute-start.18) | collective-permute-done | bytes 786464 | tf_op jit(solution)/shard_map/ppermute | solution.py:28
  502.0 10.7 collective-permute-done.24
  533.4 23.7 %reduce-scatter.6.cloned.1.call-done = bf16[1,256,1024]{2,1,0:T(8,128)(2,1)} async-done(((bf16[8,256,1024]{2,1,0:T(8,128)(2,1)}), bf16[1,256,1024]{2,1,0:T(8,128)(2,1)}) %reduce-scatter.6.cloned.1.call-update) | async-done | bytes 524304 | tf_op jit(solution)/shard_map/reduce_scatter | solution.py:63
  557.6 13.2 %collective-permute-done.27 = bf16[256,1024]{1,0:T(8,128)(2,1)S(1)} collective-permute-done((bf16[256,1024]{1,0:T(8,128)(2,1)}, bf16[256,1024]{1,0:T(8,128)(2,1)S(1)}, u32[]{:S(2)}, u32[]{:S(2)}) %collective-permute-start.27) | collective-permute-done | bytes 524320 | tf_op jit(solution)/shard_map/ppermute | solution.py:28
  576.4 6.8 copy.187
  594.6 34.0 %reduce-scatter.12.cloned.1.call-done = bf16[1,192,768]{2,1,0:T(8,128)(2,1)} async-done(((bf16[8,192,768]{2,1,0:T(8,128)(2,1)}), bf16[1,192,768]{2,1,0:T(8,128)(2,1)}) %reduce-scatter.12.cloned.1.call-update) | async-done | bytes 294928 | tf_op jit(solution)/shard_map/reduce_scatter | solution.py:63
  632.9 4.9 fusion.88
  640.1 60.4 %reduce-scatter.8.cloned.1.call-done = bf16[1,48,3072]{2,1,0:T(8,128)(2,1)} async-done(((bf16[8,48,3072]{2,1,0:T(8,128)(2,1)}), bf16[1,48,3072]{2,1,0:T(8,128)(2,1)}) %reduce-scatter.8.cloned.1.call-update) | async-done | bytes 294928 | tf_op jit(solution)/shard_map/reduce_scatter | solution.py:63
  731.1 35.1 %reduce-scatter.10.cloned.1.call-done = bf16[1,48,1024]{2,1,0:T(8,128)(2,1)} async-done(((bf16[8,48,1024]{2,1,0:T(8,128)(2,1)}), bf16[1,48,1024]{2,1,0:T(8,128)(2,1)}) %reduce-scatter.10.cloned.1.call-update) | async-done | bytes 98320 | tf_op jit(solution)/shard_map/reduce_scatter | solution.py:63
  767.8 313.4 %reduce-scatter.14.cloned.1.call-done = bf16[1,4,3,192,512]{4,3,2,1,0:T(8,128)(2,1)} async-done(((bf16[8,4,3,192,512]{4,3,2,1,0:T(8,128)(2,1)}), bf16[1,4,3,192,512]{4,3,2,1,0:T(8,128)(2,1)}) %reduce-scatter.14.cloned.1.call-update) | async-done | bytes 2359312 | tf_op jit(solution)/shard_map/reduce_scatter | solution.py:63
  (321 shorter events, 213.3 us)
Async XLA Ops:
  7.2 31.8 %all-gather.8.cloned.1.call-start = ((), (), s32[]{:S(2)}) async-start(), calls=%async_computation.11 | async-start | bytes 3932160 | tf_op jit(solution)/shard_map/all_gather | solution.py:437
  9.4 90.9 %all-gather.6.cloned.1.call-start = ((), (), s32[]{:S(2)}) async-start(), calls=%async_computation.10 | async-start | bytes 5898240 | tf_op jit(solution)/shard_map/all_gather | solution.py:440
  10.2 166.5 %all-gather.10.cloned.1.call-start = ((), (), s32[]{:S(2)}) async-start(), calls=%async_computation.12 | async-start | bytes 4718592 | tf_op jit(solution)/shard_map/all_gather | solution.py:460
  42.8 170.8 %all-gather.12.cloned.1.call-start = ((), (), s32[]{:S(2)}) async-start(), calls=%async_computation.18 | async-start | bytes 5898240 | tf_op jit(solution)/shard_map/all_gather | solution.py:441
  45.0 186.3 %collective-permute-start.3 = (bf16[256,1536]{0,1:T(8,128)(2,1)}, bf16[256,1536]{0,1:T(8,128)(2,1)}, u32[]{:S(2)}, u32[]{:S(2)}) collective-permute-start(bf16[256,1536]{0,1:T(8,128)(2,1)} %copy.214), channel_id=1, source_target_pairs={{0,2},{1,3},{2,0},{3,1},{4,6},{5,7},{6,4},{7,5},{8,10},{9,11},{10,... | collective-permute-start | bytes 2359304 | tf_op jit(solution)/shard_map/ppermute | solution.py:28
  46.5 175.9 %all-to-all-start.1 = ((bf16[4,256,384]{2,1,0:T(8,128)(2,1)}), bf16[4,256,384]{2,1,0:T(8,128)(2,1)}, u32[]{:S(2)}, u32[]{:S(2)}) async-start(bf16[4,256,384]{2,1,0:T(8,128)(2,1)} %bitcast.170), calls=%async_computation.1 | async-start | bytes 1572864 | tf_op jit(solution)/shard_map/all_to_all | solution.py:451
  222.4 45.3 %all-to-all-start = ((bf16[4,384,512]{1,2,0:T(8,128)(2,1)}), bf16[4,384,512]{1,2,0:T(8,128)(2,1)}, u32[]{:S(2)}, u32[]{:S(2)}) async-start(bf16[4,384,512]{1,2,0:T(8,128)(2,1)} %maximum_bitcast_fusion), calls=%async_computation | async-start | bytes 3145728 | tf_op jit(solution)/shard_map/all_to_all | solution.py:450
  228.2 328.8 %reduce-scatter.6.cloned.1.call-start = ((), (), s32[]{:S(2)}) async-start(), calls=%async_computation.13 | async-start | bytes 4718592 | tf_op jit(solution)/shard_map/reduce_scatter | solution.py:63
  231.1 34.0 %collective-permute-start = (bf16[256,1536]{0,1:T(8,128)(2,1)S(1)}, bf16[256,1536]{0,1:T(8,128)(2,1)}, u32[]{:S(2)}, u32[]{:S(2)}) collective-permute-start(bf16[256,1536]{0,1:T(8,128)(2,1)S(1)} %get-tuple-element.129), channel_id=1, source_target_pairs={{0,2},{1,3},{2,0},{3,1},{4,6},{5,7},{6,4},{7,5},{8,10},{9,11},{10,... | collective-permute-start | bytes 2359304 | tf_op jit(solution)/shard_map/ppermute | solution.py:28
  231.2 38.3 %collective-permute-start.4 = (bf16[256,1536]{0,1:T(8,128)(2,1)}, bf16[256,1536]{0,1:T(8,128)(2,1)}, u32[]{:S(2)}, u32[]{:S(2)}) collective-permute-start(bf16[256,1536]{0,1:T(8,128)(2,1)} %copy.214), channel_id=1, source_target_pairs={{0,1},{1,0},{2,3},{3,2},{4,5},{5,4},{6,7},{7,6},{8,9},{9,8},{10,11... | collective-permute-start | bytes 2359304 | tf_op jit(solution)/shard_map/ppermute | solution.py:28
  231.3 38.1 %collective-permute-start.5 = (bf16[256,1536]{0,1:T(8,128)(2,1)}, bf16[256,1536]{0,1:T(8,128)(2,1)}, u32[]{:S(2)}, u32[]{:S(2)}) collective-permute-start(bf16[256,1536]{0,1:T(8,128)(2,1)} %collective-permute-done.3), channel_id=1, source_target_pairs={{0,1},{1,0},{2,3},{3,2},{4,5},{5,4},{6,7},{7,6},{8,9},{9,8},{10,11... | collective-permute-start | bytes 2359304 | tf_op jit(solution)/shard_map/ppermute | solution.py:28
  231.7 32.0 %collective-permute-start.6 = (s32[256,6]{0,1:T(8,128)S(1)}, s32[256,6]{0,1:T(8,128)S(1)}, u32[]{:S(2)}, u32[]{:S(2)}) collective-permute-start(s32[256,6]{0,1:T(8,128)S(1)} %bitcast.184), channel_id=1, source_target_pairs={{0,2},{1,3},{2,0},{3,1},{4,6},{5,7},{6,4},{7,5},{8,10},{9,11},{10,... | collective-permute-start | bytes 18440 | tf_op jit(solution)/shard_map/ppermute | solution.py:28
  233.6 30.1 %collective-permute-start.7 = (s32[256,6]{0,1:T(8,128)S(1)}, s32[256,6]{0,1:T(8,128)S(1)}, u32[]{:S(2)}, u32[]{:S(2)}) collective-permute-start(s32[256,6]{0,1:T(8,128)S(1)} %bitcast.185), channel_id=1, source_target_pairs={{0,1},{1,0},{2,3},{3,2},{4,5},{5,4},{6,7},{7,6},{8,9},{9,8},{10,11... | collective-permute-start | bytes 18440 | tf_op jit(solution)/shard_map/ppermute | solution.py:28
  402.3 20.2 %collective-permute-start.12 = (bf16[256,1536]{0,1:T(8,128)(2,1)}, bf16[256,1536]{0,1:T(8,128)(2,1)S(1)}, u32[]{:S(2)}, u32[]{:S(2)}) collective-permute-start(bf16[256,1536]{0,1:T(8,128)(2,1)} %slice.295), channel_id=1, source_target_pairs={{0,2},{1,3},{2,0},{3,1},{4,6},{5,7},{6,4},{7,5},{8,10},{9,11},{10,... | collective-permute-start | bytes 2359304 | tf_op jit(solution)/shard_map/ppermute | solution.py:28
  458.5 170.1 %reduce-scatter.12.cloned.1.call-start = ((), (), s32[]{:S(2)}) async-start(), calls=%async_computation.16 | async-start | bytes 2654208 | tf_op jit(solution)/shard_map/reduce_scatter | solution.py:63
  465.4 235.1 %reduce-scatter.8.cloned.1.call-start = ((), (), s32[]{:S(2)}) async-start(), calls=%async_computation.14 | async-start | bytes 2654208 | tf_op jit(solution)/shard_map/reduce_scatter | solution.py:63
  465.5 23.6 %collective-permute-start.18 = (bf16[256,1536]{1,0:T(8,128)(2,1)S(1)}, bf16[256,1536]{1,0:T(8,128)(2,1)}, u32[]{:S(2)}, u32[]{:S(2)}) collective-permute-start(bf16[256,1536]{1,0:T(8,128)(2,1)S(1)} %get-tuple-element.24), channel_id=1, source_target_pairs={{0,2},{1,3},{2,0},{3,1},{4,6},{5,7},{6,4},{7,5},{8,10},{9,11},{10,... | collective-permute-start | bytes 2359304 | tf_op jit(solution)/shard_map/ppermute | solution.py:28
  473.5 26.4 %collective-permute-start.19 = (bf16[256,1536]{1,0:T(8,128)(2,1)S(1)}, bf16[256,1536]{1,0:T(8,128)(2,1)}, u32[]{:S(2)}, u32[]{:S(2)}) collective-permute-start(bf16[256,1536]{1,0:T(8,128)(2,1)S(1)} %get-tuple-element.24), channel_id=1, source_target_pairs={{0,1},{1,0},{2,3},{3,2},{4,5},{5,4},{6,7},{7,6},{8,9},{9,8},{10,11... | collective-permute-start | bytes 2359304 | tf_op jit(solution)/shard_map/ppermute | solution.py:28
  492.1 20.7 %collective-permute-start.24 = (bf16[256,1536]{1,0:T(8,128)(2,1)}, bf16[256,1536]{1,0:T(8,128)(2,1)}, u32[]{:S(2)}, u32[]{:S(2)}) collective-permute-start(bf16[256,1536]{1,0:T(8,128)(2,1)} %get-tuple-element.29), channel_id=1, source_target_pairs={{0,2},{1,3},{2,0},{3,1},{4,6},{5,7},{6,4},{7,5},{8,10},{9,11},{10,... | collective-permute-start | bytes 2359304 | tf_op jit(solution)/shard_map/ppermute | solution.py:28
  499.6 29.3 %collective-permute-start.25 = (bf16[256,1536]{1,0:T(8,128)(2,1)}, bf16[256,1536]{1,0:T(8,128)(2,1)S(1)}, u32[]{:S(2)}, u32[]{:S(2)}) collective-permute-start(bf16[256,1536]{1,0:T(8,128)(2,1)} %get-tuple-element.29), channel_id=1, source_target_pairs={{0,1},{1,0},{2,3},{3,2},{4,5},{5,4},{6,7},{7,6},{8,9},{9,8},{10,11... | collective-permute-start | bytes 2359304 | tf_op jit(solution)/shard_map/ppermute | solution.py:28
  500.4 20.7 %collective-permute-start.15 = (bf16[256,384]{0,1:T(8,128)(2,1)S(1)}, bf16[256,384]{0,1:T(8,128)(2,1)S(1)}, u32[]{:S(2)}, u32[]{:S(2)}) collective-permute-start(bf16[256,384]{0,1:T(8,128)(2,1)S(1)} %get-tuple-element.144), channel_id=1, source_target_pairs={{0,2},{1,3},{2,0},{3,1},{4,6},{5,7},{6,4},{7,5},{8,10},{9,11},{10,... | collective-permute-start | bytes 589832 | tf_op jit(solution)/shard_map/ppermute | solution.py:28
  533.3 232.9 %reduce-scatter.10.cloned.1.call-start = ((), (), s32[]{:S(2)}) async-start(), calls=%async_computation.15 | async-start | bytes 884736 | tf_op jit(solution)/shard_map/reduce_scatter | solution.py:63
  575.7 505.6 %reduce-scatter.14.cloned.1.call-start = ((), (), s32[]{:S(2)}) async-start(), calls=%async_computation.17 | async-start | bytes 21233664 | tf_op jit(solution)/shard_map/reduce_scatter | solution.py:63
  594.1 126.8 %collective-permute-start.10 = (bf16[256,1536]{0,1:T(8,128)(2,1)}, bf16[256,1536]{0,1:T(8,128)(2,1)}, u32[]{:S(2)}, u32[]{:S(2)}) collective-permute-start(bf16[256,1536]{0,1:T(8,128)(2,1)} %slice.296), channel_id=1, source_target_pairs={{0,2},{1,3},{2,0},{3,1},{4,6},{5,7},{6,4},{7,5},{8,10},{9,11},{10,... | collective-permute-start | bytes 2359304 | tf_op jit(solution)/shard_map/ppermute | solution.py:28
  (83 other events, 1111.4 us)
Sparse Core Ops, SparseCore 0:
  10.2 28.7 all-gather.7
  40.5 59.6 all-gather.5
  103.0 73.6 all-gather.9
  178.1 35.4 all-gather.11
  458.6 98.3 reduce-scatter.5
  560.8 67.8 reduce-scatter.11
  632.5 67.9 reduce-scatter.7
  704.2 61.9 reduce-scatter.9
  770.1 311.0 reduce-scatter.13

commit v2 on v1

v2 whole, which is shorter than its diff:
```python
import jax
import jax.numpy as jnp
from jax import lax
from jax.experimental import pallas as pl
from jax.experimental.pallas import tpu as pltpu
from jax.sharding import PartitionSpec as P

QUERY_HEADS = 12
KEY_VALUE_HEADS = 4
HEAD_DIM = 128
TOP = 6
EXPERTS = 16

epsilon = 1e-05
large_negative = -1e30
highest = lax.Precision.HIGHEST
ORDER = (0, 2, 1, 3)


def dot32(left, right, dims=None):
    if dims is None:
        return jnp.dot(left, right, preferred_element_type=jnp.float32)
    return lax.dot_general(left, right, (dims, ((), ())), preferred_element_type=jnp.float32)


def flip(value, axis, bits):
    count = lax.axis_size(axis)
    return lax.ppermute(value, axis, [(i, i ^ bits) for i in range(count)])


def shift(value, steps):
    count = lax.axis_size("ctx")
    return lax.ppermute(value, "ctx", [(i, (i + 2 * steps) % count) for i in range(count)])


def after(value, *earlier):
    return lax.optimization_barrier((value,) + earlier)[0]


def gather_pieces(value):
    across = flip(value, "wa", 2)
    return [value, across, flip(value, "wa", 1), flip(across, "wa", 1)]


def ordered(pieces, index):
    chip, core = index // 2, index % 2
    near = [jnp.where(core == i, pieces[0], pieces[2]) for i in range(2)]
    far = [jnp.where(core == i, pieces[1], pieces[3]) for i in range(2)]
    return jnp.concatenate(
        [jnp.where(chip == i // 2, near[i % 2], far[i % 2]) for i in range(4)], axis=0
    )


def exchange(pieces, index):
    received = []
    for bits in ORDER:
        piece = lax.dynamic_index_in_dim(pieces, index ^ bits, 0, keepdims=False)
        received.append(piece if bits == 0 else flip(piece, "wa", bits))
    return jnp.concatenate(received, axis=0)


def reduce_rows(keep, send, kind):
    near = keep + flip(send, "wa", 1).astype(jnp.float32)
    quarter = keep.shape[0] // 2
    return near[:quarter] + flip(near[quarter:].astype(kind), "wa", 2).astype(jnp.float32)


def scatter_small(value):
    rows, width = value.shape
    contexts, members = lax.axis_size("ctx"), lax.axis_size("wa")
    each = width // (contexts * members)
    spread = value.reshape(rows, contexts, members, each).transpose(2, 0, 1, 3)
    spread = spread.reshape(members, rows, contexts * each)
    first = jnp.sum(lax.all_to_all(spread, "wa", 0, 0, tiled=True), axis=0)
    second = first.reshape(rows, contexts, each).transpose(1, 0, 2)
    return jnp.sum(lax.all_to_all(second, "ctx", 0, 0, tiled=True), axis=0)


def sides():
    count = lax.axis_size("ctx")
    return [list(range(side, count, 2)) for side in range(2)]


def scatter_ctx(value, index):
    lines = value.shape[0] // 2
    line, side = index // 2, index % 2
    pairs = value.reshape((lines, 2) + value.shape[1:])
    keep = lax.dynamic_index_in_dim(pairs, side, 1, keepdims=False)
    send = lax.dynamic_index_in_dim(pairs, 1 - side, 1, keepdims=False)
    near = keep.astype(jnp.float32) + flip(send, "ctx", 1).astype(jnp.float32)
    low = near.astype(jnp.bfloat16)
    total = lax.dynamic_index_in_dim(near, line, 0, keepdims=False)
    for steps in range(1, lines):
        piece = lax.dynamic_index_in_dim(low, (line + lines - steps) % lines, 0, keepdims=False)
        total = total + shift(piece, -steps).astype(jnp.float32)
    return total


def scatter_lines(value):
    return lax.psum_scatter(
        value, "ctx", scatter_dimension=0, axis_index_groups=sides(), tiled=True
    )[0]


def silu_parts(values):
    sigmoid_of = jax.nn.sigmoid(values)
    return (values * sigmoid_of, sigmoid_of * (1.0 + values * (1.0 - sigmoid_of)))


def rms_back(grad_normed, normed, inverse, gain_values):
    scaled = grad_normed * gain_values
    return (
        jnp.sum(grad_normed * normed, axis=0),
        inverse * (scaled - normed * jnp.mean(scaled * normed, axis=-1, keepdims=True)),
    )


def attention_masks(starts_ref, block, half_rows, shape):
    rows = block * half_rows + lax.broadcasted_iota(jnp.int32, shape, 0) % half_rows
    first = jnp.zeros(shape, jnp.int32)
    for document in range(1, starts_ref.shape[0]):
        start = starts_ref[document]
        first = jnp.where(start <= rows, jnp.maximum(first, start), first)
    return first, rows


def block_bounds(starts_ref, block, half_rows):
    top = block * half_rows
    first = jnp.int32(0)
    for document in range(1, starts_ref.shape[0]):
        start = starts_ref[document]
        first = jnp.where(start <= top, jnp.maximum(first, start), first)
    return first // half_rows


def block_place(block, own, contexts):
    late = (block >= contexts).astype(jnp.int32)
    device = jnp.where(block < contexts, block, 2 * contexts - 1 - block)
    lines = contexts // 2
    behind = own // 2 - device // 2
    behind = jnp.where(behind < 0, behind + lines, behind)
    return (((own + device) % 2) * lines + behind) * 2 + late


def attention_forward_kernel(starts_ref, own_ref, q_ref, kv_ref, o_ref, lse_ref, s_ref):
    blocks, half_rows, _ = kv_ref.shape
    contexts = blocks // 2
    ratio = q_ref.shape[1] // HEAD_DIM
    rows = ratio * half_rows
    scale = HEAD_DIM ** (-0.5)
    for half in range(2):
        block = own_ref[0] if half == 0 else blocks - 1 - own_ref[0]
        queries = jnp.concatenate(
            [
                q_ref[half * half_rows : (half + 1) * half_rows, h * HEAD_DIM : (h + 1) * HEAD_DIM]
                for h in range(ratio)
            ],
            axis=0,
        )
        low = block_bounds(starts_ref, block, half_rows)
        first, position = attention_masks(starts_ref, block, half_rows, (rows, half_rows))
        column = lax.broadcasted_iota(jnp.int32, (rows, half_rows), 1)

        def score_step(step, running):
            keys = kv_ref[block_place(step, own_ref[0], contexts), :, :HEAD_DIM]
            scores = dot32(queries, keys, ((1,), (1,))) * scale
            at = column + step * half_rows
            scores = jnp.where((at >= first) & (at <= position), scores, large_negative)
            s_ref[step - low] = scores
            return jnp.maximum(running, scores)

        running = lax.fori_loop(
            low, block + 1, score_step, jnp.full((rows, half_rows), large_negative, jnp.float32)
        )
        row_max = jnp.max(running, axis=1, keepdims=True)

        def sum_step(step, total):
            expo = jnp.exp(s_ref[step - low] - row_max)
            s_ref[step - low] = expo
            return total + expo

        total = lax.fori_loop(
            low, block + 1, sum_step, jnp.zeros((rows, half_rows), jnp.float32)
        )
        row_sum = jnp.sum(total, axis=1, keepdims=True)
        inverse = 1.0 / row_sum

        def value_step(step, accum):
            weights = (s_ref[step - low] * inverse).astype(jnp.bfloat16)
            return accum + dot32(weights, kv_ref[block_place(step, own_ref[0], contexts), :, HEAD_DIM:])

        accum = lax.fori_loop(
            low, block + 1, value_step, jnp.zeros((rows, HEAD_DIM), jnp.float32)
        )
        log_sum = row_max + jnp.log(row_sum)
        lse_ref[0, half] = jnp.broadcast_to(log_sum, (rows, half_rows))
        for h in range(ratio):
            o_ref[half * half_rows : (half + 1) * half_rows, h * HEAD_DIM : (h + 1) * HEAD_DIM] = (
                accum[h * half_rows : (h + 1) * half_rows].astype(jnp.bfloat16)
            )


def attention_forward(starts, own, queries, kv):
    rows, width = queries.shape
    blocks, half_rows, _ = kv.shape
    ratio = QUERY_HEADS // KEY_VALUE_HEADS
    stacked = ratio * half_rows
    kv_spec = pl.BlockSpec((blocks, half_rows, 2 * HEAD_DIM), lambda g, *_: (0, 0, g))
    q_spec = pl.BlockSpec((rows, ratio * HEAD_DIM), lambda g, *_: (0, g))
    return pl.pallas_call(
        attention_forward_kernel,
        grid_spec=pltpu.PrefetchScalarGridSpec(
            num_scalar_prefetch=2,
            grid=(KEY_VALUE_HEADS,),
            in_specs=[q_spec, kv_spec],
            out_specs=[
                q_spec,
                pl.BlockSpec((1, 2, stacked, half_rows), lambda g, *_: (g, 0, 0, 0)),
            ],
            scratch_shapes=[pltpu.VMEM((blocks, stacked, half_rows), jnp.float32)],
        ),
        out_shape=(
            jax.ShapeDtypeStruct((rows, width), jnp.bfloat16),
            jax.ShapeDtypeStruct((KEY_VALUE_HEADS, 2, stacked, half_rows), jnp.float32),
        ),
        compiler_params=pltpu.CompilerParams(vmem_limit_bytes=48 << 20),
        cost_estimate=pl.CostEstimate(
            flops=2 * rows * width * blocks * half_rows * 2,
            bytes_accessed=4 * rows * width + 4 * blocks * half_rows * 512,
            transcendentals=rows * QUERY_HEADS * blocks * half_rows // 2,
        ),
        name="attention_forward",
    )(starts, own, queries, kv)


def attention_backward_kernel(
    starts_ref, own_ref, q_ref, do_ref, kv_ref, lse_ref, dq_ref, keep_ref, send_ref, p_ref, dp_ref, dka_ref, dva_ref
):
    blocks, half_rows, _ = kv_ref.shape
    contexts = blocks // 2
    ratio = q_ref.shape[1] // HEAD_DIM
    rows = ratio * half_rows
    scale = HEAD_DIM ** (-0.5)
    dka_ref[...] = jnp.zeros_like(dka_ref)
    dva_ref[...] = jnp.zeros_like(dva_ref)

    def stack(ref, half):
        return jnp.concatenate(
            [
                ref[half * half_rows : (half + 1) * half_rows, h * HEAD_DIM : (h + 1) * HEAD_DIM]
                for h in range(ratio)
            ],
            axis=0,
        )

    for half in range(2):
        block = own_ref[0] if half == 0 else blocks - 1 - own_ref[0]
        queries = stack(q_ref, half)
        grads = stack(do_ref, half)
        log_sum = lse_ref[0, half]
        low = block_bounds(starts_ref, block, half_rows)
        first, position = attention_masks(starts_ref, block, half_rows, (rows, half_rows))
        column = lax.broadcasted_iota(jnp.int32, (rows, half_rows), 1)

        def prob_step(step, running):
            place = block_place(step, own_ref[0], contexts)
            scores = dot32(queries, kv_ref[place, :, :HEAD_DIM], ((1,), (1,))) * scale
            at = column + step * half_rows
            probs = jnp.where(
                (at >= first) & (at <= position), jnp.exp(scores - log_sum), 0.0
            )
            prob_grads = dot32(grads, kv_ref[place, :, HEAD_DIM:], ((1,), (1,)))
            p_ref[step - low] = probs
            dp_ref[step - low] = prob_grads
            return running + probs * prob_grads

        running = lax.fori_loop(
            low, block + 1, prob_step, jnp.zeros((rows, half_rows), jnp.float32)
        )
        delta = jnp.sum(running, axis=1, keepdims=True)

        def grad_step(step, query_grad):
            place = block_place(step, own_ref[0], contexts)
            probs = p_ref[step - low]
            score_low = (probs * (dp_ref[step - low] - delta)).astype(jnp.bfloat16)
            dka_ref[place] += dot32(score_low, queries, ((0,), (0,)))
            dva_ref[place] += dot32(probs.astype(jnp.bfloat16), grads, ((0,), (0,)))
            return query_grad + dot32(score_low, kv_ref[place, :, :HEAD_DIM])

        query_grad = lax.fori_loop(
            low, block + 1, grad_step, jnp.zeros((rows, HEAD_DIM), jnp.float32)
        )
        for h in range(ratio):
            dq_ref[half * half_rows : (half + 1) * half_rows, h * HEAD_DIM : (h + 1) * HEAD_DIM] = (
                query_grad[h * half_rows : (h + 1) * half_rows] * scale
            ).astype(jnp.bfloat16)
    for out_ref, places in ((keep_ref, slice(0, contexts)), (send_ref, slice(contexts, blocks))):
        out_ref[:, :, :HEAD_DIM] = (dka_ref[places] * scale).astype(jnp.bfloat16)
        out_ref[:, :, HEAD_DIM:] = dva_ref[places].astype(jnp.bfloat16)


def attention_backward(starts, own, queries, grads, kv, log_sums):
    rows, width = queries.shape
    blocks, half_rows, kv_width = kv.shape
    ratio = QUERY_HEADS // KEY_VALUE_HEADS
    stacked = ratio * half_rows
    kv_spec = pl.BlockSpec((blocks, half_rows, 2 * HEAD_DIM), lambda g, *_: (0, 0, g))
    part_spec = pl.BlockSpec((blocks // 2, half_rows, 2 * HEAD_DIM), lambda g, *_: (0, 0, g))
    q_spec = pl.BlockSpec((rows, ratio * HEAD_DIM), lambda g, *_: (0, g))
    return pl.pallas_call(
        attention_backward_kernel,
        grid_spec=pltpu.PrefetchScalarGridSpec(
            num_scalar_prefetch=2,
            grid=(KEY_VALUE_HEADS,),
            in_specs=[
                q_spec,
                q_spec,
                kv_spec,
                pl.BlockSpec((1, 2, stacked, half_rows), lambda g, *_: (g, 0, 0, 0)),
            ],
            out_specs=[q_spec, part_spec, part_spec],
            scratch_shapes=[
                pltpu.VMEM((blocks, stacked, half_rows), jnp.float32),
                pltpu.VMEM((blocks, stacked, half_rows), jnp.float32),
                pltpu.VMEM((blocks, half_rows, HEAD_DIM), jnp.float32),
                pltpu.VMEM((blocks, half_rows, HEAD_DIM), jnp.float32),
            ],
        ),
        out_shape=(
            jax.ShapeDtypeStruct((rows, width), jnp.bfloat16),
            jax.ShapeDtypeStruct((blocks // 2, half_rows, kv_width), jnp.bfloat16),
            jax.ShapeDtypeStruct((blocks // 2, half_rows, kv_width), jnp.bfloat16),
        ),
        compiler_params=pltpu.CompilerParams(vmem_limit_bytes=58 << 20),
        cost_estimate=pl.CostEstimate(
            flops=5 * rows * width * blocks * half_rows * 2,
            bytes_accessed=8 * rows * width + 8 * blocks * half_rows * kv_width,
            transcendentals=rows * QUERY_HEADS * blocks * half_rows // 2,
        ),
        name="attention_backward",
    )(starts, own, queries, grads, kv, log_sums)


def experts_kernel(
    at_ref, x0, x1, x2, x3, dy0, dy1, dy2, dy3, g_ref, wg_ref, wu_ref, wd_ref, shared_ref,
    out_ref, dx_ref, out_low_ref, dx_low_ref, dg_ref, term_ref, pair_term_ref,
    x_ref, dy_ref, he_ref, da_ref, db_ref, tail_ref, sem,
):
    local = pl.program_id(0)
    last = pl.num_programs(0) - 1
    expert = at_ref[0] + local
    side = at_ref[1]
    total_rows, width = x_ref.shape
    step_rows = 256
    per = term_ref.shape[4]
    tall = 384
    shared = shared_ref.shape[1] // 3

    @pl.when(local == 0)
    def _():
        copies = []
        for number, (whole, parts) in enumerate(((x_ref, (x0, x1, x2, x3)), (dy_ref, (dy0, dy1, dy2, dy3)))):
            size = total_rows // 4
            for part, source in enumerate(parts):
                copies.append(
                    pltpu.make_async_copy(
                        source, whole.at[pl.ds(part * size, size), :], sem.at[number * 4 + part]
                    )
                )
        for copy in copies:
            copy.start()
        out_ref[...] = jnp.zeros_like(out_ref)
        dx_ref[...] = jnp.zeros_like(dx_ref)
        tail_ref[...] = jnp.zeros_like(tail_ref)
        dg_ref[...] = jnp.zeros_like(dg_ref)
        for copy in copies:
            copy.wait()

    half = total_rows // 2

    def add(number, rows, value):
        if rows.start < half:
            (out_ref, dx_ref)[number][rows, :] += value
        else:
            tail_ref[number, slice(rows.start - half, rows.stop - half), :] += value

    def store(low, begin, target, number):
        for part in range(low.shape[0] // per):
            device = begin // per + part
            target[(side + device) % 2, device // 2, number] = low[part * per : (part + 1) * per]

    for begin in range(0, total_rows, step_rows):
        rows = slice(begin, begin + step_rows)
        x = x_ref[rows, :]
        lane = lax.broadcasted_iota(jnp.int32, (step_rows, g_ref.shape[1]), 1)
        mine = lane == expert
        gate = jnp.sum(jnp.where(mine, g_ref[rows, :], 0.0), axis=1, keepdims=True)
        pre = dot32(x, wg_ref[0])
        up = dot32(x, wu_ref[0])
        back = dot32(dy_ref[rows, :], wd_ref[0], ((1,), (1,)))
        silu, slope = silu_parts(pre)
        hidden = (silu * up).astype(jnp.bfloat16).astype(jnp.float32)
        dg_ref[rows, :] += jnp.where(mine, jnp.sum(hidden * back, axis=1, keepdims=True), 0.0)
        hidden_low = (gate * hidden).astype(jnp.bfloat16)
        he_ref[rows, :] = hidden_low
        add(0, rows, dot32(hidden_low, wd_ref[0]))
        back = gate * back
        pre_low = (back * up * slope).astype(jnp.bfloat16)
        up_low = (back * silu).astype(jnp.bfloat16)
        da_ref[rows, :] = pre_low
        db_ref[rows, :] = up_low
        add(1, rows, dot32(pre_low, wg_ref[0], ((1,), (1,))) + dot32(up_low, wu_ref[0], ((1,), (1,))))

    for begin in range(0, width, tall):
        columns = slice(begin, begin + tall)
        for number, (left, right) in enumerate(((x_ref, da_ref), (x_ref, db_ref), (dy_ref, he_ref))):
            low = dot32(left[:, columns], right[...], ((0,), (0,))).astype(jnp.bfloat16)
            store(low, begin, term_ref.at[0], number)

    @pl.when(local == last)
    def _():
        for begin in range(0, total_rows, step_rows):
            rows = slice(begin, begin + step_rows)
            x = x_ref[rows, :]
            both = dot32(x, shared_ref[:, : 2 * shared])
            pre, up = both[:, :shared], both[:, shared:]
            silu, slope = silu_parts(pre)
            hidden = (silu * up).astype(jnp.bfloat16)
            he_ref[rows, :shared] = hidden
            add(0, rows, dot32(hidden, shared_ref[:, 2 * shared :], ((1,), (1,))))
            back = dot32(dy_ref[rows, :], shared_ref[:, 2 * shared :])
            da_ref[rows, :shared] = (back * up * slope).astype(jnp.bfloat16)
            da_ref[rows, shared:] = (back * silu).astype(jnp.bfloat16)
            add(1, rows, dot32(da_ref[rows, :], shared_ref[:, : 2 * shared], ((1,), (1,))))
        out_low_ref[...] = tail_ref[0].astype(jnp.bfloat16)
        dx_low_ref[...] = tail_ref[1].astype(jnp.bfloat16)
        for begin in range(0, width, tall):
            columns = slice(begin, begin + tall)
            low = dot32(x_ref[:, columns], da_ref[...], ((0,), (0,))).astype(jnp.bfloat16)
            store(low[:, :shared], begin, pair_term_ref, 0)
            store(low[:, shared:], begin, pair_term_ref, 1)
            low = dot32(dy_ref[:, columns], he_ref[:, :shared], ((0,), (0,))).astype(jnp.bfloat16)
            store(low, begin, pair_term_ref, 2)


def experts_call(at, x, dy, gates, gate_w, up_w, down_w, shared_w, contexts):
    rows, width = 4 * x[0].shape[0], x[0].shape[1]
    count, _, hidden = gate_w.shape
    shared = shared_w.shape[1] // 3
    per = width // contexts
    lines = contexts // 2
    once = pl.Buffered(1)
    whole = lambda shape: pl.BlockSpec(shape, lambda e, *_: (0,) * len(shape), pipeline_mode=once)
    weight = lambda shape: pl.BlockSpec((1,) + shape, lambda e, *_: (e, 0, 0))
    term = pl.BlockSpec((1, 2, lines, 3, per, hidden), lambda e, *_: (e, 0, 0, 0, 0, 0))
    term_shape = jax.ShapeDtypeStruct((count, 2, lines, 3, per, hidden), jnp.bfloat16)
    pair_shape = jax.ShapeDtypeStruct((2, lines, 3, per, shared), jnp.bfloat16)
    return pl.pallas_call(
        experts_kernel,
        grid_spec=pltpu.PrefetchScalarGridSpec(
            num_scalar_prefetch=1,
            grid=(count,),
            in_specs=[pl.BlockSpec(memory_space=pl.ANY)] * 8
            + [
                whole((rows, EXPERTS)),
                weight((width, hidden)),
                weight((width, hidden)),
                weight((hidden, width)),
                whole(shared_w.shape),
            ],
            out_specs=[
                whole((rows // 2, width)),
                whole((rows // 2, width)),
                whole((rows // 2, width)),
                whole((rows // 2, width)),
                whole((rows, EXPERTS)),
                term,
                whole(pair_shape.shape),
            ],
            scratch_shapes=[pltpu.VMEM((rows, width), jnp.bfloat16)] * 2
            + [pltpu.VMEM((rows, hidden), jnp.bfloat16)] * 3
            + [pltpu.VMEM((2, rows // 2, width), jnp.float32), pltpu.SemaphoreType.DMA((8,))],
        ),
        out_shape=(
            jax.ShapeDtypeStruct((rows // 2, width), jnp.float32),
            jax.ShapeDtypeStruct((rows // 2, width), jnp.float32),
            jax.ShapeDtypeStruct((rows // 2, width), jnp.bfloat16),
            jax.ShapeDtypeStruct((rows // 2, width), jnp.bfloat16),
            jax.ShapeDtypeStruct((rows, EXPERTS), jnp.float32),
            term_shape,
            pair_shape,
        ),
        compiler_params=pltpu.CompilerParams(vmem_limit_bytes=60 << 20),
        cost_estimate=pl.CostEstimate(
            flops=18 * count * rows * width * hidden + 18 * rows * width * shared,
            bytes_accessed=16 * rows * width + 12 * count * width * hidden,
            transcendentals=count * rows * hidden,
        ),
        name="experts",
    )(at, *x, *dy, gates, gate_w, up_w, down_w, shared_w)


def dense_gates(logits, routes):
    chosen = jnp.any(
        routes[:, :, None] == jnp.arange(EXPERTS, dtype=jnp.int32)[None, None, :], axis=1
    )
    top = jnp.max(jnp.where(chosen, logits, large_negative), axis=-1, keepdims=True)
    expo = jnp.where(chosen, jnp.exp(logits - top), 0.0)
    return expo / jnp.sum(expo, axis=-1, keepdims=True)


def shards(
    tokens, doc_starts, routes, norm_gain_1, query_weight, key_matrix, value_matrix, out_weight,
    norm_gain_2, router_weight, shared_gate, shared_up, shared_down, expert_gate, expert_up,
    expert_down, out_grad,
):
    contexts, members = lax.axis_size("ctx"), lax.axis_size("wa")
    context, member = lax.axis_index("ctx"), lax.axis_index("wa")
    half_rows, width = tokens.shape[3], tokens.shape[4]
    rows = 2 * half_rows
    share = width // members
    each = share // contexts
    lines = contexts // 2
    kv_width = 2 * key_matrix.shape[1]
    starts = doc_starts[0]
    own = context[None].astype(jnp.int32)
    inputs = tokens.reshape(rows, width).astype(jnp.float32)
    grad_low = out_grad.reshape(rows, width)
    grad_rows = grad_low.astype(jnp.float32)

    beside = lambda k, v: jnp.stack(
        [k.reshape(-1, KEY_VALUE_HEADS, HEAD_DIM), v.reshape(-1, KEY_VALUE_HEADS, HEAD_DIM)], axis=2
    ).reshape(-1, kv_width)
    apart = lambda kv: jnp.moveaxis(
        kv.reshape(-1, KEY_VALUE_HEADS, 2, HEAD_DIM), 2, 0
    ).reshape(2, -1, kv_width // 2)
    small = jnp.concatenate([router_weight, norm_gain_1[:, None], norm_gain_2[:, None]], axis=1)
    small = jnp.pad(small, ((0, 0), (0, 128 - EXPERTS - 2)))
    kv_pieces = gather_pieces(jnp.concatenate([beside(key_matrix, value_matrix), small], axis=1))
    kv_across = kv_pieces[1]
    kv_full = ordered(kv_pieces, member)
    router_full = kv_full[:, kv_width : kv_width + EXPERTS]
    gain_one = kv_full[:, kv_width + EXPERTS].astype(jnp.float32)
    gain_two = kv_full[:, kv_width + EXPERTS + 1].astype(jnp.float32)
    kv_full = kv_full[:, :kv_width]
    query_full = lax.all_gather(after(query_weight, kv_across), "wa", axis=0, tiled=True)
    out_full = lax.all_gather(after(out_weight, kv_across), "wa", axis=0, tiled=False)

    inverse_one = lax.rsqrt(jnp.mean(inputs * inputs, axis=-1, keepdims=True) + epsilon)
    normed_one = inputs * inverse_one
    normed_low = (normed_one * gain_one).astype(jnp.bfloat16)
    kv_own = dot32(normed_low, kv_full).astype(jnp.bfloat16).reshape(2, half_rows, kv_width)
    ring, other = [kv_own], []
    for step in range(lines - 1):
        ring.append(shift(after(ring[-1], *other), 1))
        other.append(flip(ring[step], "ctx", 1))
    other.append(flip(ring[-1], "ctx", 1))
    kv_all = jnp.concatenate(ring + other, axis=0)
    queries = dot32(normed_low, query_full).astype(jnp.bfloat16)

    hidden_share = shared_gate.shape[1] // members
    routes_all = jnp.concatenate(gather_pieces(after(routes.reshape(rows, TOP), ring[1])), axis=0)
    grad_pieces = gather_pieces(after(grad_low, ring[2]))
    queries = after(queries, routes_all, *grad_pieces)
    shared_w = jnp.concatenate(
        [
            shared_gate.reshape(share, members, hidden_share),
            shared_up.reshape(share, members, hidden_share),
            shared_down.T.reshape(share, members, hidden_share),
        ],
        axis=2,
    ).transpose(1, 0, 2)
    shared_w = lax.all_to_all(after(shared_w, ring[-1]), "wa", 0, 0, tiled=True)
    shared_w = shared_w.reshape(width, 3 * hidden_share)
    by_share = lambda value: value.reshape(rows, contexts, members, each).transpose(2, 0, 1, 3).reshape(
        members, rows, share
    )

    attended, log_sums = attention_forward(starts, own, queries, kv_all)
    mixed = jnp.concatenate([dot32(attended, out_full[m]) for m in range(members)], axis=1)
    residual = inputs + mixed
    inverse_two = lax.rsqrt(jnp.mean(residual * residual, axis=-1, keepdims=True) + epsilon)
    normed_two = residual * inverse_two
    second_low = after((normed_two * gain_two).astype(jnp.bfloat16), shared_w)

    second_pieces = gather_pieces(second_low)
    logits = jnp.concatenate([dot32(piece, router_full) for piece in second_pieces], axis=0)
    gates_all = dense_gates(logits, routes_all)
    at = jnp.stack([member * expert_gate.shape[0], context % 2]).astype(jnp.int32)
    out_keep, dx_keep, out_send, dx_send, gate_back, terms, pair_terms = experts_call(
        at, second_pieces, grad_pieces, gates_all, expert_gate, expert_up, expert_down,
        shared_w, contexts,
    )
    half = 2 * rows
    first_other = flip(terms[1, 1], "ctx", 1)
    second_other = flip(terms[2, 1], "ctx", 1)
    dx_own = reduce_rows(dx_keep, dx_send, jnp.bfloat16)
    gate_back = reduce_rows(gate_back[:half], gate_back[half:], jnp.float32)
    line_sums = scatter_lines(terms[0].swapaxes(0, 1))

    gates = gates_all[:rows]
    logit_grad = gates * (gate_back - jnp.sum(gates * gate_back, axis=-1, keepdims=True))
    router_term = lax.dot_general(
        logit_grad, second_low.astype(jnp.float32), (((0,), (0,)), ((), ())), precision=highest
    )
    second_grad = dx_own + jnp.dot(logit_grad, router_full.astype(jnp.float32).T, precision=highest)
    gain_two_term, residual_back = rms_back(second_grad, normed_two, inverse_two, gain_two)
    residual_grad = grad_rows + residual_back
    mix_low = residual_grad.astype(jnp.bfloat16)

    attended_grad = sum(
        dot32(mix_low[:, m * share : (m + 1) * share], out_full[m], ((1,), (1,)))
        for m in range(members)
    ).astype(jnp.bfloat16)
    query_low, kv_keep, kv_send = attention_backward(starts, own, queries, attended_grad, kv_all, log_sums)
    by_line = lambda parts: parts.reshape(lines, rows, kv_width)
    kv_near = by_line(kv_keep).astype(jnp.float32) + flip(by_line(kv_send), "ctx", 1).astype(jnp.float32)
    kv_parts = kv_near.astype(jnp.bfloat16)
    kv_low = kv_near[0]
    for steps in range(1, lines):
        kv_low = kv_low + shift(kv_parts[steps], -steps).astype(jnp.float32)
    kv_low = kv_low.astype(jnp.bfloat16)

    by_units = lambda value: value.reshape(-1, contexts, members, each).transpose(2, 0, 1, 3).reshape(
        members, -1, share
    )

    def widened(term, extra):
        count = extra.shape[0]
        total = jnp.sum(exchange(by_units(extra), member).reshape(members, count, share), axis=0)
        columns = jnp.pad(total, ((0, 128 - count), (0, 0))).T
        return jnp.concatenate([term, columns], axis=1).astype(jnp.bfloat16).reshape(contexts, each, -1)

    def side_sum(expert, received):
        near = terms[expert, 0].astype(jnp.float32) + received.astype(jnp.float32)
        return near.astype(jnp.bfloat16)

    near_one = side_sum(1, after(first_other, query_low))
    sum_one = scatter_lines(near_one)
    third_other = flip(after(terms[3, 1], near_one), "ctx", 1)

    normed_share = exchange(after(by_share(normed_low), query_low), member)
    query_all = jnp.concatenate(gather_pieces(query_low), axis=0)
    query_term = dot32(normed_share, query_all, ((0,), (0,))).astype(jnp.bfloat16)
    attended_all = jnp.concatenate(gather_pieces(after(attended, query_low)), axis=0)
    mix_share = exchange(after(by_share(mix_low), query_low), member)
    out_term = dot32(mix_share, attended_all, ((0,), (0,)))
    out_term = widened(out_term, jnp.concatenate([router_term, gain_two_term[None]], axis=0))
    out_own = reduce_rows(out_keep, after(out_send, out_term), jnp.bfloat16)
    block_out = (residual + out_own).astype(jnp.bfloat16).reshape(tokens.shape)

    near_two = side_sum(2, after(second_other, near_one))
    sum_two = scatter_lines(near_two)
    query_weight_grad = scatter_ctx(
        after(query_term.reshape(contexts, each, width), kv_near), context
    )
    out_sum = scatter_ctx(after(out_term, kv_near), context)
    out_weight_grad = out_sum[:, :width].T
    router_weight_grad = out_sum[:, width : width + EXPERTS]
    norm_gain_2_grad = out_sum[:, width + EXPERTS]

    kv_low_all = jnp.concatenate(gather_pieces(kv_low), axis=0)
    kv_term = dot32(normed_share, kv_low_all, ((0,), (0,)))
    first_grad = dot32(query_low, query_full, ((1,), (1,))) + dot32(kv_low, kv_full, ((1,), (1,)))
    gain_one_term, input_back = rms_back(first_grad, normed_one, inverse_one, gain_one)
    tokens_grad = (residual_grad + input_back).astype(jnp.bfloat16).reshape(tokens.shape)
    kv_sum = scatter_ctx(widened(kv_term, gain_one_term[None]), context)
    key_weight_grad, value_weight_grad = apart(kv_sum[:, :kv_width])
    norm_gain_1_grad = kv_sum[:, kv_width]

    near_three = side_sum(3, after(third_other, kv_low))
    sum_three = scatter_lines(near_three)
    sum_zero = line_sums[0].astype(jnp.float32) + flip(line_sums[1], "ctx", 1).astype(jnp.float32)
    expert_sums = [sum_zero, sum_one, sum_two, sum_three]
    expert_gate_grad = jnp.stack([total[0] for total in expert_sums]).astype(jnp.float32)
    expert_up_grad = jnp.stack([total[1] for total in expert_sums]).astype(jnp.float32)
    expert_down_grad = jnp.stack([total[2].T for total in expert_sums]).astype(jnp.float32)

    received = flip(after(pair_terms[1], near_two), "ctx", 1)
    near = pair_terms[0].astype(jnp.float32) + received.astype(jnp.float32)
    low = near.astype(jnp.bfloat16)
    line = context // 2
    shared_sum = lax.dynamic_index_in_dim(near, line, 0, keepdims=False)
    for steps in range(1, lines):
        piece = lax.dynamic_index_in_dim(low, (line + lines - steps) % lines, 0, keepdims=False)
        shared_sum = shared_sum + shift(piece, -steps).astype(jnp.float32)
    shared_sum = shared_sum.reshape(3, members, each, hidden_share).transpose(1, 0, 2, 3)
    shared_sum = lax.all_to_all(shared_sum, "wa", 0, 0, tiled=True)
    shared_gate_grad = shared_sum[:, 0].transpose(1, 0, 2).reshape(each, members * hidden_share)
    shared_up_grad = shared_sum[:, 1].transpose(1, 0, 2).reshape(each, members * hidden_share)
    shared_down_grad = shared_sum[:, 2].transpose(0, 2, 1).reshape(members * hidden_share, each)
    return (
        block_out,
        tokens_grad,
        norm_gain_1_grad,
        query_weight_grad,
        key_weight_grad,
        value_weight_grad,
        out_weight_grad,
        norm_gain_2_grad,
        router_weight_grad,
        shared_gate_grad,
        shared_up_grad,
        shared_down_grad,
        expert_gate_grad,
        expert_up_grad,
        expert_down_grad,
    )


def solution(mesh):
    return jax.shard_map(
        shards,
        mesh=mesh,
        in_specs=(
            P("wa", "ctx", None, None, None),
            P("wa", None),
            P("wa", "ctx", None, None, None),
            P("wa"),
            P("wa", None),
            P("wa", None),
            P("wa", None),
            P(None, "wa"),
            P("wa"),
            P("wa", None),
            P("wa", None),
            P("wa", None),
            P(None, "wa"),
            P("wa", None, None),
            P("wa", None, None),
            P("wa", None, None),
            P("wa", "ctx", None, None, None),
        ),
        out_specs=(
            P("wa", "ctx", None, None, None),
            P("wa", "ctx", None, None, None),
            P(("ctx", "wa")),
            P(("ctx", "wa"), None),
            P(("ctx", "wa"), None),
            P(("ctx", "wa"), None),
            P(None, ("ctx", "wa")),
            P(("ctx", "wa")),
            P(("ctx", "wa"), None),
            P(("ctx", "wa"), None),
            P(("ctx", "wa"), None),
            P(None, ("ctx", "wa")),
            P("wa", "ctx", None),
            P("wa", "ctx", None),
            P("wa", None, "ctx"),
        ),
        check_vma=False,
    )
```

time: 1110 us -> 781 us (0.70)
  waiting for transfers between devices: 723 us -> 354 us
  starting transfers between devices: 54.7 us -> 121 us
  matrix products: 60.3 us -> 40.7 us
  other arithmetic: 42.9 us -> 59.2 us
    reduce_scatter x5 -> x4, waiting for transfers between devices: 467 us -> 0.05 us  [scatter_lines(): lax.psum_scatter(value, 'ctx', scatter_dimension=0, axis_index_groups=sid...]
    ppermute x30 -> x52, waiting for transfers between devices: 99.5 us -> 252 us  [flip(): return lax.ppermute(value, axis, [(i, i ^ bits) for i in range(count)])]
    all_gather x4 -> x2, waiting for transfers between devices: 152 us -> 0.01 us  [the longest x1 0.01 us: shards(): lax.all_gather(after(query_weight, kv_across), 'wa', axis=0, tiled=True)]
    ppermute x0 -> x18, waiting for transfers between devices: none -> 100 us  [shift(): lax.ppermute(value, 'ctx', [(i, (i + 2 * steps) % count) for i in range(c...]
    ppermute x0 -> x18, starting transfers between devices: none -> 50.9 us  [shift(): lax.ppermute(value, 'ctx', [(i, (i + 2 * steps) % count) for i in range(c...]
    ppermute x30 -> x52, starting transfers between devices: 30.6 us -> 60.6 us  [flip(): return lax.ppermute(value, axis, [(i, i ^ bits) for i in range(count)])]
    concatenate x8 -> x5, other arithmetic: 16.8 us -> 0.54 us  [the longest x1 0.31 us: ordered(): jnp.concatenate([jnp.where(chip == i // 2, near[i % 2], far[i % 2]) for i...]
    pallas_call x3 -> x0, local copies, waits for them, and re-layouts: 14.9 us -> none  [experts_call(): pl.pallas_call(experts_kernel, grid_spec=pltpu.PrefetchScalarGridSpec(num...]
  transfers between devices with their start and end apart: 44 -> 78, of which waited for: 23 -> 40; matrix products, arithmetic and copies ran while one was open for 10% -> 18% of each run, Pallas kernels for 2% -> 4%
where the time goes in v2:
time: 781 us; the launch traced here: 772 us
  waiting for transfers between devices  354 us (45%)
  starting transfers between devices  121 us (15%)
  Pallas kernels  120 us (15%)
  local copies, waits for them, and re-layouts  62 us (8%)
  other arithmetic  59.2 us (8%)
  matrix products  40.7 us (5%)
  between operations  15.6 us (2%)
    ppermute x52, waiting for transfers between devices, flip(): return lax.ppermute(value, axis, [(i, i ^ bits) for i in range(count)])  252 us
    ppermute x18, waiting for transfers between devices, shift(): lax.ppermute(value, 'ctx', [(i, (i + 2 * steps) % count) for i in range(c...  100 us
    pallas_call x1, Pallas kernels, experts_call(): pl.pallas_call(experts_kernel, grid_spec=pltpu.PrefetchScalarGridSpec(num...  85.5 us
    ppermute x52, starting transfers between devices, flip(): return lax.ppermute(value, axis, [(i, i ^ bits) for i in range(count)])  60.6 us
    ppermute x18, starting transfers between devices, shift(): lax.ppermute(value, 'ctx', [(i, (i + 2 * steps) % count) for i in range(c...  50.9 us
    dot_general x9, matrix products, dot32(): lax.dot_general(left, right, (dims, ((), ())), preferred_element_type=jnp...  22 us
    unnamed x141, local copies, waits for them, and re-layouts  20.9 us
    pallas_call x1, Pallas kernels, attention_backward(): pl.pallas_call(attention_backward_kernel, grid_spec=pltpu.PrefetchScalarG...  18.6 us
  transfers between devices with their start and end apart: 78, of which 40 were waited for; matrix products, arithmetic and copies ran while one was open for 18% of the time, Pallas kernels for 4%

profile of v2, /device:TPU:10, one launch (start us, length us, event | category | flops | bytes accessed | tf_op | source)
XLA Modules:
  0.0 771.7 jit_solution(11960017511259916552)
XLA Ops:
  10.6 20.9 %collective-permute-done.1 = bf16[384,1152]{0,1:T(8,128)(2,1)S(1)} collective-permute-done((bf16[384,1152]{0,1:T(8,128)(2,1)S(1)}, bf16[384,1152]{0,1:T(8,128)(2,1)S(1)}, u32[]{:S(2)}, u32[]{:S(2)}) %collective-permute-start.1) | collective-permute-done | bytes 884768 | tf_op jit(solution)/shard_map/ppermute | solution.py:28
  46.4 11.0 %collective-permute-done.3 = bf16[2,128,1024]{2,1,0:T(8,128)(2,1)} collective-permute-done((bf16[2,128,1024]{2,1,0:T(8,128)(2,1)}, bf16[2,128,1024]{2,1,0:T(8,128)(2,1)}, u32[]{:S(2)}, u32[]{:S(2)}) %collective-permute-start.3) | collective-permute-done | bytes 524320 | tf_op jit(solution)/shard_map/ppermute | solution.py:33
  78.7 6.7 collective-permute-done.13
  96.8 13.6 %collective-permute-done.9.dy1 = bf16[256,1536]{1,0:T(8,128)(2,1)} collective-permute-done((bf16[256,1536]{1,0:T(8,128)(2,1)S(1)}, bf16[256,1536]{1,0:T(8,128)(2,1)}, u32[]{:S(2)}, u32[]{:S(2)}) %collective-permute-start.9) | collective-permute-done | bytes 786464 | tf_op jit(solution)/shard_map/ppermute | solution.py:28
  119.0 15.4 %attention_forward.1 = (bf16[256,1536]{1,0:T(8,128)(2,1)S(1)}, f32[4,2,384,128]{3,2,1,0:T(8,128)S(1)}) custom-call(s32[8]{0:T(128)S(1)} %bitcast.401, s32[1]{0:T(128)} %bitcast.2.own_ref, bf16[256,1536]{1,0:T(8,128)(2,1)S(1)} %convolution_convert_fusion.q_ref, bf16[16,128,1024]{2,1,0:T(8,128)(2,1)} %constant_dynamic-update-slice_fusion.4.kv_ref), custom_call_target="tpu_custom_call" | custom-call | flops 3221225472 | bytes 5767168 | tf_op jit(solution)/shard_map/attention_forward/pallas_call | solution.py:210
  144.5 9.9 %collective-permute-start.17 = (bf16[256,1536]{1,0:T(8,128)(2,1)}, bf16[256,1536]{1,0:T(8,128)(2,1)}, u32[]{:S(2)}, u32[]{:S(2)}) collective-permute-start(bf16[256,1536]{1,0:T(8,128)(2,1)} %multiply_convert_fusion.1.x0), channel_id=1, source_target_pairs={{0,1},{1,0},{2,3},{3,2},{4,5},{5,4},{6,7},{7,6},{8,9},{9,8},{10,11... | collective-permute-start | bytes 2359304 | tf_op jit(solution)/shard_map/ppermute | solution.py:28
  155.7 9.3 %collective-permute-start.18 = (bf16[256,1536]{1,0:T(8,128)(2,1)}, bf16[256,1536]{1,0:T(8,128)(2,1)S(1)}, u32[]{:S(2)}, u32[]{:S(2)}) collective-permute-start(bf16[256,1536]{1,0:T(8,128)(2,1)} %collective-permute-done.16.x1), channel_id=1, source_target_pairs={{0,1},{1,0},{2,3},{3,2},{4,5},{5,4},{6,7},{7,6},{8,9},{9,8},{10,11... | collective-permute-start | bytes 2359304 | tf_op jit(solution)/shard_map/ppermute | solution.py:28
  171.6 85.5 %experts.1 = (f32[512,1536]{1,0:T(8,128)}, f32[512,1536]{1,0:T(8,128)}, bf16[512,1536]{1,0:T(8,128)(2,1)}, bf16[512,1536]{1,0:T(8,128)(2,1)}, f32[1024,16]{1,0:T...) custom-call(s32[2]{0:T(128)} %pad_add_fusion.at_ref, ...), custom_call_target="tpu_custom_call" | custom-call | flops 65229815808 | bytes 62914560 | tf_op jit(solution)/shard_map/experts/pallas_call | solution.py:458
  280.3 8.2 %collective-permute-done.20 = bf16[256,1536]{1,0:T(8,128)(2,1)S(1)} collective-permute-done((bf16[256,1536]{1,0:T(8,128)(2,1)S(1)}, bf16[256,1536]{1,0:T(8,128)(2,1)S(1)}, u32[]{:S(2)}, u32[]{:S(2)}) %collective-permute-start.20) | collective-permute-done | bytes 786464 | tf_op jit(solution)/shard_map/ppermute | solution.py:28
  295.1 18.6 %attention_backward.1 = (bf16[256,1536]{1,0:T(8,128)(2,1)}, bf16[8,128,1024]{2,1,0:T(8,128)(2,1)}, bf16[8,128,1024]{2,1,0:T(8,128)(2,1)}) custom-call(s32[8]{0:T(128)} %bitcast.400, s32[1]{0:T(128)} %bitcast.2.own_ref, bf16[256,1536]{1,0:T(8,128)(2,1)} %copy-done.1, bf16[256,1536]{1,0:T(8,128)(2,1)} %fusion.29.do_ref, ...), custom_call_target="tpu_custom_call" | custom-call | flops 8053063680 | bytes 19922944 | tf_op jit(solution)/shard_map/attention_backward/pallas_call | solution.py:310
  313.7 17.4 %collective-permute-done.63 = bf16[4,3,192,512]{3,2,1,0:T(8,128)(2,1)} collective-permute-done((bf16[4,3,192,512]{3,2,1,0:T(8,128)(2,1)S(1)}, bf16[4,3,192,512]{3,2,1,0:T(8,128)(2,1)}, u32[]{:S(2)}, u32[]{:S(2)}) %collective-permute-start.63) | collective-permute-done | bytes 2359328 | tf_op jit(solution)/shard_map/ppermute | solution.py:28
  339.6 45.0 %collective-permute-done.34 = bf16[4,256,1024]{2,1,0:T(8,128)(2,1)S(1)} collective-permute-done((bf16[4,256,1024]{2,1,0:T(8,128)(2,1)}, bf16[4,256,1024]{2,1,0:T(8,128)(2,1)S(1)}, u32[]{:S(2)}, u32[]{:S(2)}) %collective-permute-start.34) | collective-permute-done | bytes 2097184 | tf_op jit(solution)/shard_map/ppermute | solution.py:28
  388.1 12.7 %collective-permute-start.36 = (bf16[256,1024]{1,0:T(8,128)(2,1)S(1)}, bf16[256,1024]{1,0:T(8,128)(2,1)S(1)}, u32[]{:S(2)}, u32[]{:S(2)}) collective-permute-start(bf16[256,1024]{1,0:T(8,128)(2,1)S(1)} %get-tuple-element.227), channel_id=1, source_target_pairs={{0,16},{4,20},{8,24},{12,28},{16,0},{20,4},{24,8},{28,12},{1,17},{... | collective-permute-start | bytes 1572872 | tf_op jit(solution)/shard_map/ppermute | solution.py:33
  403.7 31.5 %collective-permute-done.62 = bf16[4,3,192,512]{3,2,1,0:T(8,128)(2,1)S(1)} collective-permute-done((bf16[4,3,192,512]{3,2,1,0:T(8,128)(2,1)}, bf16[4,3,192,512]{3,2,1,0:T(8,128)(2,1)S(1)}, u32[]{:S(2)}, u32[]{:S(2)}) %collective-permute-start.62) | collective-permute-done | bytes 2359328 | tf_op jit(solution)/shard_map/ppermute | solution.py:28
  439.8 10.6 %collective-permute-done.37 = bf16[256,1024]{1,0:T(8,128)(2,1)S(1)} collective-permute-done((bf16[256,1024]{1,0:T(8,128)(2,1)S(1)}, bf16[256,1024]{1,0:T(8,128)(2,1)S(1)}, u32[]{:S(2)}, u32[]{:S(2)}) %collective-permute-start.37) | collective-permute-done | bytes 524320 | tf_op jit(solution)/shard_map/ppermute | solution.py:33
  451.5 32.2 %collective-permute-done.69 = bf16[4,3,192,512]{3,2,1,0:T(8,128)(2,1)S(1)} collective-permute-done((bf16[4,3,192,512]{3,2,1,0:T(8,128)(2,1)}, bf16[4,3,192,512]{3,2,1,0:T(8,128)(2,1)S(1)}, u32[]{:S(2)}, u32[]{:S(2)}) %collective-permute-start.69) | collective-permute-done | bytes 2359328 | tf_op jit(solution)/shard_map/ppermute | solution.py:28
  518.0 9.1 %collective-permute-done.29 = f32[17,384]{1,0:T(8,128)S(1)} collective-permute-done((f32[17,384]{1,0:T(8,128)S(1)}, f32[17,384]{1,0:T(8,128)S(1)}, u32[]{:S(2)}, u32[]{:S(2)}) %collective-permute-start.29) | collective-permute-done | bytes 26144 | tf_op jit(solution)/shard_map/ppermute | solution.py:28
  569.5 16.2 %collective-permute-done.54 = bf16[4,48,1536]{2,1,0:T(8,128)(2,1)} collective-permute-done((bf16[4,48,1536]{2,1,0:T(8,128)(2,1)}, bf16[4,48,1536]{2,1,0:T(8,128)(2,1)}, u32[]{:S(2)}, u32[]{:S(2)}) %collective-permute-start.54) | collective-permute-done | bytes 589856 | tf_op jit(solution)/shard_map/ppermute | solution.py:28
  587.1 11.1 %collective-permute-start.56 = (bf16[48,1536]{1,0:T(8,128)(2,1)S(1)}, bf16[48,1536]{1,0:T(8,128)(2,1)S(1)}, u32[]{:S(2)}, u32[]{:S(2)}) collective-permute-start(bf16[48,1536]{1,0:T(8,128)(2,1)S(1)} %get-tuple-element.260), channel_id=1, source_target_pairs={{0,16},{4,20},{8,24},{12,28},{16,0},{20,4},{24,8},{28,12},{1,17},{... | collective-permute-start | bytes 442376 | tf_op jit(solution)/shard_map/ppermute | solution.py:33
  607.2 9.2 %collective-permute-done.56 = bf16[48,1536]{1,0:T(8,128)(2,1)S(1)} collective-permute-done((bf16[48,1536]{1,0:T(8,128)(2,1)S(1)}, bf16[48,1536]{1,0:T(8,128)(2,1)S(1)}, u32[]{:S(2)}, u32[]{:S(2)}) %collective-permute-start.56) | collective-permute-done | bytes 147488 | tf_op jit(solution)/shard_map/ppermute | solution.py:33
  619.8 14.0 %collective-permute-done.57 = bf16[48,1536]{1,0:T(8,128)(2,1)S(1)} collective-permute-done((bf16[48,1536]{1,0:T(8,128)(2,1)S(1)}, bf16[48,1536]{1,0:T(8,128)(2,1)S(1)}, u32[]{:S(2)}, u32[]{:S(2)}) %collective-permute-start.57) | collective-permute-done | bytes 147488 | tf_op jit(solution)/shard_map/ppermute | solution.py:33
  651.7 17.6 %collective-permute-done.64 = bf16[4,3,192,256]{3,2,1,0:T(8,128)(2,1)} collective-permute-done((bf16[4,3,192,256]{3,2,1,0:T(8,128)(2,1)}, bf16[4,3,192,256]{3,2,1,0:T(8,128)(2,1)}, u32[]{:S(2)}, u32[]{:S(2)}) %collective-permute-start.64) | collective-permute-done | bytes 1179680 | tf_op jit(solution)/shard_map/ppermute | solution.py:28
  721.1 9.1 %collective-permute-done.49 = bf16[48,1152]{0,1:T(8,128)(2,1)} collective-permute-done((bf16[48,1152]{0,1:T(8,128)(2,1)S(1)}, bf16[48,1152]{0,1:T(8,128)(2,1)}, u32[]{:S(2)}, u32[]{:S(2)}) %collective-permute-start.49) | collective-permute-done | bytes 110624 | tf_op jit(solution)/shard_map/ppermute | solution.py:33
  749.3 10.1 %collective-permute-done.68 = bf16[3,192,512]{2,1,0:T(8,128)(2,1)} collective-permute-done((bf16[3,192,512]{2,1,0:T(8,128)(2,1)}, bf16[3,192,512]{2,1,0:T(8,128)(2,1)}, u32[]{:S(2)}, u32[]{:S(2)}) %collective-permute-start.68) | collective-permute-done | bytes 589856 | tf_op jit(solution)/shard_map/ppermute | solution.py:28
  (423 shorter events, 311.2 us)
Async XLA Ops:
  7.2 107.7 %all-gather.4.cloned.1.call-start = ((), (), s32[]{:S(2)}) async-start(), calls=%async_computation.6 | async-start | bytes 5898240 | tf_op jit(solution)/shard_map/all_gather | solution.py:546
  31.4 104.1 %all-gather.6.cloned.1.call-start = ((), (), s32[]{:S(2)}) async-start(), calls=%async_computation.11 | async-start | bytes 5898240 | tf_op jit(solution)/shard_map/all_gather | solution.py:547
  75.5 34.9 %collective-permute-start.9 = (bf16[256,1536]{1,0:T(8,128)(2,1)S(1)}, bf16[256,1536]{1,0:T(8,128)(2,1)}, u32[]{:S(2)}, u32[]{:S(2)}) collective-permute-start(bf16[256,1536]{1,0:T(8,128)(2,1)S(1)} %bitcast.413), channel_id=1, source_target_pairs={{0,2},{1,3},{2,0},{3,1},{4,6},{5,7},{6,4},{7,5},{8,10},{9,11},{10,... | collective-permute-start | bytes 2359304 | tf_op jit(solution)/shard_map/ppermute | solution.py:28
  77.2 34.0 %collective-permute-start.14 = (bf16[2,128,1024]{2,1,0:T(8,128)(2,1)S(1)}, bf16[2,128,1024]{2,1,0:T(8,128)(2,1)}, u32[]{:S(2)}, u32[]{:S(2)}) collective-permute-start(bf16[2,128,1024]{2,1,0:T(8,128)(2,1)S(1)} %collective-permute-done.8), channel_id=1, source_target_pairs={{0,4},{4,0},{8,12},{12,8},{16,20},{20,16},{24,28},{28,24},{1,5},{5... | collective-permute-start | bytes 1572872 | tf_op jit(solution)/shard_map/ppermute | solution.py:28
  78.7 40.3 %collective-permute-start.10 = (bf16[256,1536]{1,0:T(8,128)(2,1)S(1)}, bf16[256,1536]{1,0:T(8,128)(2,1)}, u32[]{:S(2)}, u32[]{:S(2)}) collective-permute-start(bf16[256,1536]{1,0:T(8,128)(2,1)S(1)} %bitcast.414), channel_id=1, source_target_pairs={{0,1},{1,0},{2,3},{3,2},{4,5},{5,4},{6,7},{7,6},{8,9},{9,8},{10,11... | collective-permute-start | bytes 2359304 | tf_op jit(solution)/shard_map/ppermute | solution.py:28
  87.8 55.6 %all-to-all-start = ((bf16[4,384,768]{2,1,0:T(8,128)(2,1)}), bf16[4,384,768]{2,1,0:T(8,128)(2,1)}, u32[]{:S(2)}, u32[]{:S(2)}) async-start(bf16[4,384,768]{2,1,0:T(8,128)(2,1)} %maximum_bitcast_fusion), calls=%async_computation | async-start | bytes 4718592 | tf_op jit(solution)/shard_map/all_to_all | solution.py:573
  92.8 649.1 %reduce-scatter.5.cloned.1.call-start = ((), (), s32[]{:S(2)}) async-start(), calls=%async_computation.7 | async-start | bytes 5898240 | tf_op jit(solution)/shard_map/reduce_scatter | solution.py:100
  262.1 483.2 %reduce-scatter.7.cloned.1.call-start = ((), (), s32[]{:S(2)}) async-start(), calls=%async_computation.8 | async-start | bytes 2949120 | tf_op jit(solution)/shard_map/reduce_scatter | solution.py:100
  277.0 54.2 %collective-permute-start.63 = (bf16[4,3,192,512]{3,2,1,0:T(8,128)(2,1)S(1)}, bf16[4,3,192,512]{3,2,1,0:T(8,128)(2,1)}, u32[]{:S(2)}, u32[]{:S(2)}) collective-permute-start(bf16[4,3,192,512]{3,2,1,0:T(8,128)(2,1)S(1)} %get-tuple-element.215), channel_id=1, source_target_pairs={{0,4},{4,0},{8,12},{12,8},{16,20},{20,16},{24,28},{28,24},{1,5},{5... | collective-permute-start | bytes 7077896 | tf_op jit(solution)/shard_map/ppermute | solution.py:28
  335.7 411.0 %reduce-scatter.9.cloned.1.call-start = ((), (), s32[]{:S(2)}) async-start(), calls=%async_computation.9 | async-start | bytes 2949120 | tf_op jit(solution)/shard_map/reduce_scatter | solution.py:100
  335.8 48.8 %collective-permute-start.34 = (bf16[4,256,1024]{2,1,0:T(8,128)(2,1)}, bf16[4,256,1024]{2,1,0:T(8,128)(2,1)S(1)}, u32[]{:S(2)}, u32[]{:S(2)}) collective-permute-start(bf16[4,256,1024]{2,1,0:T(8,128)(2,1)} %bitcast.456), channel_id=1, source_target_pairs={{0,4},{4,0},{8,12},{12,8},{16,20},{20,16},{24,28},{28,24},{1,5},{5... | collective-permute-start | bytes 6291464 | tf_op jit(solution)/shard_map/ppermute | solution.py:28
  337.6 97.6 %collective-permute-start.62 = (bf16[4,3,192,512]{3,2,1,0:T(8,128)(2,1)}, bf16[4,3,192,512]{3,2,1,0:T(8,128)(2,1)S(1)}, u32[]{:S(2)}, u32[]{:S(2)}) collective-permute-start(bf16[4,3,192,512]{3,2,1,0:T(8,128)(2,1)} %get-tuple-element.216), channel_id=1, source_target_pairs={{0,4},{4,0},{8,12},{12,8},{16,20},{20,16},{24,28},{28,24},{1,5},{5... | collective-permute-start | bytes 7077896 | tf_op jit(solution)/shard_map/ppermute | solution.py:28
  337.9 145.9 %collective-permute-start.69 = (bf16[4,3,192,512]{3,2,1,0:T(8,128)(2,1)}, bf16[4,3,192,512]{3,2,1,0:T(8,128)(2,1)S(1)}, u32[]{:S(2)}, u32[]{:S(2)}) collective-permute-start(bf16[4,3,192,512]{3,2,1,0:T(8,128)(2,1)} %get-tuple-element.77), channel_id=1, source_target_pairs={{0,4},{4,0},{8,12},{12,8},{16,20},{20,16},{24,28},{28,24},{1,5},{5... | collective-permute-start | bytes 7077896 | tf_op jit(solution)/shard_map/ppermute | solution.py:28
  387.4 47.8 %collective-permute-start.35 = (bf16[256,1024]{1,0:T(8,128)(2,1)S(1)}, bf16[256,1024]{1,0:T(8,128)(2,1)S(1)}, u32[]{:S(2)}, u32[]{:S(2)}) collective-permute-start(bf16[256,1024]{1,0:T(8,128)(2,1)S(1)} %get-tuple-element.225), channel_id=1, source_target_pairs={{0,24},{4,28},{8,0},{12,4},{16,8},{20,12},{24,16},{28,20},{1,25},{... | collective-permute-start | bytes 1572872 | tf_op jit(solution)/shard_map/ppermute | solution.py:33
  388.1 51.7 %collective-permute-start.36 = (bf16[256,1024]{1,0:T(8,128)(2,1)S(1)}, bf16[256,1024]{1,0:T(8,128)(2,1)S(1)}, u32[]{:S(2)}, u32[]{:S(2)}) collective-permute-start(bf16[256,1024]{1,0:T(8,128)(2,1)S(1)} %get-tuple-element.227), channel_id=1, source_target_pairs={{0,16},{4,20},{8,24},{12,28},{16,0},{20,4},{24,8},{28,12},{1,17},{... | collective-permute-start | bytes 1572872 | tf_op jit(solution)/shard_map/ppermute | solution.py:33
  400.8 49.6 %collective-permute-start.37 = (bf16[256,1024]{1,0:T(8,128)(2,1)S(1)}, bf16[256,1024]{1,0:T(8,128)(2,1)S(1)}, u32[]{:S(2)}, u32[]{:S(2)}) collective-permute-start(bf16[256,1024]{1,0:T(8,128)(2,1)S(1)} %get-tuple-element.226), channel_id=1, source_target_pairs={{0,8},{4,12},{8,16},{12,20},{16,24},{20,28},{24,0},{28,4},{1,9},{5... | collective-permute-start | bytes 1572872 | tf_op jit(solution)/shard_map/ppermute | solution.py:33
  489.8 258.2 %reduce-scatter.11.cloned.1.call-start = ((), (), s32[]{:S(2)}) async-start(), calls=%async_computation.10 | async-start | bytes 2949120 | tf_op jit(solution)/shard_map/reduce_scatter | solution.py:100
  503.7 39.7 %collective-permute-start.27 = (bf16[256,1536]{1,0:T(8,128)(2,1)S(1)}, bf16[256,1536]{1,0:T(8,128)(2,1)}, u32[]{:S(2)}, u32[]{:S(2)}) collective-permute-start(bf16[256,1536]{1,0:T(8,128)(2,1)S(1)} %get-tuple-element.65), channel_id=1, source_target_pairs={{0,1},{1,0},{2,3},{3,2},{4,5},{5,4},{6,7},{7,6},{8,9},{9,8},{10,11... | collective-permute-start | bytes 2359304 | tf_op jit(solution)/shard_map/ppermute | solution.py:28
  549.9 94.9 %collective-permute-start.32 = (bf16[512,1536]{1,0:T(8,128)(2,1)}, bf16[512,1536]{1,0:T(8,128)(2,1)}, u32[]{:S(2)}, u32[]{:S(2)}) collective-permute-start(bf16[512,1536]{1,0:T(8,128)(2,1)} %get-tuple-element.66), channel_id=1, source_target_pairs={{0,1},{1,0},{2,3},{3,2},{4,5},{5,4},{6,7},{7,6},{8,9},{9,8},{10,11... | collective-permute-start | bytes 4718600 | tf_op jit(solution)/shard_map/ppermute | solution.py:28
  556.1 42.0 %collective-permute-start.58 = (bf16[4,48,1664]{2,1,0:T(8,128)(2,1)S(1)}, bf16[4,48,1664]{2,1,0:T(8,128)(2,1)}, u32[]{:S(2)}, u32[]{:S(2)}) collective-permute-start(bf16[4,48,1664]{2,1,0:T(8,128)(2,1)S(1)} %dynamic-slice_bitcast_fusion), channel_id=1, source_target_pairs={{0,4},{4,0},{8,12},{12,8},{16,20},{20,16},{24,28},{28,24},{1,5},{5... | collective-permute-start | bytes 1916936 | tf_op jit(solution)/shard_map/ppermute | solution.py:28
  562.3 82.5 %collective-permute-start.41 = (bf16[256,1024]{1,0:T(8,128)(2,1)}, bf16[256,1024]{1,0:T(8,128)(2,1)}, u32[]{:S(2)}, u32[]{:S(2)}) collective-permute-start(bf16[256,1024]{1,0:T(8,128)(2,1)} %fusion.64), channel_id=1, source_target_pairs={{0,2},{1,3},{2,0},{3,1},{4,6},{5,7},{6,4},{7,5},{8,10},{9,11},{10,... | collective-permute-start | bytes 1572872 | tf_op jit(solution)/shard_map/ppermute | solution.py:28
  598.2 35.7 %collective-permute-start.57 = (bf16[48,1536]{1,0:T(8,128)(2,1)S(1)}, bf16[48,1536]{1,0:T(8,128)(2,1)S(1)}, u32[]{:S(2)}, u32[]{:S(2)}) collective-permute-start(bf16[48,1536]{1,0:T(8,128)(2,1)S(1)} %get-tuple-element.259), channel_id=1, source_target_pairs={{0,8},{4,12},{8,16},{12,20},{16,24},{20,28},{24,0},{28,4},{1,9},{5... | collective-permute-start | bytes 442376 | tf_op jit(solution)/shard_map/ppermute | solution.py:33
  607.2 33.3 %collective-permute-start.59 = (bf16[48,1664]{1,0:T(8,128)(2,1)S(1)}, bf16[48,1664]{1,0:T(8,128)(2,1)S(1)}, u32[]{:S(2)}, u32[]{:S(2)}) collective-permute-start(bf16[48,1664]{1,0:T(8,128)(2,1)S(1)} %get-tuple-element.243), channel_id=1, source_target_pairs={{0,24},{4,28},{8,0},{12,4},{16,8},{20,12},{24,16},{28,20},{1,25},{... | collective-permute-start | bytes 479240 | tf_op jit(solution)/shard_map/ppermute | solution.py:33
  705.1 34.7 %all-to-all-start.1 = ((f32[4,3,48,256]{3,2,1,0:T(8,128)}), f32[4,3,48,256]{3,2,1,0:T(8,128)S(1)}, u32[]{:S(2)}, u32[]{:S(2)}) async-start(f32[4,3,48,256]{3,2,1,0:T(8,128)} %copy.248), calls=%async_computation.1 | async-start | bytes 1179648 | tf_op jit(solution)/shard_map/all_to_all | solution.py:688
  (114 other events, 1263.8 us)
Sparse Core Ops, SparseCore 0:
  31.6 37.6 all-gather.3
  70.8 62.9 all-gather.5
  262.3 96.4 reduce-scatter.4
  360.9 71.1 reduce-scatter.6
  489.9 57.7 reduce-scatter.8
  563.9 79.5 reduce-scatter.10

commit v3 on v2

--- a/solution.py
+++ b/solution.py
@@ -1,3 +1,5 @@
+import functools
+
 import jax
 import jax.numpy as jnp
 from jax import lax
@@ -56,7 +58,7 @@
     for bits in ORDER:
         piece = lax.dynamic_index_in_dim(pieces, index ^ bits, 0, keepdims=False)
         received.append(piece if bits == 0 else flip(piece, "wa", bits))
-    return jnp.concatenate(received, axis=0)
+    return received
 
 
 def reduce_rows(keep, send, kind):
@@ -81,13 +83,14 @@
     return [list(range(side, count, 2)) for side in range(2)]
 
 
-def scatter_ctx(value, index):
-    lines = value.shape[0] // 2
-    line, side = index // 2, index % 2
-    pairs = value.reshape((lines, 2) + value.shape[1:])
-    keep = lax.dynamic_index_in_dim(pairs, side, 1, keepdims=False)
-    send = lax.dynamic_index_in_dim(pairs, 1 - side, 1, keepdims=False)
-    near = keep.astype(jnp.float32) + flip(send, "ctx", 1).astype(jnp.float32)
+def to_side(value, index):
+    pairs = value.reshape((value.shape[0] // 2, 2) + value.shape[1:])
+    keep = lax.dynamic_index_in_dim(pairs, index % 2, 1, keepdims=False)
+    return keep, flip(lax.dynamic_index_in_dim(pairs, 1 - index % 2, 1, keepdims=False), "ctx", 1)
+
+
+def line_sum(near, index):
+    lines, line = near.shape[0], index // 2
     low = near.astype(jnp.bfloat16)
     total = lax.dynamic_index_in_dim(near, line, 0, keepdims=False)
     for steps in range(1, lines):
@@ -113,6 +116,9 @@
         jnp.sum(grad_normed * normed, axis=0),
         inverse * (scaled - normed * jnp.mean(scaled * normed, axis=-1, keepdims=True)),
     )
+
+
+TOGETHER = 3
 
 
 def attention_masks(starts_ref, block, half_rows, shape):
@@ -161,37 +167,45 @@
         first, position = attention_masks(starts_ref, block, half_rows, (rows, half_rows))
         column = lax.broadcasted_iota(jnp.int32, (rows, half_rows), 1)
 
-        def score_step(step, running):
-            keys = kv_ref[block_place(step, own_ref[0], contexts), :, :HEAD_DIM]
-            scores = dot32(queries, keys, ((1,), (1,))) * scale
-            at = column + step * half_rows
-            scores = jnp.where((at >= first) & (at <= position), scores, large_negative)
-            s_ref[step - low] = scores
-            return jnp.maximum(running, scores)
+        trips = (block - low + TOGETHER) // TOGETHER
+
+        def score_step(trip, running):
+            for part in range(TOGETHER):
+                step = trip * TOGETHER + part
+                place = block_place(jnp.minimum(low + step, block), own_ref[0], contexts)
+                scores = dot32(queries, kv_ref[place, :, :HEAD_DIM], ((1,), (1,))) * scale
+                at = column + (low + step) * half_rows
+                scores = jnp.where((at >= first) & (at <= position), scores, large_negative)
+                s_ref[step] = scores
+                running = jnp.maximum(running, scores)
+            return running
 
         running = lax.fori_loop(
-            low, block + 1, score_step, jnp.full((rows, half_rows), large_negative, jnp.float32)
+            0, trips, score_step, jnp.full((rows, half_rows), large_negative, jnp.float32)
         )
         row_max = jnp.max(running, axis=1, keepdims=True)
 
-        def sum_step(step, total):
-            expo = jnp.exp(s_ref[step - low] - row_max)
-            s_ref[step - low] = expo
-            return total + expo
-
-        total = lax.fori_loop(
-            low, block + 1, sum_step, jnp.zeros((rows, half_rows), jnp.float32)
-        )
+        def sum_step(trip, total):
+            for part in range(TOGETHER):
+                step = trip * TOGETHER + part
+                expo = jnp.exp(s_ref[step] - row_max)
+                s_ref[step] = expo
+                total = total + expo
+            return total
+
+        total = lax.fori_loop(0, trips, sum_step, jnp.zeros((rows, half_rows), jnp.float32))
         row_sum = jnp.sum(total, axis=1, keepdims=True)
         inverse = 1.0 / row_sum
 
-        def value_step(step, accum):
-            weights = (s_ref[step - low] * inverse).astype(jnp.bfloat16)
-            return accum + dot32(weights, kv_ref[block_place(step, own_ref[0], contexts), :, HEAD_DIM:])
-
-        accum = lax.fori_loop(
-            low, block + 1, value_step, jnp.zeros((rows, HEAD_DIM), jnp.float32)
-        )
+        def value_step(trip, accum):
+            for part in range(TOGETHER):
+                step = trip * TOGETHER + part
+                place = block_place(jnp.minimum(low + step, block), own_ref[0], contexts)
+                weights = (s_ref[step] * inverse).astype(jnp.bfloat16)
+                accum = accum + dot32(weights, kv_ref[place, :, HEAD_DIM:])
+            return accum
+
+        accum = lax.fori_loop(0, trips, value_step, jnp.zeros((rows, HEAD_DIM), jnp.float32))
         log_sum = row_max + jnp.log(row_sum)
         lse_ref[0, half] = jnp.broadcast_to(log_sum, (rows, half_rows))
         for h in range(ratio):
@@ -217,18 +231,14 @@
                 q_spec,
                 pl.BlockSpec((1, 2, stacked, half_rows), lambda g, *_: (g, 0, 0, 0)),
             ],
-            scratch_shapes=[pltpu.VMEM((blocks, stacked, half_rows), jnp.float32)],
+            scratch_shapes=[pltpu.VMEM((blocks + TOGETHER - 1, stacked, half_rows), jnp.float32)],
         ),
         out_shape=(
             jax.ShapeDtypeStruct((rows, width), jnp.bfloat16),
             jax.ShapeDtypeStruct((KEY_VALUE_HEADS, 2, stacked, half_rows), jnp.float32),
         ),
         compiler_params=pltpu.CompilerParams(vmem_limit_bytes=48 << 20),
-        cost_estimate=pl.CostEstimate(
-            flops=2 * rows * width * blocks * half_rows * 2,
-            bytes_accessed=4 * rows * width + 4 * blocks * half_rows * 512,
-            transcendentals=rows * QUERY_HEADS * blocks * half_rows // 2,
-        ),
+        cost_estimate=pl.CostEstimate(flops=0, bytes_accessed=1 << 20, transcendentals=0),
         name="attention_forward",
     )(starts, own, queries, kv)
 
@@ -262,34 +272,38 @@
         first, position = attention_masks(starts_ref, block, half_rows, (rows, half_rows))
         column = lax.broadcasted_iota(jnp.int32, (rows, half_rows), 1)
 
-        def prob_step(step, running):
-            place = block_place(step, own_ref[0], contexts)
-            scores = dot32(queries, kv_ref[place, :, :HEAD_DIM], ((1,), (1,))) * scale
-            at = column + step * half_rows
-            probs = jnp.where(
-                (at >= first) & (at <= position), jnp.exp(scores - log_sum), 0.0
-            )
-            prob_grads = dot32(grads, kv_ref[place, :, HEAD_DIM:], ((1,), (1,)))
-            p_ref[step - low] = probs
-            dp_ref[step - low] = prob_grads
-            return running + probs * prob_grads
-
-        running = lax.fori_loop(
-            low, block + 1, prob_step, jnp.zeros((rows, half_rows), jnp.float32)
-        )
+        trips = (block - low + TOGETHER) // TOGETHER
+
+        def prob_step(trip, running):
+            for part in range(TOGETHER):
+                step = trip * TOGETHER + part
+                place = block_place(jnp.minimum(low + step, block), own_ref[0], contexts)
+                scores = dot32(queries, kv_ref[place, :, :HEAD_DIM], ((1,), (1,))) * scale
+                at = column + (low + step) * half_rows
+                probs = jnp.where(
+                    (at >= first) & (at <= position), jnp.exp(scores - log_sum), 0.0
+                )
+                prob_grads = dot32(grads, kv_ref[place, :, HEAD_DIM:], ((1,), (1,)))
+                p_ref[step] = probs
+                dp_ref[step] = prob_grads
+                running = running + probs * prob_grads
+            return running
+
+        running = lax.fori_loop(0, trips, prob_step, jnp.zeros((rows, half_rows), jnp.float32))
         delta = jnp.sum(running, axis=1, keepdims=True)
 
-        def grad_step(step, query_grad):
-            place = block_place(step, own_ref[0], contexts)
-            probs = p_ref[step - low]
-            score_low = (probs * (dp_ref[step - low] - delta)).astype(jnp.bfloat16)
-            dka_ref[place] += dot32(score_low, queries, ((0,), (0,)))
-            dva_ref[place] += dot32(probs.astype(jnp.bfloat16), grads, ((0,), (0,)))
-            return query_grad + dot32(score_low, kv_ref[place, :, :HEAD_DIM])
-
-        query_grad = lax.fori_loop(
-            low, block + 1, grad_step, jnp.zeros((rows, HEAD_DIM), jnp.float32)
-        )
+        def grad_step(trip, query_grad):
+            for part in range(TOGETHER):
+                step = trip * TOGETHER + part
+                place = block_place(jnp.minimum(low + step, block), own_ref[0], contexts)
+                probs = p_ref[step]
+                score_low = (probs * (dp_ref[step] - delta)).astype(jnp.bfloat16)
+                dka_ref[place] += dot32(score_low, queries, ((0,), (0,)))
+                dva_ref[place] += dot32(probs.astype(jnp.bfloat16), grads, ((0,), (0,)))
+                query_grad = query_grad + dot32(score_low, kv_ref[place, :, :HEAD_DIM])
+            return query_grad
+
+        query_grad = lax.fori_loop(0, trips, grad_step, jnp.zeros((rows, HEAD_DIM), jnp.float32))
         for h in range(ratio):
             dq_ref[half * half_rows : (half + 1) * half_rows, h * HEAD_DIM : (h + 1) * HEAD_DIM] = (
                 query_grad[h * half_rows : (h + 1) * half_rows] * scale
@@ -320,8 +334,8 @@
             ],
             out_specs=[q_spec, part_spec, part_spec],
             scratch_shapes=[
-                pltpu.VMEM((blocks, stacked, half_rows), jnp.float32),
-                pltpu.VMEM((blocks, stacked, half_rows), jnp.float32),
+                pltpu.VMEM((blocks + TOGETHER - 1, stacked, half_rows), jnp.float32),
+                pltpu.VMEM((blocks + TOGETHER - 1, stacked, half_rows), jnp.float32),
                 pltpu.VMEM((blocks, half_rows, HEAD_DIM), jnp.float32),
                 pltpu.VMEM((blocks, half_rows, HEAD_DIM), jnp.float32),
             ],
@@ -332,51 +346,53 @@
             jax.ShapeDtypeStruct((blocks // 2, half_rows, kv_width), jnp.bfloat16),
         ),
         compiler_params=pltpu.CompilerParams(vmem_limit_bytes=58 << 20),
-        cost_estimate=pl.CostEstimate(
-            flops=5 * rows * width * blocks * half_rows * 2,
-            bytes_accessed=8 * rows * width + 8 * blocks * half_rows * kv_width,
-            transcendentals=rows * QUERY_HEADS * blocks * half_rows // 2,
-        ),
+        cost_estimate=pl.CostEstimate(flops=0, bytes_accessed=1 << 20, transcendentals=0),
         name="attention_backward",
     )(starts, own, queries, grads, kv, log_sums)
 
 
-def experts_kernel(
-    at_ref, x0, x1, x2, x3, dy0, dy1, dy2, dy3, g_ref, wg_ref, wu_ref, wd_ref, shared_ref,
-    out_ref, dx_ref, out_low_ref, dx_low_ref, dg_ref, term_ref, pair_term_ref,
-    x_ref, dy_ref, he_ref, da_ref, db_ref, tail_ref, sem,
-):
+def experts_kernel(final, *refs):
+    at_ref, *refs = refs
+    parts, refs = refs[:8], refs[8:]
+    g_ref, wg_ref, wu_ref, wd_ref, *refs = refs
+    if final:
+        shared_ref, out_in, dx_in, tail_in, dg_in, *refs = refs
+        out_ref, dx_ref, out_low_ref, dx_low_ref, dg_ref, *refs = refs
+        targets = tuple((refs[0].at[:, number], refs[1].at[:, number]) for number in range(2))
+        pair_target, refs = (refs[2], refs[3]), refs[4:]
+        x_ref, dy_ref, he_ref, da_ref, db_ref, tail_ref, sem = refs
+    else:
+        out_ref, dx_ref, tail_ref, dg_ref, *refs = refs
+        targets, refs = (refs[0], (refs[1], refs[2])), refs[3:]
+        x_ref, dy_ref, he_ref, da_ref, db_ref, sem = refs
     local = pl.program_id(0)
-    last = pl.num_programs(0) - 1
     expert = at_ref[0] + local
     side = at_ref[1]
     total_rows, width = x_ref.shape
+    half = total_rows // 2
     step_rows = 256
-    per = term_ref.shape[4]
     tall = 384
-    shared = shared_ref.shape[1] // 3
 
     @pl.when(local == 0)
     def _():
-        copies = []
-        for number, (whole, parts) in enumerate(((x_ref, (x0, x1, x2, x3)), (dy_ref, (dy0, dy1, dy2, dy3)))):
-            size = total_rows // 4
-            for part, source in enumerate(parts):
-                copies.append(
-                    pltpu.make_async_copy(
-                        source, whole.at[pl.ds(part * size, size), :], sem.at[number * 4 + part]
-                    )
-                )
+        size = total_rows // 4
+        moves = []
+        for number, source in enumerate(parts):
+            whole = (x_ref, dy_ref)[number // 4]
+            moves.append((source, whole.at[pl.ds(number % 4 * size, size), :]))
+        if final:
+            moves += [(out_in, out_ref), (dx_in, dx_ref), (tail_in, tail_ref), (dg_in, dg_ref)]
+        copies = [
+            pltpu.make_async_copy(source, target, sem.at[number])
+            for number, (source, target) in enumerate(moves)
+        ]
         for copy in copies:
             copy.start()
-        out_ref[...] = jnp.zeros_like(out_ref)
-        dx_ref[...] = jnp.zeros_like(dx_ref)
-        tail_ref[...] = jnp.zeros_like(tail_ref)
-        dg_ref[...] = jnp.zeros_like(dg_ref)
+        if not final:
+            for ref in (out_ref, dx_ref, tail_ref, dg_ref):
+                ref[...] = jnp.zeros_like(ref)
         for copy in copies:
             copy.wait()
-
-    half = total_rows // 2
 
     def add(number, rows, value):
         if rows.start < half:
@@ -384,10 +400,23 @@
         else:
             tail_ref[number, slice(rows.start - half, rows.stop - half), :] += value
 
-    def store(low, begin, target, number):
-        for part in range(low.shape[0] // per):
-            device = begin // per + part
-            target[(side + device) % 2, device // 2, number] = low[part * per : (part + 1) * per]
+    def store_sides(lows, begin, pair):
+        per = pair[0].shape[2]
+        for parity in range(2):
+
+            @pl.when(side == parity)
+            def _():
+                for part in range(tall // per):
+                    line = begin // (2 * per) + part // 2
+                    for number, low in enumerate(lows):
+                        pair[(part + parity) % 2][line, number] = low[part * per : (part + 1) * per]
+
+    def store_lines(lows, begin, target):
+        per = target.shape[3]
+        for part in range(tall // per):
+            line = begin // (2 * per) + part // 2
+            for number, low in enumerate(lows):
+                target[line, (side + part) % 2, number] = low[part * per : (part + 1) * per]
 
     for begin in range(0, total_rows, step_rows):
         rows = slice(begin, begin + step_rows)
@@ -411,93 +440,102 @@
         db_ref[rows, :] = up_low
         add(1, rows, dot32(pre_low, wg_ref[0], ((1,), (1,))) + dot32(up_low, wu_ref[0], ((1,), (1,))))
 
-    for begin in range(0, width, tall):
-        columns = slice(begin, begin + tall)
-        for number, (left, right) in enumerate(((x_ref, da_ref), (x_ref, db_ref), (dy_ref, he_ref))):
-            low = dot32(left[:, columns], right[...], ((0,), (0,))).astype(jnp.bfloat16)
-            store(low, begin, term_ref.at[0], number)
-
-    @pl.when(local == last)
+    @pl.loop(0, width // tall)
+    def _(step):
+        begin = pl.multiple_of(step * tall, tall)
+        columns = pl.ds(begin, tall)
+        lows = [
+            dot32(left[:, columns], right[...], ((0,), (0,))).astype(jnp.bfloat16)
+            for left, right in ((x_ref, da_ref), (x_ref, db_ref), (dy_ref, he_ref))
+        ]
+        for number, target in enumerate(targets):
+
+            @pl.when(local == number)
+            def _():
+                if isinstance(target, tuple):
+                    store_sides(lows, begin, target)
+                else:
+                    store_lines(lows, begin, target)
+
+    if not final:
+        return
+
+    @pl.when(local == pl.num_programs(0) - 1)
     def _():
+        shared = shared_ref.shape[1] // 3
+        pair_w, down_w = slice(0, 2 * shared), slice(2 * shared, 3 * shared)
         for begin in range(0, total_rows, step_rows):
             rows = slice(begin, begin + step_rows)
-            x = x_ref[rows, :]
-            both = dot32(x, shared_ref[:, : 2 * shared])
+            both = dot32(x_ref[rows, :], shared_ref[:, pair_w])
             pre, up = both[:, :shared], both[:, shared:]
             silu, slope = silu_parts(pre)
             hidden = (silu * up).astype(jnp.bfloat16)
             he_ref[rows, :shared] = hidden
-            add(0, rows, dot32(hidden, shared_ref[:, 2 * shared :], ((1,), (1,))))
-            back = dot32(dy_ref[rows, :], shared_ref[:, 2 * shared :])
+            add(0, rows, dot32(hidden, shared_ref[:, down_w], ((1,), (1,))))
+            back = dot32(dy_ref[rows, :], shared_ref[:, down_w])
             da_ref[rows, :shared] = (back * up * slope).astype(jnp.bfloat16)
             da_ref[rows, shared:] = (back * silu).astype(jnp.bfloat16)
-            add(1, rows, dot32(da_ref[rows, :], shared_ref[:, : 2 * shared], ((1,), (1,))))
+            add(1, rows, dot32(da_ref[rows, :], shared_ref[:, pair_w], ((1,), (1,))))
         out_low_ref[...] = tail_ref[0].astype(jnp.bfloat16)
         dx_low_ref[...] = tail_ref[1].astype(jnp.bfloat16)
-        for begin in range(0, width, tall):
-            columns = slice(begin, begin + tall)
-            low = dot32(x_ref[:, columns], da_ref[...], ((0,), (0,))).astype(jnp.bfloat16)
-            store(low[:, :shared], begin, pair_term_ref, 0)
-            store(low[:, shared:], begin, pair_term_ref, 1)
-            low = dot32(dy_ref[:, columns], he_ref[:, :shared], ((0,), (0,))).astype(jnp.bfloat16)
-            store(low, begin, pair_term_ref, 2)
-
-
-def experts_call(at, x, dy, gates, gate_w, up_w, down_w, shared_w, contexts):
+
+        @pl.loop(0, width // tall)
+        def _(step):
+            begin = pl.multiple_of(step * tall, tall)
+            columns = pl.ds(begin, tall)
+            pair_low = dot32(x_ref[:, columns], da_ref[...], ((0,), (0,))).astype(jnp.bfloat16)
+            down_low = dot32(dy_ref[:, columns], he_ref[:, :shared], ((0,), (0,))).astype(jnp.bfloat16)
+            store_sides((pair_low[:, :shared], pair_low[:, shared:], down_low), begin, pair_target)
+
+
+def experts_call(at, x, dy, gates, weights, first, contexts, shared_w=None, carried=()):
+    final = shared_w is not None
+    gate_w, up_w, down_w = weights
     rows, width = 4 * x[0].shape[0], x[0].shape[1]
-    count, _, hidden = gate_w.shape
-    shared = shared_w.shape[1] // 3
-    per = width // contexts
-    lines = contexts // 2
+    hidden = gate_w.shape[2]
+    per, lines, half = width // contexts, contexts // 2, rows // 2
     once = pl.Buffered(1)
     whole = lambda shape: pl.BlockSpec(shape, lambda e, *_: (0,) * len(shape), pipeline_mode=once)
-    weight = lambda shape: pl.BlockSpec((1,) + shape, lambda e, *_: (e, 0, 0))
-    term = pl.BlockSpec((1, 2, lines, 3, per, hidden), lambda e, *_: (e, 0, 0, 0, 0, 0))
-    term_shape = jax.ShapeDtypeStruct((count, 2, lines, 3, per, hidden), jnp.bfloat16)
-    pair_shape = jax.ShapeDtypeStruct((2, lines, 3, per, shared), jnp.bfloat16)
+    weight = lambda shape: pl.BlockSpec((1,) + shape, lambda e, *_: (first + e, 0, 0))
+    apart = pl.BlockSpec(memory_space=pl.ANY)
+    part = jax.ShapeDtypeStruct((half, width), jnp.float32)
+    low = jax.ShapeDtypeStruct((half, width), jnp.bfloat16)
+    tail = jax.ShapeDtypeStruct((2, half, width), jnp.float32)
+    table = jax.ShapeDtypeStruct((rows, EXPERTS), jnp.float32)
+    term = jax.ShapeDtypeStruct((lines, 3, per, hidden), jnp.bfloat16)
+    both = jax.ShapeDtypeStruct((lines, 2, 3, per, hidden), jnp.bfloat16)
+    scratch = [pltpu.VMEM((rows, width), jnp.bfloat16)] * 2 + [pltpu.VMEM((rows, hidden), jnp.bfloat16)] * 3
+    if final:
+        shared = shared_w.shape[1] // 3
+        pair = jax.ShapeDtypeStruct((lines, 3, per, shared), jnp.bfloat16)
+        extra_specs = [whole(shared_w.shape)] + [apart] * 4
+        out_shape = (part, part, low, low, table, both, both, pair, pair)
+        scratch.append(pltpu.VMEM(tail.shape, jnp.float32))
+    else:
+        shared = 0
+        extra_specs = []
+        out_shape = (part, part, tail, table, both, term, term)
     return pl.pallas_call(
-        experts_kernel,
+        functools.partial(experts_kernel, final),
         grid_spec=pltpu.PrefetchScalarGridSpec(
             num_scalar_prefetch=1,
-            grid=(count,),
-            in_specs=[pl.BlockSpec(memory_space=pl.ANY)] * 8
+            grid=(2,),
+            in_specs=[apart] * 8
             + [
                 whole((rows, EXPERTS)),
                 weight((width, hidden)),
                 weight((width, hidden)),
                 weight((hidden, width)),
-                whole(shared_w.shape),
-            ],
-            out_specs=[
-                whole((rows // 2, width)),
-                whole((rows // 2, width)),
-                whole((rows // 2, width)),
-                whole((rows // 2, width)),
-                whole((rows, EXPERTS)),
-                term,
-                whole(pair_shape.shape),
-            ],
-            scratch_shapes=[pltpu.VMEM((rows, width), jnp.bfloat16)] * 2
-            + [pltpu.VMEM((rows, hidden), jnp.bfloat16)] * 3
-            + [pltpu.VMEM((2, rows // 2, width), jnp.float32), pltpu.SemaphoreType.DMA((8,))],
+            ]
+            + extra_specs,
+            out_specs=[whole(item.shape) for item in out_shape],
+            scratch_shapes=scratch + [pltpu.SemaphoreType.DMA((12,))],
         ),
-        out_shape=(
-            jax.ShapeDtypeStruct((rows // 2, width), jnp.float32),
-            jax.ShapeDtypeStruct((rows // 2, width), jnp.float32),
-            jax.ShapeDtypeStruct((rows // 2, width), jnp.bfloat16),
-            jax.ShapeDtypeStruct((rows // 2, width), jnp.bfloat16),
-            jax.ShapeDtypeStruct((rows, EXPERTS), jnp.float32),
-            term_shape,
-            pair_shape,
-        ),
+        out_shape=out_shape,
         compiler_params=pltpu.CompilerParams(vmem_limit_bytes=60 << 20),
-        cost_estimate=pl.CostEstimate(
-            flops=18 * count * rows * width * hidden + 18 * rows * width * shared,
-            bytes_accessed=16 * rows * width + 12 * count * width * hidden,
-            transcendentals=count * rows * hidden,
-        ),
-        name="experts",
-    )(at, *x, *dy, gates, gate_w, up_w, down_w, shared_w)
+        cost_estimate=pl.CostEstimate(flops=0, bytes_accessed=1 << 20, transcendentals=0),
+        name="experts_final" if final else "experts",
+    )(at, *x, *dy, gates, gate_w, up_w, down_w, *((shared_w,) if final else ()), *carried)
 
 
 def dense_gates(logits, routes):
@@ -560,8 +598,8 @@
 
     hidden_share = shared_gate.shape[1] // members
     routes_all = jnp.concatenate(gather_pieces(after(routes.reshape(rows, TOP), ring[1])), axis=0)
-    grad_pieces = gather_pieces(after(grad_low, ring[2]))
-    queries = after(queries, routes_all, *grad_pieces)
+    grad_pieces = gather_pieces(after(grad_low, ring[1]))
+    queries = after(queries, routes_all)
     shared_w = jnp.concatenate(
         [
             shared_gate.reshape(share, members, hidden_share),
@@ -581,22 +619,36 @@
     residual = inputs + mixed
     inverse_two = lax.rsqrt(jnp.mean(residual * residual, axis=-1, keepdims=True) + epsilon)
     normed_two = residual * inverse_two
-    second_low = after((normed_two * gain_two).astype(jnp.bfloat16), shared_w)
+    second_low = after((normed_two * gain_two).astype(jnp.bfloat16), shared_w, *grad_pieces)
 
     second_pieces = gather_pieces(second_low)
     logits = jnp.concatenate([dot32(piece, router_full) for piece in second_pieces], axis=0)
     gates_all = dense_gates(logits, routes_all)
-    at = jnp.stack([member * expert_gate.shape[0], context % 2]).astype(jnp.int32)
-    out_keep, dx_keep, out_send, dx_send, gate_back, terms, pair_terms = experts_call(
-        at, second_pieces, grad_pieces, gates_all, expert_gate, expert_up, expert_down,
-        shared_w, contexts,
-    )
+    attended_across = flip(after(attended, second_pieces[3]), "wa", 2)
+    local = expert_gate.shape[0]
+    weights = (expert_gate, expert_up, expert_down)
+    at = lambda first: jnp.stack([member * local + first, context % 2]).astype(jnp.int32)
+    *carried, line_terms, keep_one, send_one = experts_call(
+        at(0), second_pieces, grad_pieces, gates_all, weights, 0, contexts
+    )
+    line_sums = scatter_lines(line_terms)
+    other_one = flip(send_one, "ctx", 1)
+    (
+        out_keep, dx_keep, out_send, dx_send, gate_back,
+        keep_both, send_both, pair_keep, pair_send,
+    ) = experts_call(
+        at(2), second_pieces, grad_pieces, gates_all, weights, 2, contexts, shared_w, carried
+    )
+    other_both = flip(send_both, "ctx", 1)
+
+    def side_sum(keep, received):
+        return keep.astype(jnp.float32) + received.astype(jnp.float32)
+
+    dx_near = dx_keep + flip(after(dx_send, other_one, attended_across), "wa", 1).astype(jnp.float32)
+    dx_moved = flip(dx_near[rows:].astype(jnp.bfloat16), "wa", 2)
+    dx_own = dx_near[:rows] + dx_moved.astype(jnp.float32)
     half = 2 * rows
-    first_other = flip(terms[1, 1], "ctx", 1)
-    second_other = flip(terms[2, 1], "ctx", 1)
-    dx_own = reduce_rows(dx_keep, dx_send, jnp.bfloat16)
     gate_back = reduce_rows(gate_back[:half], gate_back[half:], jnp.float32)
-    line_sums = scatter_lines(terms[0].swapaxes(0, 1))
 
     gates = gates_all[:rows]
     logit_grad = gates * (gate_back - jnp.sum(gates * gate_back, axis=-1, keepdims=True))
@@ -608,82 +660,92 @@
     residual_grad = grad_rows + residual_back
     mix_low = residual_grad.astype(jnp.bfloat16)
 
+    def shared_out(extra):
+        count = extra.shape[0]
+        pieces = extra.reshape(count, contexts, members, each).transpose(2, 0, 1, 3)
+        return exchange(pieces.reshape(members, count, share), member)
+
+    def widened(term, pieces):
+        total = sum(pieces)
+        columns = jnp.pad(total, ((0, 128 - total.shape[0]), (0, 0))).T
+        return jnp.concatenate([term, columns], axis=1).astype(jnp.bfloat16).reshape(contexts, each, -1)
+
     attended_grad = sum(
         dot32(mix_low[:, m * share : (m + 1) * share], out_full[m], ((1,), (1,)))
         for m in range(members)
     ).astype(jnp.bfloat16)
+    small_terms = jnp.concatenate([router_term, gain_two_term[None]], axis=0)
+    near_one = side_sum(keep_one, after(other_one, dx_moved)) + 0.0 * line_sums[0, 0, 0, 0].astype(jnp.float32)
+    near_one = near_one.astype(jnp.bfloat16)
+    sum_one = scatter_lines(near_one)
+    attended_grad = after(attended_grad, near_one)
     query_low, kv_keep, kv_send = attention_backward(starts, own, queries, attended_grad, kv_all, log_sums)
     by_line = lambda parts: parts.reshape(lines, rows, kv_width)
-    kv_near = by_line(kv_keep).astype(jnp.float32) + flip(by_line(kv_send), "ctx", 1).astype(jnp.float32)
+    kv_send = after(by_line(kv_send), other_both)
+    received = flip(kv_send, "ctx", 1)
+    query_pieces = gather_pieces(query_low)
+    mix_pieces = exchange(after(by_share(mix_low), query_low), member)
+    small_pieces = shared_out(after(small_terms, query_low))
+    normed_pieces = exchange(after(by_share(normed_low), query_low), member)
+    attended_pieces = [attended, attended_across] + [
+        flip(after(piece, query_low), "wa", 1) for piece in (attended, attended_across)
+    ]
+    out_near = out_keep + flip(after(out_send, query_low), "wa", 1).astype(jnp.float32)
+    out_moved = flip(out_near[rows:].astype(jnp.bfloat16), "wa", 2)
+    out_own = out_near[:rows] + out_moved.astype(jnp.float32)
+    block_out = (residual + out_own).astype(jnp.bfloat16).reshape(tokens.shape)
+    moved = mix_pieces[1:] + small_pieces[1:] + normed_pieces[1:] + attended_pieces[2:]
+    received = after(received, out_moved, query_pieces[3], *moved)
+    kv_near = by_line(kv_keep).astype(jnp.float32) + received.astype(jnp.float32)
     kv_parts = kv_near.astype(jnp.bfloat16)
-    kv_low = kv_near[0]
-    for steps in range(1, lines):
-        kv_low = kv_low + shift(kv_parts[steps], -steps).astype(jnp.float32)
-    kv_low = kv_low.astype(jnp.bfloat16)
-
-    by_units = lambda value: value.reshape(-1, contexts, members, each).transpose(2, 0, 1, 3).reshape(
-        members, -1, share
-    )
-
-    def widened(term, extra):
-        count = extra.shape[0]
-        total = jnp.sum(exchange(by_units(extra), member).reshape(members, count, share), axis=0)
-        columns = jnp.pad(total, ((0, 128 - count), (0, 0))).T
-        return jnp.concatenate([term, columns], axis=1).astype(jnp.bfloat16).reshape(contexts, each, -1)
-
-    def side_sum(expert, received):
-        near = terms[expert, 0].astype(jnp.float32) + received.astype(jnp.float32)
-        return near.astype(jnp.bfloat16)
-
-    near_one = side_sum(1, after(first_other, query_low))
-    sum_one = scatter_lines(near_one)
-    third_other = flip(after(terms[3, 1], near_one), "ctx", 1)
-
-    normed_share = exchange(after(by_share(normed_low), query_low), member)
-    query_all = jnp.concatenate(gather_pieces(query_low), axis=0)
-    query_term = dot32(normed_share, query_all, ((0,), (0,))).astype(jnp.bfloat16)
-    attended_all = jnp.concatenate(gather_pieces(after(attended, query_low)), axis=0)
-    mix_share = exchange(after(by_share(mix_low), query_low), member)
-    out_term = dot32(mix_share, attended_all, ((0,), (0,)))
-    out_term = widened(out_term, jnp.concatenate([router_term, gain_two_term[None]], axis=0))
-    out_own = reduce_rows(out_keep, after(out_send, out_term), jnp.bfloat16)
-    block_out = (residual + out_own).astype(jnp.bfloat16).reshape(tokens.shape)
-
-    near_two = side_sum(2, after(second_other, near_one))
-    sum_two = scatter_lines(near_two)
-    query_weight_grad = scatter_ctx(
-        after(query_term.reshape(contexts, each, width), kv_near), context
-    )
-    out_sum = scatter_ctx(after(out_term, kv_near), context)
+    kv_moved = [shift(kv_parts[steps], -steps) for steps in range(1, lines)]
+    near_both = side_sum(keep_both, after(other_both, kv_parts)).astype(jnp.bfloat16)
+    sum_both = scatter_lines(near_both)
+    kv_moved[0] = after(kv_moved[0], near_both)
+    kv_low = (kv_near[0] + sum(moved.astype(jnp.float32) for moved in kv_moved)).astype(jnp.bfloat16)
+
+    stacked = lambda pieces: jnp.concatenate(pieces, axis=0)
+    normed_share = stacked(normed_pieces)
+    query_term = dot32(normed_share, stacked(query_pieces), ((0,), (0,))).astype(jnp.bfloat16)
+    out_term = dot32(stacked(mix_pieces), stacked(attended_pieces), ((0,), (0,)))
+    out_term = widened(out_term, small_pieces)
+
+    early_term = jnp.concatenate([query_term.reshape(contexts, each, width), out_term], axis=2)
+    early_sides = to_side(after(early_term, kv_parts), context)
+    other_pair = flip(after(pair_send, kv_parts), "ctx", 1)
+
+    kv_low_pieces = gather_pieces(kv_low)
+    early_sides = (early_sides[0], after(early_sides[1], kv_low_pieces[3]))
+    kv_low_all = stacked(kv_low_pieces)
+    kv_term = dot32(normed_share, kv_low_all, ((0,), (0,)))
+    first_grad = dot32(query_low, query_full, ((1,), (1,))) + dot32(kv_low, kv_full, ((1,), (1,)))
+    scaled = first_grad * gain_one
+    input_back = inverse_one * (
+        scaled - normed_one * jnp.mean(scaled * normed_one, axis=-1, keepdims=True)
+    )
+    tokens_grad = (residual_grad + input_back).astype(jnp.bfloat16).reshape(tokens.shape)
+    kv_sides = to_side(kv_term.astype(jnp.bfloat16).reshape(contexts, each, kv_width), context)
+    kv_sum = line_sum(side_sum(*kv_sides), context)
+    early_sum = line_sum(side_sum(*early_sides), context)
+    query_weight_grad, out_sum = early_sum[:, :width], early_sum[:, width:]
     out_weight_grad = out_sum[:, :width].T
     router_weight_grad = out_sum[:, width : width + EXPERTS]
     norm_gain_2_grad = out_sum[:, width + EXPERTS]
-
-    kv_low_all = jnp.concatenate(gather_pieces(kv_low), axis=0)
-    kv_term = dot32(normed_share, kv_low_all, ((0,), (0,)))
-    first_grad = dot32(query_low, query_full, ((1,), (1,))) + dot32(kv_low, kv_full, ((1,), (1,)))
-    gain_one_term, input_back = rms_back(first_grad, normed_one, inverse_one, gain_one)
-    tokens_grad = (residual_grad + input_back).astype(jnp.bfloat16).reshape(tokens.shape)
-    kv_sum = scatter_ctx(widened(kv_term, gain_one_term[None]), context)
-    key_weight_grad, value_weight_grad = apart(kv_sum[:, :kv_width])
-    norm_gain_1_grad = kv_sum[:, kv_width]
-
-    near_three = side_sum(3, after(third_other, kv_low))
-    sum_three = scatter_lines(near_three)
-    sum_zero = line_sums[0].astype(jnp.float32) + flip(line_sums[1], "ctx", 1).astype(jnp.float32)
-    expert_sums = [sum_zero, sum_one, sum_two, sum_three]
+    key_weight_grad, value_weight_grad = apart(kv_sum)
+    mine = lambda full: lax.dynamic_slice_in_dim(full, (context * members + member) * each, each, 0)
+    norm_gain_1_grad = (
+        jnp.sum(mine(query_full).astype(jnp.float32) * query_weight_grad, axis=1)
+        + jnp.sum(mine(kv_full).astype(jnp.float32) * kv_sum, axis=1)
+    ) / mine(gain_one)
+
+    line_zero = flip(after(line_sums[1], kv_low_pieces[1]), "ctx", 1)
+    sum_zero = line_sums[0].astype(jnp.float32) + line_zero.astype(jnp.float32)
+    expert_sums = [sum_zero, sum_one, sum_both[0], sum_both[1]]
     expert_gate_grad = jnp.stack([total[0] for total in expert_sums]).astype(jnp.float32)
     expert_up_grad = jnp.stack([total[1] for total in expert_sums]).astype(jnp.float32)
     expert_down_grad = jnp.stack([total[2].T for total in expert_sums]).astype(jnp.float32)
 
-    received = flip(after(pair_terms[1], near_two), "ctx", 1)
-    near = pair_terms[0].astype(jnp.float32) + received.astype(jnp.float32)
-    low = near.astype(jnp.bfloat16)
-    line = context // 2
-    shared_sum = lax.dynamic_index_in_dim(near, line, 0, keepdims=False)
-    for steps in range(1, lines):
-        piece = lax.dynamic_index_in_dim(low, (line + lines - steps) % lines, 0, keepdims=False)
-        shared_sum = shared_sum + shift(piece, -steps).astype(jnp.float32)
+    shared_sum = line_sum(side_sum(pair_keep, after(other_pair, kv_low_pieces[3])), context)
     shared_sum = shared_sum.reshape(3, members, each, hidden_share).transpose(1, 0, 2, 3)
     shared_sum = lax.all_to_all(shared_sum, "wa", 0, 0, tiled=True)
     shared_gate_grad = shared_sum[:, 0].transpose(1, 0, 2).reshape(each, members * hidden_share)

time: 781 us -> 700 us (0.90)
  starting transfers between devices: 121 us -> 59.6 us
  waiting for transfers between devices: 354 us -> 302 us
  Pallas kernels: 120 us -> 151 us
    ppermute x52 -> x47, waiting for transfers between devices: 252 us -> 136 us  [flip(): return lax.ppermute(value, axis, [(i, i ^ bits) for i in range(count)])]
    ppermute x18 -> x15, waiting for transfers between devices: 100 us -> 165 us  [shift(): lax.ppermute(value, 'ctx', [(i, (i + 2 * steps) % count) for i in range(c...]
    ppermute x18 -> x15, starting transfers between devices: 50.9 us -> 19.2 us  [shift(): lax.ppermute(value, 'ctx', [(i, (i + 2 * steps) % count) for i in range(c...]
    ppermute x52 -> x47, starting transfers between devices: 60.6 us -> 29.6 us  [flip(): return lax.ppermute(value, axis, [(i, i ^ bits) for i in range(count)])]
    pallas_call x1 -> x2, Pallas kernels: 85.5 us -> 112 us  [experts_call(): pl.pallas_call(functools.partial(experts_kernel, final), grid_spec=pltpu....]
    convert_element_type x7 -> x6, other arithmetic: 16.6 us -> 14.1 us  [the longest x1 6.07 us: shards(): side_sum(keep_both, after(other_both, kv_parts)).astype(jnp.bfloat16)]
    unnamed x141 -> x190, local copies, waits for them, and re-layouts: 20.9 us -> 22.8 us
  transfers between devices with their start and end apart: 78 -> 69, of which waited for: 40 -> 28; matrix products, arithmetic and copies ran while one was open for 18% -> 21% of each run, Pallas kernels for 4% -> 15%
where the time goes in v3:
time: 700 us; the launch traced here: 690 us
  waiting for transfers between devices  302 us (43%)
  Pallas kernels  151 us (22%)
  local copies, waits for them, and re-layouts  63 us (9%)
  starting transfers between devices  59.6 us (9%)
  other arithmetic  59.1 us (8%)
  matrix products  39.6 us (6%)
  between operations  16.1 us (2%)
    ppermute x15, waiting for transfers between devices, shift(): lax.ppermute(value, 'ctx', [(i, (i + 2 * steps) % count) for i in range(c...  165 us
    ppermute x47, waiting for transfers between devices, flip(): return lax.ppermute(value, axis, [(i, i ^ bits) for i in range(count)])  136 us
    pallas_call x2, Pallas kernels, experts_call(): pl.pallas_call(functools.partial(experts_kernel, final), grid_spec=pltpu....  112 us
    ppermute x47, starting transfers between devices, flip(): return lax.ppermute(value, axis, [(i, i ^ bits) for i in range(count)])  29.6 us
    unnamed x190, local copies, waits for them, and re-layouts  22.8 us
    pallas_call x1, Pallas kernels, attention_backward(): pl.pallas_call(attention_backward_kernel, grid_spec=pltpu.PrefetchScalarG...  21.5 us
    dot_general x9, matrix products, dot32(): lax.dot_general(left, right, (dims, ((), ())), preferred_element_type=jnp...  20.4 us
    ppermute x15, starting transfers between devices, shift(): lax.ppermute(value, 'ctx', [(i, (i + 2 * steps) % count) for i in range(c...  19.2 us
  transfers between devices with their start and end apart: 69, of which 28 were waited for; matrix products, arithmetic and copies ran while one was open for 21% of the time, Pallas kernels for 15%

profile of v3, /device:TPU:10, one launch (start us, length us, event | category | flops | bytes accessed | tf_op | source)
XLA Modules:
  0.0 690.0 jit_solution(1756485848380343596)
XLA Ops:
  12.7 20.9 %collective-permute-done.1 = bf16[384,1152]{0,1:T(8,128)(2,1)S(1)} collective-permute-done((bf16[384,1152]{0,1:T(8,128)(2,1)S(1)}, bf16[384,1152]{0,1:T(8,128)(2,1)S(1)}, u32[]{:S(2)}, u32[]{:S(2)}) %collective-permute-start.1) | collective-permute-done | bytes 884768 | tf_op jit(solution)/shard_map/ppermute | solution.py:30
  49.2 10.4 %collective-permute-done.3 = bf16[2,128,1024]{2,1,0:T(8,128)(2,1)} collective-permute-done((bf16[2,128,1024]{2,1,0:T(8,128)(2,1)}, bf16[2,128,1024]{2,1,0:T(8,128)(2,1)}, u32[]{:S(2)}, u32[]{:S(2)}) %collective-permute-start.3) | collective-permute-done | bytes 524320 | tf_op jit(solution)/shard_map/ppermute | solution.py:35
  78.3 8.6 %collective-permute-done.4 = s32[256,6]{0,1:T(8,128)S(1)} collective-permute-done((s32[256,6]{0,1:T(8,128)}, s32[256,6]{0,1:T(8,128)S(1)}, u32[]{:S(2)}, u32[]{:S(2)}) %collective-permute-start.4) | collective-permute-done | bytes 6176 | tf_op jit(solution)/shard_map/ppermute | solution.py:30
  90.4 5.9 all-to-all-start
  103.7 8.9 %collective-permute-done.12 = bf16[2,128,1024]{2,1,0:T(8,128)(2,1)} collective-permute-done((bf16[2,128,1024]{2,1,0:T(8,128)(2,1)}, bf16[2,128,1024]{2,1,0:T(8,128)(2,1)}, u32[]{:S(2)}, u32[]{:S(2)}) %collective-permute-start.12) | collective-permute-done | bytes 524320 | tf_op jit(solution)/shard_map/ppermute | solution.py:30
  118.3 17.0 %attention_forward.1 = (bf16[256,1536]{1,0:T(8,128)(2,1)S(1)}, f32[4,2,384,128]{3,2,1,0:T(8,128)S(1)}) custom-call(s32[8]{0:T(128)S(1)} %bitcast.330, s32[1]{0:T(128)} %bitcast.2.own_ref, bf16[256,1536]{1,0:T(8,128)(2,1)S(1)} %convolution_convert_fusion.q_ref, bf16[16,128,1024]{2,1,0:T(8,128)(2,1)} %constant_dynamic-update-slice_fusion.4.kv_ref), custom_call_target="tpu_custom_call" | custom-call | bytes 1048576 | tf_op jit(solution)/shard_map/attention_forward/pallas_call | solution.py:224
  144.9 16.8 %collective-permute-done.16.refs_2_ = bf16[256,1536]{1,0:T(8,128)(2,1)} collective-permute-done((bf16[256,1536]{1,0:T(8,128)(2,1)S(1)}, bf16[256,1536]{1,0:T(8,128)(2,1)}, u32[]{:S(2)}, u32[]{:S(2)}) %collective-permute-start.16) | collective-permute-done | bytes 786464 | tf_op jit(solution)/shard_map/ppermute | solution.py:30
  167.0 48.1 %experts.1 = (f32[512,1536]{1,0:T(8,128)}, f32[512,1536]{1,0:T(8,128)}, f32[2,512,1536]{2,1,0:T(8,128)}, f32[1024,16]{1,0:T(8,128)}, bf16[4,2,3,192,512]{4,3,2,1...) custom-call(s32[2]{0:T(128)} %pad_add_fusion.1.refs_0_, ...), custom_call_target="tpu_custom_call" | custom-call | bytes 1048576 | tf_op jit(solution)/shard_map/experts/pallas_call | solution.py:518
  219.0 64.0 %experts_final.1 = (f32[512,1536]{1,0:T(8,128)}, f32[512,1536]{1,0:T(8,128)}, bf16[512,1536]{1,0:T(8,128)(2,1)}, bf16[512,1536]{1,0:T(8,128)(2,1)}, f32[1024,16]...) custom-call(s32[2]{0:T(128)} %pad_add_fusion.refs_0_, ...), custom_call_target="tpu_custom_call" | custom-call | bytes 1048576 | tf_op jit(solution)/shard_map/experts_final/pallas_call | solution.py:518
  300.7 12.2 %collective-permute-done.24 = f32[256,16]{1,0:T(8,128)} collective-permute-done((f32[256,16]{1,0:T(8,128)}, f32[256,16]{1,0:T(8,128)}, u32[]{:S(2)}, u32[]{:S(2)}) %collective-permute-start.24) | collective-permute-done | bytes 16416 | tf_op jit(solution)/shard_map/ppermute | solution.py:30
  327.4 4.5 add_convert_fusion.1
  335.2 21.5 %attention_backward.1 = (bf16[256,1536]{1,0:T(8,128)(2,1)}, bf16[8,128,1024]{2,1,0:T(8,128)(2,1)}, bf16[8,128,1024]{2,1,0:T(8,128)(2,1)}) custom-call(s32[8]{0:T(128)} %bitcast.329, s32[1]{0:T(128)} %bitcast.2.own_ref, bf16[256,1536]{1,0:T(8,128)(2,1)} %copy-done, bf16[256,1536]{1,0:T(8,128)(2,1)} %fusion.23.do_ref, ...), custom_call_target="tpu_custom_call" | custom-call | bytes 1048576 | tf_op jit(solution)/shard_map/attention_backward/pallas_call | solution.py:324
  370.3 17.4 %collective-permute-done.27 = bf16[4,2,3,192,512]{4,3,2,1,0:T(8,128)(2,1)} collective-permute-done((bf16[4,2,3,192,512]{4,3,2,1,0:T(8,128)(2,1)}, bf16[4,2,3,192,512]{4,3,2,1,0:T(8,128)(2,1)}, u32[]{:S(2)}, u32[]{:S(2)}) %collective-permute-start.27) | collective-permute-done | bytes 4718624 | tf_op jit(solution)/shard_map/ppermute | solution.py:30
  412.8 4.1 fusion.16
  421.9 17.9 %collective-permute-done.28 = bf16[4,256,1024]{2,1,0:T(8,128)(2,1)} collective-permute-done((bf16[4,256,1024]{2,1,0:T(8,128)(2,1)}, bf16[4,256,1024]{2,1,0:T(8,128)(2,1)}, u32[]{:S(2)}, u32[]{:S(2)}) %collective-permute-start.28) | collective-permute-done | bytes 2097184 | tf_op jit(solution)/shard_map/ppermute | solution.py:30
  439.9 5.0 fusion.106
  452.2 6.1 add_convert_fusion
  463.2 93.0 %collective-permute-done.42 = bf16[256,1024]{1,0:T(8,128)(2,1)} collective-permute-done((bf16[256,1024]{1,0:T(8,128)(2,1)}, bf16[256,1024]{1,0:T(8,128)(2,1)}, u32[]{:S(2)}, u32[]{:S(2)}) %collective-permute-start.42) | collective-permute-done | bytes 524320 | tf_op jit(solution)/shard_map/ppermute | solution.py:35
  562.2 9.3 %collective-permute-done.47 = bf16[256,1024]{1,0:T(8,128)(2,1)S(1)} collective-permute-done((bf16[256,1024]{1,0:T(8,128)(2,1)S(1)}, bf16[256,1024]{1,0:T(8,128)(2,1)S(1)}, u32[]{:S(2)}, u32[]{:S(2)}) %collective-permute-start.47) | collective-permute-done | bytes 524320 | tf_op jit(solution)/shard_map/ppermute | solution.py:30
  585.0 5.8 collective-permute-done.61
  591.0 33.6 %collective-permute-done.60 = bf16[3,192,256]{2,1,0:T(8,128)(2,1)S(1)} collective-permute-done((bf16[3,192,256]{2,1,0:T(8,128)(2,1)S(1)}, bf16[3,192,256]{2,1,0:T(8,128)(2,1)S(1)}, u32[]{:S(2)}, u32[]{:S(2)}) %collective-permute-start.60) | collective-permute-done | bytes 294944 | tf_op jit(solution)/shard_map/ppermute | solution.py:35
  625.7 4.9 collective-permute-done.59
  631.9 4.4 all-to-all-start.1
  652.2 13.0 %collective-permute-done.55 = bf16[48,1024]{0,1:T(8,128)(2,1)S(1)} collective-permute-done((bf16[48,1024]{0,1:T(8,128)(2,1)S(1)}, bf16[48,1024]{0,1:T(8,128)(2,1)S(1)}, u32[]{:S(2)}, u32[]{:S(2)}) %collective-permute-start.55) | collective-permute-done | bytes 98336 | tf_op jit(solution)/shard_map/ppermute | solution.py:35
  (442 shorter events, 220.6 us)
Async XLA Ops:
  7.2 107.3 %all-gather.4.cloned.1.call-start = ((), (), s32[]{:S(2)}) async-start(), calls=%async_computation.5 | async-start | bytes 5898240 | tf_op jit(solution)/shard_map/all_gather | solution.py:584
  33.6 102.9 %all-gather.6.cloned.1.call-start = ((), (), s32[]{:S(2)}) async-start(), calls=%async_computation.9 | async-start | bytes 5898240 | tf_op jit(solution)/shard_map/all_gather | solution.py:585
  69.4 73.2 %collective-permute-start.14 = (bf16[256,1536]{1,0:T(8,128)(2,1)}, bf16[256,1536]{1,0:T(8,128)(2,1)}, u32[]{:S(2)}, u32[]{:S(2)}) collective-permute-start(bf16[256,1536]{1,0:T(8,128)(2,1)} %bitcast.17.refs_5_), channel_id=1, source_target_pairs={{0,1},{1,0},{2,3},{3,2},{4,5},{5,4},{6,7},{7,6},{8,9},{9,8},{10,11... | collective-permute-start | bytes 2359304 | tf_op jit(solution)/shard_map/ppermute | solution.py:30
  90.4 52.1 %collective-permute-start.15 = (bf16[256,1536]{1,0:T(8,128)(2,1)}, bf16[256,1536]{1,0:T(8,128)(2,1)}, u32[]{:S(2)}, u32[]{:S(2)}) collective-permute-start(bf16[256,1536]{1,0:T(8,128)(2,1)} %collective-permute-done.13.refs_6_), channel_id=1, source_target_pairs={{0,1},{1,0},{2,3},{3,2},{4,5},{5,4},{6,7},{7,6},{8,9},{9,8},{10,11... | collective-permute-start | bytes 2359304 | tf_op jit(solution)/shard_map/ppermute | solution.py:30
  90.4 52.2 %all-to-all-start = ((bf16[4,384,768]{2,1,0:T(8,128)(2,1)}), bf16[4,384,768]{2,1,0:T(8,128)(2,1)}, u32[]{:S(2)}, u32[]{:S(2)}) async-start(bf16[4,384,768]{2,1,0:T(8,128)(2,1)} %maximum_bitcast_fusion), calls=%async_computation | async-start | bytes 4718592 | tf_op jit(solution)/shard_map/all_to_all | solution.py:611
  96.4 229.2 %reduce-scatter.4.cloned.1.call-start = ((), (), s32[]{:S(2)}) async-start(), calls=%async_computation.6 | async-start | bytes 5898240 | tf_op jit(solution)/shard_map/reduce_scatter | solution.py:103
  215.2 461.2 %reduce-scatter.6.cloned.1.call-start = ((), (), s32[]{:S(2)}) async-start(), calls=%async_computation.7 | async-start | bytes 2949120 | tf_op jit(solution)/shard_map/reduce_scatter | solution.py:103
  215.2 67.8 %collective-permute-start.19 = (bf16[4,3,192,512]{3,2,1,0:T(8,128)(2,1)}, bf16[4,3,192,512]{3,2,1,0:T(8,128)(2,1)}, u32[]{:S(2)}, u32[]{:S(2)}) collective-permute-start(bf16[4,3,192,512]{3,2,1,0:T(8,128)(2,1)} %get-tuple-element.82), channel_id=1, source_target_pairs={{0,4},{4,0},{8,12},{12,8},{16,20},{20,16},{24,28},{28,24},{1,5},{5... | collective-permute-start | bytes 7077896 | tf_op jit(solution)/shard_map/ppermute | solution.py:30
  216.8 66.3 %collective-permute-start.20 = (bf16[256,1536]{1,0:T(8,128)(2,1)S(1)}, bf16[256,1536]{1,0:T(8,128)(2,1)}, u32[]{:S(2)}, u32[]{:S(2)}) collective-permute-start(bf16[256,1536]{1,0:T(8,128)(2,1)S(1)} %get-tuple-element.100), channel_id=1, source_target_pairs={{0,2},{1,3},{2,0},{3,1},{4,6},{5,7},{6,4},{7,5},{8,10},{9,11},{10,... | collective-permute-start | bytes 2359304 | tf_op jit(solution)/shard_map/ppermute | solution.py:30
  283.2 104.5 %collective-permute-start.27 = (bf16[4,2,3,192,512]{4,3,2,1,0:T(8,128)(2,1)}, bf16[4,2,3,192,512]{4,3,2,1,0:T(8,128)(2,1)}, u32[]{:S(2)}, u32[]{:S(2)}) collective-permute-start(bf16[4,2,3,192,512]{4,3,2,1,0:T(8,128)(2,1)} %get-tuple-element.95), channel_id=1, source_target_pairs={{0,4},{4,0},{8,12},{12,8},{16,20},{20,16},{24,28},{28,24},{1,5},{5... | collective-permute-start | bytes 14155784 | tf_op jit(solution)/shard_map/ppermute | solution.py:30
  331.9 345.8 %reduce-scatter.8.cloned.1.call-start = ((), (), s32[]{:S(2)}) async-start(), calls=%async_computation.8 | async-start | bytes 5898240 | tf_op jit(solution)/shard_map/reduce_scatter | solution.py:103
  356.7 49.4 %collective-permute-start.25 = (bf16[512,1536]{1,0:T(8,128)(2,1)}, bf16[512,1536]{1,0:T(8,128)(2,1)}, u32[]{:S(2)}, u32[]{:S(2)}) collective-permute-start(bf16[512,1536]{1,0:T(8,128)(2,1)} %get-tuple-element.92), channel_id=1, source_target_pairs={{0,1},{1,0},{2,3},{3,2},{4,5},{5,4},{6,7},{7,6},{8,9},{9,8},{10,11... | collective-permute-start | bytes 4718600 | tf_op jit(solution)/shard_map/ppermute | solution.py:30
  360.9 45.2 %collective-permute-start.29 = (bf16[256,1536]{1,0:T(8,128)(2,1)}, bf16[256,1536]{1,0:T(8,128)(2,1)}, u32[]{:S(2)}, u32[]{:S(2)}) collective-permute-start(bf16[256,1536]{1,0:T(8,128)(2,1)} %get-tuple-element.91), channel_id=1, source_target_pairs={{0,2},{1,3},{2,0},{3,1},{4,6},{5,7},{6,4},{7,5},{8,10},{9,11},{10,... | collective-permute-start | bytes 2359304 | tf_op jit(solution)/shard_map/ppermute | solution.py:30
  391.9 48.0 %collective-permute-start.28 = (bf16[4,256,1024]{2,1,0:T(8,128)(2,1)}, bf16[4,256,1024]{2,1,0:T(8,128)(2,1)}, u32[]{:S(2)}, u32[]{:S(2)}) collective-permute-start(bf16[4,256,1024]{2,1,0:T(8,128)(2,1)} %bitcast.23), channel_id=1, source_target_pairs={{0,4},{4,0},{8,12},{12,8},{16,20},{20,16},{24,28},{28,24},{1,5},{5... | collective-permute-start | bytes 6291464 | tf_op jit(solution)/shard_map/ppermute | solution.py:30
  446.0 110.2 %collective-permute-start.44 = (bf16[256,1024]{1,0:T(8,128)(2,1)}, bf16[256,1024]{1,0:T(8,128)(2,1)S(1)}, u32[]{:S(2)}, u32[]{:S(2)}) collective-permute-start(bf16[256,1024]{1,0:T(8,128)(2,1)} %get-tuple-element.258), channel_id=1, source_target_pairs={{0,8},{4,12},{8,16},{12,20},{16,24},{20,28},{24,0},{28,4},{1,9},{5... | collective-permute-start | bytes 1572872 | tf_op jit(solution)/shard_map/ppermute | solution.py:35
  447.8 108.4 %collective-permute-start.43 = (bf16[256,1024]{1,0:T(8,128)(2,1)S(1)}, bf16[256,1024]{1,0:T(8,128)(2,1)}, u32[]{:S(2)}, u32[]{:S(2)}) collective-permute-start(bf16[256,1024]{1,0:T(8,128)(2,1)S(1)} %get-tuple-element.259), channel_id=1, source_target_pairs={{0,16},{4,20},{8,24},{12,28},{16,0},{20,4},{24,8},{28,12},{1,17},{... | collective-permute-start | bytes 1572872 | tf_op jit(solution)/shard_map/ppermute | solution.py:35
  450.0 106.2 %collective-permute-start.42 = (bf16[256,1024]{1,0:T(8,128)(2,1)}, bf16[256,1024]{1,0:T(8,128)(2,1)}, u32[]{:S(2)}, u32[]{:S(2)}) collective-permute-start(bf16[256,1024]{1,0:T(8,128)(2,1)} %get-tuple-element.257), channel_id=1, source_target_pairs={{0,24},{4,28},{8,0},{12,4},{16,8},{20,12},{24,16},{28,20},{1,25},{... | collective-permute-start | bytes 1572872 | tf_op jit(solution)/shard_map/ppermute | solution.py:35
  460.3 116.5 %collective-permute-start.46 = (bf16[4,48,3200]{2,1,0:T(8,128)(2,1)S(1)}, bf16[4,48,3200]{2,1,0:T(8,128)(2,1)S(1)}, u32[]{:S(2)}, u32[]{:S(2)}) collective-permute-start(bf16[4,48,3200]{2,1,0:T(8,128)(2,1)S(1)} %dynamic-slice_bitcast_fusion), channel_id=1, source_target_pairs={{0,4},{4,0},{8,12},{12,8},{16,20},{20,16},{24,28},{28,24},{1,5},{5... | collective-permute-start | bytes 3686408 | tf_op jit(solution)/shard_map/ppermute | solution.py:30
  462.1 116.0 %collective-permute-start.57 = (bf16[4,3,192,256]{3,2,1,0:T(8,128)(2,1)S(1)}, bf16[4,3,192,256]{3,2,1,0:T(8,128)(2,1)S(1)}, u32[]{:S(2)}, u32[]{:S(2)}) collective-permute-start(bf16[4,3,192,256]{3,2,1,0:T(8,128)(2,1)S(1)} %copy-done.65), channel_id=1, source_target_pairs={{0,4},{4,0},{8,12},{12,8},{16,20},{20,16},{24,28},{28,24},{1,5},{5... | collective-permute-start | bytes 3538952 | tf_op jit(solution)/shard_map/ppermute | solution.py:30
  578.1 58.2 %collective-permute-start.51 = (bf16[48,3200]{1,0:T(8,128)(2,1)}, bf16[48,3200]{1,0:T(8,128)(2,1)S(1)}, u32[]{:S(2)}, u32[]{:S(2)}) collective-permute-start(bf16[48,3200]{1,0:T(8,128)(2,1)} %get-tuple-element.261), channel_id=1, source_target_pairs={{0,8},{4,12},{8,16},{12,20},{16,24},{20,28},{24,0},{28,4},{1,9},{5... | collective-permute-start | bytes 921608 | tf_op jit(solution)/shard_map/ppermute | solution.py:35
  578.1 58.2 %collective-permute-start.50 = (bf16[48,3200]{1,0:T(8,128)(2,1)}, bf16[48,3200]{1,0:T(8,128)(2,1)}, u32[]{:S(2)}, u32[]{:S(2)}) collective-permute-start(bf16[48,3200]{1,0:T(8,128)(2,1)} %get-tuple-element.262), channel_id=1, source_target_pairs={{0,16},{4,20},{8,24},{12,28},{16,0},{20,4},{24,8},{28,12},{1,17},{... | collective-permute-start | bytes 921608 | tf_op jit(solution)/shard_map/ppermute | solution.py:35
  579.2 45.4 %collective-permute-start.60 = (bf16[3,192,256]{2,1,0:T(8,128)(2,1)S(1)}, bf16[3,192,256]{2,1,0:T(8,128)(2,1)S(1)}, u32[]{:S(2)}, u32[]{:S(2)}) collective-permute-start(bf16[3,192,256]{2,1,0:T(8,128)(2,1)S(1)} %get-tuple-element.273), channel_id=1, source_target_pairs={{0,8},{4,12},{8,16},{12,20},{16,24},{20,28},{24,0},{28,4},{1,9},{5... | collective-permute-start | bytes 884744 | tf_op jit(solution)/shard_map/ppermute | solution.py:35
  584.1 46.5 %collective-permute-start.59 = (bf16[3,192,256]{2,1,0:T(8,128)(2,1)S(1)}, bf16[3,192,256]{2,1,0:T(8,128)(2,1)S(1)}, u32[]{:S(2)}, u32[]{:S(2)}) collective-permute-start(bf16[3,192,256]{2,1,0:T(8,128)(2,1)S(1)} %get-tuple-element.274), channel_id=1, source_target_pairs={{0,16},{4,20},{8,24},{12,28},{16,0},{20,4},{24,8},{28,12},{1,17},{... | collective-permute-start | bytes 884744 | tf_op jit(solution)/shard_map/ppermute | solution.py:35
  631.9 41.2 %all-to-all-start.1 = ((f32[4,3,48,256]{3,2,1,0:T(8,128)}), f32[4,3,48,256]{3,2,1,0:T(8,128)}, u32[]{:S(2)}, u32[]{:S(2)}) async-start(f32[4,3,48,256]{3,2,1,0:T(8,128)} %copy.222), calls=%async_computation.2 | async-start | bytes 1179648 | tf_op jit(solution)/shard_map/all_to_all | solution.py:750
  (131 other events, 1484.6 us)
Sparse Core Ops, SparseCore 0:
  33.7 38.6 all-gather.3
  74.0 53.9 all-gather.5
  215.3 88.3 reduce-scatter.3
  332.0 48.6 reduce-scatter.5
  458.4 120.6 reduce-scatter.7

commit v4 on v3

--- a/solution.py
+++ b/solution.py
@@ -356,49 +356,54 @@
     parts, refs = refs[:8], refs[8:]
     g_ref, wg_ref, wu_ref, wd_ref, *refs = refs
     if final:
-        shared_ref, out_in, dx_in, tail_in, dg_in, *refs = refs
-        out_ref, dx_ref, out_low_ref, dx_low_ref, dg_ref, *refs = refs
+        shared_ref, out_in, dx_in, dg_in, *refs = refs
+        out_hbm, dx_hbm, out_low_ref, dx_low_ref, dg_ref, *refs = refs
         targets = tuple((refs[0].at[:, number], refs[1].at[:, number]) for number in range(2))
         pair_target, refs = (refs[2], refs[3]), refs[4:]
-        x_ref, dy_ref, he_ref, da_ref, db_ref, tail_ref, sem = refs
+        x_ref, dy_ref, he_ref, da_ref, db_ref, out_ref, dx_ref, sem = refs
     else:
-        out_ref, dx_ref, tail_ref, dg_ref, *refs = refs
-        targets, refs = (refs[0], (refs[1], refs[2])), refs[3:]
-        x_ref, dy_ref, he_ref, da_ref, db_ref, sem = refs
+        out_hbm, dx_hbm, dg_ref, line_hbm, *refs = refs
+        x_ref, dy_ref, he_ref, da_ref, db_ref, out_ref, dx_ref, line_ref, sem = refs[2:]
+        targets = (line_ref, (refs[0], refs[1]))
+        line_copy = pltpu.make_async_copy(line_ref, line_hbm, sem.at[19])
     local = pl.program_id(0)
     expert = at_ref[0] + local
     side = at_ref[1]
     total_rows, width = x_ref.shape
     half = total_rows // 2
-    step_rows = 256
+    step_rows = total_rows // 4
     tall = 384
+
+    def loads(number):
+        rows = pl.ds(number * step_rows, step_rows)
+        moves = [(parts[number], x_ref.at[rows, :]), (parts[4 + number], dy_ref.at[rows, :])]
+        if final:
+            moves += [(out_in.at[rows, :], out_ref.at[rows, :]), (dx_in.at[rows, :], dx_ref.at[rows, :])]
+            if number == 0:
+                moves.append((dg_in, dg_ref))
+        return [
+            pltpu.make_async_copy(source, target, sem.at[number * 5 + place])
+            for place, (source, target) in enumerate(moves)
+        ]
+
+    def results(number, count):
+        rows = pl.ds(number * count, count)
+        return [
+            pltpu.make_async_copy(ref.at[rows, :], hbm.at[rows, :], sem.at[number * 2 + place])
+            for place, (ref, hbm) in enumerate(((out_ref, out_hbm), (dx_ref, dx_hbm)))
+        ]
 
     @pl.when(local == 0)
     def _():
-        size = total_rows // 4
-        moves = []
-        for number, source in enumerate(parts):
-            whole = (x_ref, dy_ref)[number // 4]
-            moves.append((source, whole.at[pl.ds(number % 4 * size, size), :]))
-        if final:
-            moves += [(out_in, out_ref), (dx_in, dx_ref), (tail_in, tail_ref), (dg_in, dg_ref)]
-        copies = [
-            pltpu.make_async_copy(source, target, sem.at[number])
-            for number, (source, target) in enumerate(moves)
-        ]
-        for copy in copies:
-            copy.start()
+        for number in range(4):
+            for copy in loads(number):
+                copy.start()
         if not final:
-            for ref in (out_ref, dx_ref, tail_ref, dg_ref):
+            for ref in (out_ref, dx_ref, dg_ref):
                 ref[...] = jnp.zeros_like(ref)
-        for copy in copies:
-            copy.wait()
 
     def add(number, rows, value):
-        if rows.start < half:
-            (out_ref, dx_ref)[number][rows, :] += value
-        else:
-            tail_ref[number, slice(rows.start - half, rows.stop - half), :] += value
+        (out_ref, dx_ref)[number][rows, :] += value
 
     def store_sides(lows, begin, pair):
         per = pair[0].shape[2]
@@ -418,8 +423,14 @@
             for number, low in enumerate(lows):
                 target[line, (side + part) % 2, number] = low[part * per : (part + 1) * per]
 
-    for begin in range(0, total_rows, step_rows):
-        rows = slice(begin, begin + step_rows)
+    for number in range(4):
+        rows = slice(number * step_rows, (number + 1) * step_rows)
+
+        @pl.when(local == 0)
+        def _():
+            for copy in loads(number):
+                copy.wait()
+
         x = x_ref[rows, :]
         lane = lax.broadcasted_iota(jnp.int32, (step_rows, g_ref.shape[1]), 1)
         mine = lane == expert
@@ -439,6 +450,12 @@
         da_ref[rows, :] = pre_low
         db_ref[rows, :] = up_low
         add(1, rows, dot32(pre_low, wg_ref[0], ((1,), (1,))) + dot32(up_low, wu_ref[0], ((1,), (1,))))
+        if not final:
+
+            @pl.when(local == 1)
+            def _():
+                for copy in results(number, step_rows):
+                    copy.start()
 
     @pl.loop(0, width // tall)
     def _(step):
@@ -458,6 +475,18 @@
                     store_lines(lows, begin, target)
 
     if not final:
+
+        @pl.when(local == 0)
+        def _():
+            line_copy.start()
+
+        @pl.when(local == 1)
+        def _():
+            line_copy.wait()
+            for number in range(4):
+                for copy in results(number, step_rows):
+                    copy.wait()
+
         return
 
     @pl.when(local == pl.num_programs(0) - 1)
@@ -476,8 +505,10 @@
             da_ref[rows, :shared] = (back * up * slope).astype(jnp.bfloat16)
             da_ref[rows, shared:] = (back * silu).astype(jnp.bfloat16)
             add(1, rows, dot32(da_ref[rows, :], shared_ref[:, pair_w], ((1,), (1,))))
-        out_low_ref[...] = tail_ref[0].astype(jnp.bfloat16)
-        dx_low_ref[...] = tail_ref[1].astype(jnp.bfloat16)
+        for copy in results(0, half):
+            copy.start()
+        out_low_ref[...] = out_ref[half:, :].astype(jnp.bfloat16)
+        dx_low_ref[...] = dx_ref[half:, :].astype(jnp.bfloat16)
 
         @pl.loop(0, width // tall)
         def _(step):
@@ -486,6 +517,9 @@
             pair_low = dot32(x_ref[:, columns], da_ref[...], ((0,), (0,))).astype(jnp.bfloat16)
             down_low = dot32(dy_ref[:, columns], he_ref[:, :shared], ((0,), (0,))).astype(jnp.bfloat16)
             store_sides((pair_low[:, :shared], pair_low[:, shared:], down_low), begin, pair_target)
+
+        for copy in results(0, half):
+            copy.wait()
 
 
 def experts_call(at, x, dy, gates, weights, first, contexts, shared_w=None, carried=()):
@@ -500,21 +534,24 @@
     apart = pl.BlockSpec(memory_space=pl.ANY)
     part = jax.ShapeDtypeStruct((half, width), jnp.float32)
     low = jax.ShapeDtypeStruct((half, width), jnp.bfloat16)
-    tail = jax.ShapeDtypeStruct((2, half, width), jnp.float32)
+    full = jax.ShapeDtypeStruct((rows, width), jnp.float32)
     table = jax.ShapeDtypeStruct((rows, EXPERTS), jnp.float32)
     term = jax.ShapeDtypeStruct((lines, 3, per, hidden), jnp.bfloat16)
     both = jax.ShapeDtypeStruct((lines, 2, 3, per, hidden), jnp.bfloat16)
     scratch = [pltpu.VMEM((rows, width), jnp.bfloat16)] * 2 + [pltpu.VMEM((rows, hidden), jnp.bfloat16)] * 3
+    scratch += [pltpu.VMEM((rows, width), jnp.float32)] * 2
     if final:
         shared = shared_w.shape[1] // 3
         pair = jax.ShapeDtypeStruct((lines, 3, per, shared), jnp.bfloat16)
-        extra_specs = [whole(shared_w.shape)] + [apart] * 4
+        extra_specs = [whole(shared_w.shape)] + [apart] * 3
         out_shape = (part, part, low, low, table, both, both, pair, pair)
-        scratch.append(pltpu.VMEM(tail.shape, jnp.float32))
+        outside = (0, 1)
     else:
         shared = 0
         extra_specs = []
-        out_shape = (part, part, tail, table, both, term, term)
+        out_shape = (full, full, table, both, term, term)
+        outside = (0, 1, 3)
+        scratch.append(pltpu.VMEM(both.shape, jnp.bfloat16))
     return pl.pallas_call(
         functools.partial(experts_kernel, final),
         grid_spec=pltpu.PrefetchScalarGridSpec(
@@ -528,8 +565,8 @@
                 weight((hidden, width)),
             ]
             + extra_specs,
-            out_specs=[whole(item.shape) for item in out_shape],
-            scratch_shapes=scratch + [pltpu.SemaphoreType.DMA((12,))],
+            out_specs=[apart if place in outside else whole(item.shape) for place, item in enumerate(out_shape)],
+            scratch_shapes=scratch + [pltpu.SemaphoreType.DMA((20,))],
         ),
         out_shape=out_shape,
         compiler_params=pltpu.CompilerParams(vmem_limit_bytes=60 << 20),
@@ -641,6 +678,9 @@
     )
     other_both = flip(send_both, "ctx", 1)
 
+    def nothing(arrived):
+        return 0.0 * arrived[(0,) * arrived.ndim].astype(jnp.float32)
+
     def side_sum(keep, received):
         return keep.astype(jnp.float32) + received.astype(jnp.float32)
 
@@ -660,62 +700,58 @@
     residual_grad = grad_rows + residual_back
     mix_low = residual_grad.astype(jnp.bfloat16)
 
-    def shared_out(extra):
-        count = extra.shape[0]
-        pieces = extra.reshape(count, contexts, members, each).transpose(2, 0, 1, 3)
-        return exchange(pieces.reshape(members, count, share), member)
-
-    def widened(term, pieces):
-        total = sum(pieces)
-        columns = jnp.pad(total, ((0, 128 - total.shape[0]), (0, 0))).T
-        return jnp.concatenate([term, columns], axis=1).astype(jnp.bfloat16).reshape(contexts, each, -1)
-
     attended_grad = sum(
         dot32(mix_low[:, m * share : (m + 1) * share], out_full[m], ((1,), (1,)))
         for m in range(members)
     ).astype(jnp.bfloat16)
     small_terms = jnp.concatenate([router_term, gain_two_term[None]], axis=0)
-    near_one = side_sum(keep_one, after(other_one, dx_moved)) + 0.0 * line_sums[0, 0, 0, 0].astype(jnp.float32)
+    small_terms = jnp.pad(small_terms, ((0, 128 - small_terms.shape[0]), (0, 0)))
+    small_terms = small_terms.reshape(-1, contexts, members, each).transpose(2, 0, 1, 3)
+    small_terms = small_terms.reshape(members, -1, share).astype(jnp.bfloat16)
+    near_one = side_sum(keep_one, after(other_one, dx_moved)) + nothing(line_sums)
     near_one = near_one.astype(jnp.bfloat16)
     sum_one = scatter_lines(near_one)
     attended_grad = after(attended_grad, near_one)
     query_low, kv_keep, kv_send = attention_backward(starts, own, queries, attended_grad, kv_all, log_sums)
     by_line = lambda parts: parts.reshape(lines, rows, kv_width)
-    kv_send = after(by_line(kv_send), other_both)
+    query_across = flip(query_low, "wa", 2)
+    bundle = jnp.concatenate([by_share(mix_low), by_share(normed_low), small_terms], axis=1)
+    bundle = exchange(after(bundle, query_low), member)
+    attended_core = flip(after(jnp.concatenate([attended, attended_across], axis=0), query_low), "wa", 1)
+    query_core = flip(jnp.concatenate([query_low, query_across], axis=0), "wa", 1)
+    moved = bundle[1:] + [attended_core, query_core]
+    kv_send = after(by_line(kv_send), other_both, *moved)
     received = flip(kv_send, "ctx", 1)
-    query_pieces = gather_pieces(query_low)
-    mix_pieces = exchange(after(by_share(mix_low), query_low), member)
-    small_pieces = shared_out(after(small_terms, query_low))
-    normed_pieces = exchange(after(by_share(normed_low), query_low), member)
-    attended_pieces = [attended, attended_across] + [
-        flip(after(piece, query_low), "wa", 1) for piece in (attended, attended_across)
-    ]
-    out_near = out_keep + flip(after(out_send, query_low), "wa", 1).astype(jnp.float32)
+    out_near = out_keep + flip(after(out_send, query_core), "wa", 1).astype(jnp.float32)
     out_moved = flip(out_near[rows:].astype(jnp.bfloat16), "wa", 2)
     out_own = out_near[:rows] + out_moved.astype(jnp.float32)
     block_out = (residual + out_own).astype(jnp.bfloat16).reshape(tokens.shape)
-    moved = mix_pieces[1:] + small_pieces[1:] + normed_pieces[1:] + attended_pieces[2:]
-    received = after(received, out_moved, query_pieces[3], *moved)
+    near_both = (side_sum(keep_both, other_both) + nothing(sum_one)).astype(jnp.bfloat16)
+    sum_both = scatter_lines(near_both)
+    received = after(received, near_both)
     kv_near = by_line(kv_keep).astype(jnp.float32) + received.astype(jnp.float32)
     kv_parts = kv_near.astype(jnp.bfloat16)
     kv_moved = [shift(kv_parts[steps], -steps) for steps in range(1, lines)]
-    near_both = side_sum(keep_both, after(other_both, kv_parts)).astype(jnp.bfloat16)
-    sum_both = scatter_lines(near_both)
-    kv_moved[0] = after(kv_moved[0], near_both)
+    stacked = lambda pieces: jnp.concatenate(pieces, axis=0)
+    mix_share = stacked([piece[:rows] for piece in bundle])
+    normed_share = stacked([piece[rows : 2 * rows] for piece in bundle])
+    small_share = sum(piece[2 * rows :].astype(jnp.float32) for piece in bundle)
+    query_all = stacked([query_low, query_across, query_core])
+    attended_all = stacked([attended, attended_across, attended_core])
+    early_term = jnp.concatenate(
+        [
+            dot32(normed_share, query_all, ((0,), (0,))),
+            dot32(mix_share, attended_all, ((0,), (0,))),
+            small_share.T,
+        ],
+        axis=1,
+    ).astype(jnp.bfloat16)
+    early_sides = to_side(after(early_term.reshape(contexts, each, -1), kv_parts), context)
+    other_pair = flip(after(pair_send, kv_parts), "ctx", 1)
+    kv_moved[0] = after(kv_moved[0], early_sides[1], out_moved)
     kv_low = (kv_near[0] + sum(moved.astype(jnp.float32) for moved in kv_moved)).astype(jnp.bfloat16)
 
-    stacked = lambda pieces: jnp.concatenate(pieces, axis=0)
-    normed_share = stacked(normed_pieces)
-    query_term = dot32(normed_share, stacked(query_pieces), ((0,), (0,))).astype(jnp.bfloat16)
-    out_term = dot32(stacked(mix_pieces), stacked(attended_pieces), ((0,), (0,)))
-    out_term = widened(out_term, small_pieces)
-
-    early_term = jnp.concatenate([query_term.reshape(contexts, each, width), out_term], axis=2)
-    early_sides = to_side(after(early_term, kv_parts), context)
-    other_pair = flip(after(pair_send, kv_parts), "ctx", 1)
-
     kv_low_pieces = gather_pieces(kv_low)
-    early_sides = (early_sides[0], after(early_sides[1], kv_low_pieces[3]))
     kv_low_all = stacked(kv_low_pieces)
     kv_term = dot32(normed_share, kv_low_all, ((0,), (0,)))
     first_grad = dot32(query_low, query_full, ((1,), (1,))) + dot32(kv_low, kv_full, ((1,), (1,)))
@@ -726,7 +762,8 @@
     tokens_grad = (residual_grad + input_back).astype(jnp.bfloat16).reshape(tokens.shape)
     kv_sides = to_side(kv_term.astype(jnp.bfloat16).reshape(contexts, each, kv_width), context)
     kv_sum = line_sum(side_sum(*kv_sides), context)
-    early_sum = line_sum(side_sum(*early_sides), context)
+    early_near = side_sum(early_sides[0], after(early_sides[1], kv_sides[1])) + nothing(sum_both)
+    early_sum = line_sum(early_near, context)
     query_weight_grad, out_sum = early_sum[:, :width], early_sum[:, width:]
     out_weight_grad = out_sum[:, :width].T
     router_weight_grad = out_sum[:, width : width + EXPERTS]
@@ -745,7 +782,7 @@
     expert_up_grad = jnp.stack([total[1] for total in expert_sums]).astype(jnp.float32)
     expert_down_grad = jnp.stack([total[2].T for total in expert_sums]).astype(jnp.float32)
 
-    shared_sum = line_sum(side_sum(pair_keep, after(other_pair, kv_low_pieces[3])), context)
+    shared_sum = line_sum(side_sum(pair_keep, after(other_pair, *kv_moved)), context)
     shared_sum = shared_sum.reshape(3, members, each, hidden_share).transpose(1, 0, 2, 3)
     shared_sum = lax.all_to_all(shared_sum, "wa", 0, 0, tiled=True)
     shared_gate_grad = shared_sum[:, 0].transpose(1, 0, 2).reshape(each, members * hidden_share)

time: 700 us -> 693 us (0.990)
  Pallas kernels: 151 us -> 134 us
  waiting for transfers between devices: 302 us -> 290 us
    ppermute x15, waiting for transfers between devices: 165 us -> 141 us  [shift(): lax.ppermute(value, 'ctx', [(i, (i + 2 * steps) % count) for i in range(c...]
    ppermute x47 -> x39, waiting for transfers between devices: 136 us -> 148 us  [flip(): return lax.ppermute(value, axis, [(i, i ^ bits) for i in range(count)])]
    pallas_call x2, Pallas kernels: 112 us -> 102 us  [experts_call(): pl.pallas_call(functools.partial(experts_kernel, final), grid_spec=pltpu....]
    ppermute x15, starting transfers between devices: 19.2 us -> 27.1 us  [shift(): lax.ppermute(value, 'ctx', [(i, (i + 2 * steps) % count) for i in range(c...]
    slice x1 -> x7, local copies, waits for them, and re-layouts: 1.18 us -> 8.75 us  [the longest x4 5.18 us: shards(): normed_share = stacked([piece[rows:2 * rows] for piece in bundle])]
    ppermute x47 -> x39, starting transfers between devices: 29.6 us -> 27.5 us  [flip(): return lax.ppermute(value, axis, [(i, i ^ bits) for i in range(count)])]
    unnamed x190 -> x154, local copies, waits for them, and re-layouts: 22.8 us -> 24.7 us
  transfers between devices with their start and end apart: 69 -> 61, of which waited for: 28 -> 32; matrix products, arithmetic and copies ran while one was open for 21% -> 22% of each run, Pallas kernels for 15% -> 13%
where the time goes in v4:
time: 693 us; the launch traced here: 684 us
  waiting for transfers between devices  290 us (42%)
  Pallas kernels  134 us (19%)
  local copies, waits for them, and re-layouts  68.1 us (10%)
  starting transfers between devices  66.6 us (10%)
  other arithmetic  65.3 us (9%)
  matrix products  42.2 us (6%)
  between operations  17.2 us (2%)
    ppermute x39, waiting for transfers between devices, flip(): return lax.ppermute(value, axis, [(i, i ^ bits) for i in range(count)])  148 us
    ppermute x15, waiting for transfers between devices, shift(): lax.ppermute(value, 'ctx', [(i, (i + 2 * steps) % count) for i in range(c...  141 us
    pallas_call x2, Pallas kernels, experts_call(): pl.pallas_call(functools.partial(experts_kernel, final), grid_spec=pltpu....  102 us
    ppermute x39, starting transfers between devices, flip(): return lax.ppermute(value, axis, [(i, i ^ bits) for i in range(count)])  27.5 us
    ppermute x15, starting transfers between devices, shift(): lax.ppermute(value, 'ctx', [(i, (i + 2 * steps) % count) for i in range(c...  27.1 us
    unnamed x154, local copies, waits for them, and re-layouts  24.7 us
    dot_general x9, matrix products, dot32(): lax.dot_general(left, right, (dims, ((), ())), preferred_element_type=jnp...  22.7 us
    pallas_call x1, Pallas kernels, attention_backward(): pl.pallas_call(attention_backward_kernel, grid_spec=pltpu.PrefetchScalarG...  18.2 us
  transfers between devices with their start and end apart: 61, of which 32 were waited for; matrix products, arithmetic and copies ran while one was open for 22% of the time, Pallas kernels for 13%

profile of v4, /device:TPU:10, one launch (start us, length us, event | category | flops | bytes accessed | tf_op | source)
XLA Modules:
  0.0 684.0 jit_solution(16570815672648012218)
XLA Ops:
  12.7 20.9 %collective-permute-done.1 = bf16[384,1152]{0,1:T(8,128)(2,1)S(1)} collective-permute-done((bf16[384,1152]{0,1:T(8,128)(2,1)S(1)}, bf16[384,1152]{0,1:T(8,128)(2,1)S(1)}, u32[]{:S(2)}, u32[]{:S(2)}) %collective-permute-start.1) | collective-permute-done | bytes 884768 | tf_op jit(solution)/shard_map/ppermute | solution.py:30
  49.2 10.4 %collective-permute-done.3 = bf16[2,128,1024]{2,1,0:T(8,128)(2,1)} collective-permute-done((bf16[2,128,1024]{2,1,0:T(8,128)(2,1)}, bf16[2,128,1024]{2,1,0:T(8,128)(2,1)}, u32[]{:S(2)}, u32[]{:S(2)}) %collective-permute-start.3) | collective-permute-done | bytes 524320 | tf_op jit(solution)/shard_map/ppermute | solution.py:35
  78.3 8.6 %collective-permute-done.4 = s32[256,6]{0,1:T(8,128)S(1)} collective-permute-done((s32[256,6]{0,1:T(8,128)}, s32[256,6]{0,1:T(8,128)S(1)}, u32[]{:S(2)}, u32[]{:S(2)}) %collective-permute-start.4) | collective-permute-done | bytes 6176 | tf_op jit(solution)/shard_map/ppermute | solution.py:30
  90.4 5.9 all-to-all-start
  103.7 8.9 %collective-permute-done.12 = bf16[2,128,1024]{2,1,0:T(8,128)(2,1)} collective-permute-done((bf16[2,128,1024]{2,1,0:T(8,128)(2,1)}, bf16[2,128,1024]{2,1,0:T(8,128)(2,1)}, u32[]{:S(2)}, u32[]{:S(2)}) %collective-permute-start.12) | collective-permute-done | bytes 524320 | tf_op jit(solution)/shard_map/ppermute | solution.py:30
  118.3 14.4 %attention_forward.1 = (bf16[256,1536]{1,0:T(8,128)(2,1)S(1)}, f32[4,2,384,128]{3,2,1,0:T(8,128)S(1)}) custom-call(s32[8]{0:T(128)S(1)} %bitcast.313, s32[1]{0:T(128)} %bitcast.2.own_ref, bf16[256,1536]{1,0:T(8,128)(2,1)S(1)} %convolution_convert_fusion.q_ref, bf16[16,128,1024]{2,1,0:T(8,128)(2,1)} %constant_dynamic-update-slice_fusion.4.kv_ref), custom_call_target="tpu_custom_call" | custom-call | bytes 1048576 | tf_op jit(solution)/shard_map/attention_forward/pallas_call | solution.py:224
  144.8 14.7 %collective-permute-done.16.refs_2_ = bf16[256,1536]{1,0:T(8,128)(2,1)} collective-permute-done((bf16[256,1536]{1,0:T(8,128)(2,1)S(1)}, bf16[256,1536]{1,0:T(8,128)(2,1)}, u32[]{:S(2)}, u32[]{:S(2)}) %collective-permute-start.16) | collective-permute-done | bytes 786464 | tf_op jit(solution)/shard_map/ppermute | solution.py:30
  165.7 42.7 %experts.1 = (f32[1024,1536]{1,0:T(8,128)}, f32[1024,1536]{1,0:T(8,128)}, f32[1024,16]{1,0:T(8,128)}, bf16[4,2,3,192,512]{4,3,2,1,0:T(8,128)(2,1)}, bf16[4,3,192...) custom-call(s32[2]{0:T(128)} %pad_add_fusion.1.refs_0_, bf16[256,1536]{1,0:T(8,128)(2,1)} %copy-done.4, ...), custom_call_target="tpu_custom_call" | custom-call | bytes 1048576 | tf_op jit(solution)/shard_map/experts/pallas_call | solution.py:555
  211.1 58.8 %experts_final.1 = (f32[512,1536]{1,0:T(8,128)}, f32[512,1536]{1,0:T(8,128)}, bf16[512,1536]{1,0:T(8,128)(2,1)}, bf16[512,1536]{1,0:T(8,128)(2,1)}, f32[1024,16]...) custom-call(s32[2]{0:T(128)} %pad_add_fusion.refs_0_, ...), custom_call_target="tpu_custom_call" | custom-call | bytes 1048576 | tf_op jit(solution)/shard_map/experts_final/pallas_call | solution.py:555
  288.1 11.6 %collective-permute-done.24 = f32[256,16]{1,0:T(8,128)} collective-permute-done((f32[256,16]{1,0:T(8,128)}, f32[256,16]{1,0:T(8,128)}, u32[]{:S(2)}, u32[]{:S(2)}) %collective-permute-start.24) | collective-permute-done | bytes 16416 | tf_op jit(solution)/shard_map/ppermute | solution.py:30
  324.7 18.2 %attention_backward.1 = (bf16[256,1536]{1,0:T(8,128)(2,1)}, bf16[8,128,1024]{2,1,0:T(8,128)(2,1)}, bf16[8,128,1024]{2,1,0:T(8,128)(2,1)}) custom-call(s32[8]{0:T(128)} %bitcast.312, s32[1]{0:T(128)} %bitcast.2.own_ref, bf16[256,1536]{1,0:T(8,128)(2,1)} %copy-done, bf16[256,1536]{1,0:T(8,128)(2,1)} %fusion.19.do_ref, ...), custom_call_target="tpu_custom_call" | custom-call | bytes 1048576 | tf_op jit(solution)/shard_map/attention_backward/pallas_call | solution.py:324
  349.9 13.5 %collective-permute-done.25 = bf16[256,1536]{1,0:T(8,128)(2,1)} collective-permute-done((bf16[256,1536]{1,0:T(8,128)(2,1)}, bf16[256,1536]{1,0:T(8,128)(2,1)}, u32[]{:S(2)}, u32[]{:S(2)}) %collective-permute-start.25) | collective-permute-done | bytes 786464 | tf_op jit(solution)/shard_map/ppermute | solution.py:30
  367.7 13.4 %collective-permute-done.32 = bf16[640,384]{0,1:T(8,128)(2,1)} collective-permute-done((bf16[640,384]{0,1:T(8,128)(2,1)}, bf16[640,384]{0,1:T(8,128)(2,1)}, u32[]{:S(2)}, u32[]{:S(2)}) %collective-permute-start.32) | collective-permute-done | bytes 491552 | tf_op jit(solution)/shard_map/ppermute | solution.py:30
  385.5 9.3 %collective-permute-done.30 = bf16[640,384]{0,1:T(8,128)(2,1)S(1)} collective-permute-done((bf16[640,384]{0,1:T(8,128)(2,1)}, bf16[640,384]{0,1:T(8,128)(2,1)S(1)}, u32[]{:S(2)}, u32[]{:S(2)}) %collective-permute-start.30) | collective-permute-done | bytes 491552 | tf_op jit(solution)/shard_map/ppermute | solution.py:30
  398.4 7.7 %add_convert_fusion = bf16[4,2,3,192,512]{4,3,2,1,0:T(8,128)(2,1)} fusion(bf16[4,2,3,192,512]{4,3,2,1,0:T(8,128)(2,1)} %collective-permute-done.29, bf16[4,2,3,192,512]{4,3,2,1,0:T(8,128)(2,1)} %get-tuple-element.93, f32[]{:T(128)} %bitcast.36), kind=kLoop, calls=%fused_computation | loop fusion | flops 11796480 | bytes 14155780 | tf_op jit(solution)/shard_map/convert_element_type | solution.py:729
  419.9 24.0 %collective-permute-done.34 = bf16[4,256,1024]{2,1,0:T(8,128)(2,1)} collective-permute-done((bf16[4,256,1024]{2,1,0:T(8,128)(2,1)}, bf16[4,256,1024]{2,1,0:T(8,128)(2,1)}, u32[]{:S(2)}, u32[]{:S(2)}) %collective-permute-start.34) | collective-permute-done | bytes 2097184 | tf_op jit(solution)/shard_map/ppermute | solution.py:30
  458.1 6.0 collective-permute-start.37
  470.4 33.7 %collective-permute-done.35 = bf16[256,1024]{1,0:T(8,128)(2,1)} collective-permute-done((bf16[256,1024]{1,0:T(8,128)(2,1)}, bf16[256,1024]{1,0:T(8,128)(2,1)}, u32[]{:S(2)}, u32[]{:S(2)}) %collective-permute-start.35) | collective-permute-done | bytes 524320 | tf_op jit(solution)/shard_map/ppermute | solution.py:35
  507.7 30.6 %collective-permute-done.37 = bf16[256,1024]{1,0:T(8,128)(2,1)} collective-permute-done((bf16[256,1024]{1,0:T(8,128)(2,1)}, bf16[256,1024]{1,0:T(8,128)(2,1)}, u32[]{:S(2)}, u32[]{:S(2)}) %collective-permute-start.37) | collective-permute-done | bytes 524320 | tf_op jit(solution)/shard_map/ppermute | solution.py:35
  555.0 16.2 %collective-permute-done.51 = bf16[3,192,256]{2,1,0:T(8,128)(2,1)S(1)} collective-permute-done((bf16[3,192,256]{2,1,0:T(8,128)(2,1)S(1)}, bf16[3,192,256]{2,1,0:T(8,128)(2,1)S(1)}, u32[]{:S(2)}, u32[]{:S(2)}) %collective-permute-start.51) | collective-permute-done | bytes 294944 | tf_op jit(solution)/shard_map/ppermute | solution.py:35
  597.2 5.8 collective-permute-done.53
  615.8 5.6 collective-permute-done.48
  621.4 13.2 %collective-permute-done.47 = bf16[48,1024]{0,1:T(8,128)(2,1)} collective-permute-done((bf16[48,1024]{0,1:T(8,128)(2,1)}, bf16[48,1024]{0,1:T(8,128)(2,1)}, u32[]{:S(2)}, u32[]{:S(2)}) %collective-permute-start.47) | collective-permute-done | bytes 98336 | tf_op jit(solution)/shard_map/ppermute | solution.py:35
  653.2 16.5 %collective-permute-done.44 = bf16[48,3200]{1,0:T(8,128)(2,1)S(1)} collective-permute-done((bf16[48,3200]{1,0:T(8,128)(2,1)S(1)}, bf16[48,3200]{1,0:T(8,128)(2,1)S(1)}, u32[]{:S(2)}, u32[]{:S(2)}) %collective-permute-start.44) | collective-permute-done | bytes 307232 | tf_op jit(solution)/shard_map/ppermute | solution.py:35
  (392 shorter events, 256.3 us)
Async XLA Ops:
  7.2 107.3 %all-gather.4.cloned.1.call-start = ((), (), s32[]{:S(2)}) async-start(), calls=%async_computation.5 | async-start | bytes 5898240 | tf_op jit(solution)/shard_map/all_gather | solution.py:621
  33.6 100.2 %all-gather.6.cloned.1.call-start = ((), (), s32[]{:S(2)}) async-start(), calls=%async_computation.9 | async-start | bytes 5898240 | tf_op jit(solution)/shard_map/all_gather | solution.py:622
  69.3 70.6 %collective-permute-start.14 = (bf16[256,1536]{1,0:T(8,128)(2,1)}, bf16[256,1536]{1,0:T(8,128)(2,1)}, u32[]{:S(2)}, u32[]{:S(2)}) collective-permute-start(bf16[256,1536]{1,0:T(8,128)(2,1)} %bitcast.17.refs_5_), channel_id=1, source_target_pairs={{0,1},{1,0},{2,3},{3,2},{4,5},{5,4},{6,7},{7,6},{8,9},{9,8},{10,11... | collective-permute-start | bytes 2359304 | tf_op jit(solution)/shard_map/ppermute | solution.py:30
  90.4 49.5 %collective-permute-start.15 = (bf16[256,1536]{1,0:T(8,128)(2,1)}, bf16[256,1536]{1,0:T(8,128)(2,1)}, u32[]{:S(2)}, u32[]{:S(2)}) collective-permute-start(bf16[256,1536]{1,0:T(8,128)(2,1)} %collective-permute-done.13.refs_6_), channel_id=1, source_target_pairs={{0,1},{1,0},{2,3},{3,2},{4,5},{5,4},{6,7},{7,6},{8,9},{9,8},{10,11... | collective-permute-start | bytes 2359304 | tf_op jit(solution)/shard_map/ppermute | solution.py:30
  90.4 49.5 %all-to-all-start = ((bf16[4,384,768]{2,1,0:T(8,128)(2,1)}), bf16[4,384,768]{2,1,0:T(8,128)(2,1)}, u32[]{:S(2)}, u32[]{:S(2)}) async-start(bf16[4,384,768]{2,1,0:T(8,128)(2,1)} %maximum_bitcast_fusion), calls=%async_computation | async-start | bytes 4718592 | tf_op jit(solution)/shard_map/all_to_all | solution.py:648
  96.3 210.8 %reduce-scatter.4.cloned.1.call-start = ((), (), s32[]{:S(2)}) async-start(), calls=%async_computation.6 | async-start | bytes 5898240 | tf_op jit(solution)/shard_map/reduce_scatter | solution.py:103
  208.5 188.1 %reduce-scatter.6.cloned.1.call-start = ((), (), s32[]{:S(2)}) async-start(), calls=%async_computation.7 | async-start | bytes 2949120 | tf_op jit(solution)/shard_map/reduce_scatter | solution.py:103
  208.6 61.3 %collective-permute-start.19 = (bf16[4,3,192,512]{3,2,1,0:T(8,128)(2,1)}, bf16[4,3,192,512]{3,2,1,0:T(8,128)(2,1)}, u32[]{:S(2)}, u32[]{:S(2)}) collective-permute-start(bf16[4,3,192,512]{3,2,1,0:T(8,128)(2,1)} %get-tuple-element.76), channel_id=1, source_target_pairs={{0,4},{4,0},{8,12},{12,8},{16,20},{20,16},{24,28},{28,24},{1,5},{5... | collective-permute-start | bytes 7077896 | tf_op jit(solution)/shard_map/ppermute | solution.py:30
  209.0 60.9 %collective-permute-start.20 = (bf16[256,1536]{1,0:T(8,128)(2,1)S(1)}, bf16[256,1536]{1,0:T(8,128)(2,1)S(1)}, u32[]{:S(2)}, u32[]{:S(2)}) collective-permute-start(bf16[256,1536]{1,0:T(8,128)(2,1)S(1)} %get-tuple-element.77), channel_id=1, source_target_pairs={{0,2},{1,3},{2,0},{3,1},{4,6},{5,7},{6,4},{7,5},{8,10},{9,11},{10,... | collective-permute-start | bytes 2359304 | tf_op jit(solution)/shard_map/ppermute | solution.py:30
  287.5 108.9 %collective-permute-start.29 = (bf16[4,2,3,192,512]{4,3,2,1,0:T(8,128)(2,1)}, bf16[4,2,3,192,512]{4,3,2,1,0:T(8,128)(2,1)}, u32[]{:S(2)}, u32[]{:S(2)}) collective-permute-start(bf16[4,2,3,192,512]{4,3,2,1,0:T(8,128)(2,1)} %get-tuple-element.89), channel_id=1, source_target_pairs={{0,4},{4,0},{8,12},{12,8},{16,20},{20,16},{24,28},{28,24},{1,5},{5... | collective-permute-start | bytes 14155784 | tf_op jit(solution)/shard_map/ppermute | solution.py:30
  313.6 325.8 %reduce-scatter.8.cloned.1.call-start = ((), (), s32[]{:S(2)}) async-start(), calls=%async_computation.8 | async-start | bytes 5898240 | tf_op jit(solution)/shard_map/reduce_scatter | solution.py:103
  347.2 49.2 %collective-permute-start.33 = (bf16[512,1536]{1,0:T(8,128)(2,1)}, bf16[512,1536]{1,0:T(8,128)(2,1)}, u32[]{:S(2)}, u32[]{:S(2)}) collective-permute-start(bf16[512,1536]{1,0:T(8,128)(2,1)} %pad_maximum_fusion.4), channel_id=1, source_target_pairs={{0,1},{1,0},{2,3},{3,2},{4,5},{5,4},{6,7},{7,6},{8,9},{9,8},{10,11... | collective-permute-start | bytes 4718600 | tf_op jit(solution)/shard_map/ppermute | solution.py:30
  365.8 30.6 %collective-permute-start.26 = (bf16[512,1536]{1,0:T(8,128)(2,1)}, bf16[512,1536]{1,0:T(8,128)(2,1)}, u32[]{:S(2)}, u32[]{:S(2)}) collective-permute-start(bf16[512,1536]{1,0:T(8,128)(2,1)} %pad_maximum_fusion.3), channel_id=1, source_target_pairs={{0,1},{1,0},{2,3},{3,2},{4,5},{5,4},{6,7},{7,6},{8,9},{9,8},{10,11... | collective-permute-start | bytes 4718600 | tf_op jit(solution)/shard_map/ppermute | solution.py:30
  396.4 47.5 %collective-permute-start.34 = (bf16[4,256,1024]{2,1,0:T(8,128)(2,1)}, bf16[4,256,1024]{2,1,0:T(8,128)(2,1)}, u32[]{:S(2)}, u32[]{:S(2)}) collective-permute-start(bf16[4,256,1024]{2,1,0:T(8,128)(2,1)} %bitcast.23), channel_id=1, source_target_pairs={{0,4},{4,0},{8,12},{12,8},{16,20},{20,16},{24,28},{28,24},{1,5},{5... | collective-permute-start | bytes 6291464 | tf_op jit(solution)/shard_map/ppermute | solution.py:30
  419.6 37.6 %collective-permute-start.28 = (bf16[256,1536]{1,0:T(8,128)(2,1)S(1)}, bf16[256,1536]{1,0:T(8,128)(2,1)S(1)}, u32[]{:S(2)}, u32[]{:S(2)}) collective-permute-start(bf16[256,1536]{1,0:T(8,128)(2,1)S(1)} %slice.437), channel_id=1, source_target_pairs={{0,2},{1,3},{2,0},{3,1},{4,6},{5,7},{6,4},{7,5},{8,10},{9,11},{10,... | collective-permute-start | bytes 2359304 | tf_op jit(solution)/shard_map/ppermute | solution.py:30
  449.8 54.4 %collective-permute-start.36 = (bf16[4,48,3200]{2,1,0:T(8,128)(2,1)}, bf16[4,48,3200]{2,1,0:T(8,128)(2,1)}, u32[]{:S(2)}, u32[]{:S(2)}) collective-permute-start(bf16[4,48,3200]{2,1,0:T(8,128)(2,1)} %dynamic-slice_bitcast_fusion), channel_id=1, source_target_pairs={{0,4},{4,0},{8,12},{12,8},{16,20},{20,16},{24,28},{28,24},{1,5},{5... | collective-permute-start | bytes 3686408 | tf_op jit(solution)/shard_map/ppermute | solution.py:30
  450.0 91.8 %collective-permute-start.49 = (bf16[4,3,192,256]{3,2,1,0:T(8,128)(2,1)}, bf16[4,3,192,256]{3,2,1,0:T(8,128)(2,1)}, u32[]{:S(2)}, u32[]{:S(2)}) collective-permute-start(bf16[4,3,192,256]{3,2,1,0:T(8,128)(2,1)} %get-tuple-element.100), channel_id=1, source_target_pairs={{0,4},{4,0},{8,12},{12,8},{16,20},{20,16},{24,28},{28,24},{1,5},{5... | collective-permute-start | bytes 3538952 | tf_op jit(solution)/shard_map/ppermute | solution.py:30
  453.0 51.2 %collective-permute-start.35 = (bf16[256,1024]{1,0:T(8,128)(2,1)}, bf16[256,1024]{1,0:T(8,128)(2,1)}, u32[]{:S(2)}, u32[]{:S(2)}) collective-permute-start(bf16[256,1024]{1,0:T(8,128)(2,1)} %get-tuple-element.232), channel_id=1, source_target_pairs={{0,24},{4,28},{8,0},{12,4},{16,8},{20,12},{24,16},{28,20},{1,25},{... | collective-permute-start | bytes 1572872 | tf_op jit(solution)/shard_map/ppermute | solution.py:35
  457.0 50.6 %collective-permute-start.38 = (bf16[256,1024]{1,0:T(8,128)(2,1)}, bf16[256,1024]{1,0:T(8,128)(2,1)}, u32[]{:S(2)}, u32[]{:S(2)}) collective-permute-start(bf16[256,1024]{1,0:T(8,128)(2,1)} %get-tuple-element.233), channel_id=1, source_target_pairs={{0,8},{4,12},{8,16},{12,20},{16,24},{20,28},{24,0},{28,4},{1,9},{5... | collective-permute-start | bytes 1572872 | tf_op jit(solution)/shard_map/ppermute | solution.py:35
  458.1 80.2 %collective-permute-start.37 = (bf16[256,1024]{1,0:T(8,128)(2,1)}, bf16[256,1024]{1,0:T(8,128)(2,1)}, u32[]{:S(2)}, u32[]{:S(2)}) collective-permute-start(bf16[256,1024]{1,0:T(8,128)(2,1)} %get-tuple-element.234), channel_id=1, source_target_pairs={{0,16},{4,20},{8,24},{12,28},{16,0},{20,4},{24,8},{28,12},{1,17},{... | collective-permute-start | bytes 1572872 | tf_op jit(solution)/shard_map/ppermute | solution.py:35
  541.2 40.4 %collective-permute-start.39 = (bf16[256,1024]{1,0:T(8,128)(2,1)}, bf16[256,1024]{1,0:T(8,128)(2,1)}, u32[]{:S(2)}, u32[]{:S(2)}) collective-permute-start(bf16[256,1024]{1,0:T(8,128)(2,1)} %fusion.48), channel_id=1, source_target_pairs={{0,2},{1,3},{2,0},{3,1},{4,6},{5,7},{6,4},{7,5},{8,10},{9,11},{10,... | collective-permute-start | bytes 1572872 | tf_op jit(solution)/shard_map/ppermute | solution.py:30
  541.8 51.0 %collective-permute-start.40 = (bf16[256,1024]{1,0:T(8,128)(2,1)}, bf16[256,1024]{1,0:T(8,128)(2,1)}, u32[]{:S(2)}, u32[]{:S(2)}) collective-permute-start(bf16[256,1024]{1,0:T(8,128)(2,1)} %fusion.48), channel_id=1, source_target_pairs={{0,1},{1,0},{2,3},{3,2},{4,5},{5,4},{6,7},{7,6},{8,9},{9,8},{10,11... | collective-permute-start | bytes 1572872 | tf_op jit(solution)/shard_map/ppermute | solution.py:30
  643.1 26.7 %collective-permute-start.44 = (bf16[48,3200]{1,0:T(8,128)(2,1)S(1)}, bf16[48,3200]{1,0:T(8,128)(2,1)S(1)}, u32[]{:S(2)}, u32[]{:S(2)}) collective-permute-start(bf16[48,3200]{1,0:T(8,128)(2,1)S(1)} %get-tuple-element.242), channel_id=1, source_target_pairs={{0,16},{4,20},{8,24},{12,28},{16,0},{20,4},{24,8},{28,12},{1,17},{... | collective-permute-start | bytes 921608 | tf_op jit(solution)/shard_map/ppermute | solution.py:35
  646.5 26.1 %collective-permute-start.43 = (bf16[48,3200]{1,0:T(8,128)(2,1)S(1)}, bf16[48,3200]{1,0:T(8,128)(2,1)S(1)}, u32[]{:S(2)}, u32[]{:S(2)}) collective-permute-start(bf16[48,3200]{1,0:T(8,128)(2,1)S(1)} %get-tuple-element.240), channel_id=1, source_target_pairs={{0,24},{4,28},{8,0},{12,4},{16,8},{20,12},{24,16},{28,20},{1,25},{... | collective-permute-start | bytes 921608 | tf_op jit(solution)/shard_map/ppermute | solution.py:35
  (106 other events, 997.6 us)
Sparse Core Ops, SparseCore 0:
  33.7 38.6 all-gather.3
  74.0 54.0 all-gather.5
  208.6 87.8 reduce-scatter.3
  313.8 49.1 reduce-scatter.5
  406.3 133.1 reduce-scatter.7

commit v5 on v4

--- a/solution.py
+++ b/solution.py
@@ -89,13 +89,13 @@
     return keep, flip(lax.dynamic_index_in_dim(pairs, 1 - index % 2, 1, keepdims=False), "ctx", 1)
 
 
-def line_sum(near, index):
+def line_sum(near, index, *before):
     lines, line = near.shape[0], index // 2
     low = near.astype(jnp.bfloat16)
     total = lax.dynamic_index_in_dim(near, line, 0, keepdims=False)
     for steps in range(1, lines):
         piece = lax.dynamic_index_in_dim(low, (line + lines - steps) % lines, 0, keepdims=False)
-        total = total + shift(piece, -steps).astype(jnp.float32)
+        total = total + after(shift(piece, -steps), *before).astype(jnp.float32)
     return total
 
 
@@ -751,8 +751,9 @@
     kv_moved[0] = after(kv_moved[0], early_sides[1], out_moved)
     kv_low = (kv_near[0] + sum(moved.astype(jnp.float32) for moved in kv_moved)).astype(jnp.bfloat16)
 
-    kv_low_pieces = gather_pieces(kv_low)
-    kv_low_all = stacked(kv_low_pieces)
+    kv_across = flip(kv_low, "wa", 2)
+    kv_pair = jnp.concatenate([kv_low, kv_across], axis=0)
+    kv_low_all = jnp.concatenate([kv_pair, flip(kv_pair, "wa", 1)], axis=0)
     kv_term = dot32(normed_share, kv_low_all, ((0,), (0,)))
     first_grad = dot32(query_low, query_full, ((1,), (1,))) + dot32(kv_low, kv_full, ((1,), (1,)))
     scaled = first_grad * gain_one
@@ -762,8 +763,8 @@
     tokens_grad = (residual_grad + input_back).astype(jnp.bfloat16).reshape(tokens.shape)
     kv_sides = to_side(kv_term.astype(jnp.bfloat16).reshape(contexts, each, kv_width), context)
     kv_sum = line_sum(side_sum(*kv_sides), context)
-    early_near = side_sum(early_sides[0], after(early_sides[1], kv_sides[1])) + nothing(sum_both)
-    early_sum = line_sum(early_near, context)
+    early_near = side_sum(early_sides[0], after(early_sides[1], *kv_moved))
+    early_sum = line_sum(early_near, context, kv_sides[1])
     query_weight_grad, out_sum = early_sum[:, :width], early_sum[:, width:]
     out_weight_grad = out_sum[:, :width].T
     router_weight_grad = out_sum[:, width : width + EXPERTS]
@@ -775,14 +776,14 @@
         + jnp.sum(mine(kv_full).astype(jnp.float32) * kv_sum, axis=1)
     ) / mine(gain_one)
 
-    line_zero = flip(after(line_sums[1], kv_low_pieces[1]), "ctx", 1)
+    line_zero = flip((line_sums[1].astype(jnp.float32) + nothing(sum_both)).astype(jnp.bfloat16), "ctx", 1)
     sum_zero = line_sums[0].astype(jnp.float32) + line_zero.astype(jnp.float32)
     expert_sums = [sum_zero, sum_one, sum_both[0], sum_both[1]]
     expert_gate_grad = jnp.stack([total[0] for total in expert_sums]).astype(jnp.float32)
     expert_up_grad = jnp.stack([total[1] for total in expert_sums]).astype(jnp.float32)
     expert_down_grad = jnp.stack([total[2].T for total in expert_sums]).astype(jnp.float32)
 
-    shared_sum = line_sum(side_sum(pair_keep, after(other_pair, *kv_moved)), context)
+    shared_sum = line_sum(side_sum(pair_keep, after(other_pair, kv_sides[1])), context)
     shared_sum = shared_sum.reshape(3, members, each, hidden_share).transpose(1, 0, 2, 3)
     shared_sum = lax.all_to_all(shared_sum, "wa", 0, 0, tiled=True)
     shared_gate_grad = shared_sum[:, 0].transpose(1, 0, 2).reshape(each, members * hidden_share)

time: 693 us -> 676 us (0.975)
  starting transfers between devices: 66.6 us -> 84.1 us
  waiting for transfers between devices: 290 us -> 278 us
  local copies, waits for them, and re-layouts: 68.1 us -> 56.4 us
    ppermute x15, waiting for transfers between devices: 141 us -> 124 us  [shift(): lax.ppermute(value, 'ctx', [(i, (i + 2 * steps) % count) for i in range(c...]
    ppermute x39 -> x38, starting transfers between devices: 27.5 us -> 41.3 us  [flip(): return lax.ppermute(value, axis, [(i, i ^ bits) for i in range(count)])]
    ppermute x39 -> x38, waiting for transfers between devices: 148 us -> 153 us  [flip(): return lax.ppermute(value, axis, [(i, i ^ bits) for i in range(count)])]
    unnamed x154 -> x168, local copies, waits for them, and re-layouts: 24.7 us -> 20.7 us
  transfers between devices with their start and end apart: 61 -> 60, of which waited for: 32 -> 33; matrix products, arithmetic and copies ran while one was open for 22% -> 21% of each run, Pallas kernels for 13% -> 13%
where the time goes in v5:
time: 676 us; the launch traced here: 669 us
  waiting for transfers between devices  278 us (41%)
  Pallas kernels  128 us (19%)
  starting transfers between devices  84.1 us (12%)
  other arithmetic  66.8 us (10%)
  local copies, waits for them, and re-layouts  56.4 us (8%)
  matrix products  38 us (6%)
  between operations  17.3 us (3%)
    ppermute x38, waiting for transfers between devices, flip(): return lax.ppermute(value, axis, [(i, i ^ bits) for i in range(count)])  153 us
    ppermute x15, waiting for transfers between devices, shift(): lax.ppermute(value, 'ctx', [(i, (i + 2 * steps) % count) for i in range(c...  124 us
    pallas_call x2, Pallas kernels, experts_call(): pl.pallas_call(functools.partial(experts_kernel, final), grid_spec=pltpu....  101 us
    ppermute x38, starting transfers between devices, flip(): return lax.ppermute(value, axis, [(i, i ^ bits) for i in range(count)])  41.3 us
    ppermute x15, starting transfers between devices, shift(): lax.ppermute(value, 'ctx', [(i, (i + 2 * steps) % count) for i in range(c...  31.3 us
    unnamed x168, local copies, waits for them, and re-layouts  20.7 us
    dot_general x9, matrix products, dot32(): lax.dot_general(left, right, (dims, ((), ())), preferred_element_type=jnp...  19.4 us
    pallas_call x1, Pallas kernels, attention_backward(): pl.pallas_call(attention_backward_kernel, grid_spec=pltpu.PrefetchScalarG...  14.8 us
  transfers between devices with their start and end apart: 60, of which 33 were waited for; matrix products, arithmetic and copies ran while one was open for 21% of the time, Pallas kernels for 13%

profile of v5, /device:TPU:10, one launch (start us, length us, event | category | flops | bytes accessed | tf_op | source)
XLA Modules:
  0.0 668.8 jit_solution(16998918066501057748)
XLA Ops:
  12.7 20.9 %collective-permute-done.1 = bf16[384,1152]{0,1:T(8,128)(2,1)S(1)} collective-permute-done((bf16[384,1152]{0,1:T(8,128)(2,1)S(1)}, bf16[384,1152]{0,1:T(8,128)(2,1)S(1)}, u32[]{:S(2)}, u32[]{:S(2)}) %collective-permute-start.1) | collective-permute-done | bytes 884768 | tf_op jit(solution)/shard_map/ppermute | solution.py:30
  49.2 10.4 %collective-permute-done.3 = bf16[2,128,1024]{2,1,0:T(8,128)(2,1)} collective-permute-done((bf16[2,128,1024]{2,1,0:T(8,128)(2,1)}, bf16[2,128,1024]{2,1,0:T(8,128)(2,1)}, u32[]{:S(2)}, u32[]{:S(2)}) %collective-permute-start.3) | collective-permute-done | bytes 524320 | tf_op jit(solution)/shard_map/ppermute | solution.py:35
  78.3 8.6 %collective-permute-done.4 = s32[256,6]{0,1:T(8,128)S(1)} collective-permute-done((s32[256,6]{0,1:T(8,128)}, s32[256,6]{0,1:T(8,128)S(1)}, u32[]{:S(2)}, u32[]{:S(2)}) %collective-permute-start.4) | collective-permute-done | bytes 6176 | tf_op jit(solution)/shard_map/ppermute | solution.py:30
  90.4 5.9 all-to-all-start
  103.7 8.9 %collective-permute-done.12 = bf16[2,128,1024]{2,1,0:T(8,128)(2,1)} collective-permute-done((bf16[2,128,1024]{2,1,0:T(8,128)(2,1)}, bf16[2,128,1024]{2,1,0:T(8,128)(2,1)}, u32[]{:S(2)}, u32[]{:S(2)}) %collective-permute-start.12) | collective-permute-done | bytes 524320 | tf_op jit(solution)/shard_map/ppermute | solution.py:30
  118.3 11.8 %attention_forward.1 = (bf16[256,1536]{1,0:T(8,128)(2,1)S(1)}, f32[4,2,384,128]{3,2,1,0:T(8,128)S(1)}) custom-call(s32[8]{0:T(128)S(1)} %bitcast.313, s32[1]{0:T(128)} %bitcast.2.own_ref, bf16[256,1536]{1,0:T(8,128)(2,1)S(1)} %convolution_convert_fusion.q_ref, bf16[16,128,1024]{2,1,0:T(8,128)(2,1)} %constant_dynamic-update-slice_fusion.4.kv_ref), custom_call_target="tpu_custom_call" | custom-call | bytes 1048576 | tf_op jit(solution)/shard_map/attention_forward/pallas_call | solution.py:224
  144.8 9.6 %collective-permute-done.16.refs_2_ = bf16[256,1536]{1,0:T(8,128)(2,1)} collective-permute-done((bf16[256,1536]{1,0:T(8,128)(2,1)S(1)}, bf16[256,1536]{1,0:T(8,128)(2,1)}, u32[]{:S(2)}, u32[]{:S(2)}) %collective-permute-start.16) | collective-permute-done | bytes 786464 | tf_op jit(solution)/shard_map/ppermute | solution.py:30
  163.2 42.8 %experts.1 = (f32[1024,1536]{1,0:T(8,128)}, f32[1024,1536]{1,0:T(8,128)}, f32[1024,16]{1,0:T(8,128)}, bf16[4,2,3,192,512]{4,3,2,1,0:T(8,128)(2,1)}, bf16[4,3,192...) custom-call(s32[2]{0:T(128)} %pad_add_fusion.1.refs_0_, bf16[256,1536]{1,0:T(8,128)(2,1)} %copy-done.4, ...), custom_call_target="tpu_custom_call" | custom-call | bytes 1048576 | tf_op jit(solution)/shard_map/experts/pallas_call | solution.py:555
  211.1 58.4 %experts_final.1 = (f32[512,1536]{1,0:T(8,128)}, f32[512,1536]{1,0:T(8,128)}, bf16[512,1536]{1,0:T(8,128)(2,1)}, bf16[512,1536]{1,0:T(8,128)(2,1)}, f32[1024,16]...) custom-call(s32[2]{0:T(128)} %pad_add_fusion.refs_0_, ...), custom_call_target="tpu_custom_call" | custom-call | bytes 1048576 | tf_op jit(solution)/shard_map/experts_final/pallas_call | solution.py:555
  287.0 12.3 %collective-permute-done.24 = f32[256,16]{1,0:T(8,128)} collective-permute-done((f32[256,16]{1,0:T(8,128)}, f32[256,16]{1,0:T(8,128)}, u32[]{:S(2)}, u32[]{:S(2)}) %collective-permute-start.24) | collective-permute-done | bytes 16416 | tf_op jit(solution)/shard_map/ppermute | solution.py:30
  321.6 14.8 %attention_backward.1 = (bf16[256,1536]{1,0:T(8,128)(2,1)}, bf16[8,128,1024]{2,1,0:T(8,128)(2,1)}, bf16[8,128,1024]{2,1,0:T(8,128)(2,1)}) custom-call(s32[8]{0:T(128)} %bitcast.312, s32[1]{0:T(128)} %bitcast.2.own_ref, bf16[256,1536]{1,0:T(8,128)(2,1)} %copy-done, bf16[256,1536]{1,0:T(8,128)(2,1)} %fusion.19.do_ref, ...), custom_call_target="tpu_custom_call" | custom-call | bytes 1048576 | tf_op jit(solution)/shard_map/attention_backward/pallas_call | solution.py:324
  347.0 6.3 collective-permute-done.25
  361.8 12.9 %collective-permute-done.32 = bf16[640,384]{0,1:T(8,128)(2,1)} collective-permute-done((bf16[640,384]{0,1:T(8,128)(2,1)}, bf16[640,384]{0,1:T(8,128)(2,1)}, u32[]{:S(2)}, u32[]{:S(2)}) %collective-permute-start.32) | collective-permute-done | bytes 491552 | tf_op jit(solution)/shard_map/ppermute | solution.py:30
  377.7 10.7 %collective-permute-done.30 = bf16[640,384]{0,1:T(8,128)(2,1)S(1)} collective-permute-done((bf16[640,384]{0,1:T(8,128)(2,1)}, bf16[640,384]{0,1:T(8,128)(2,1)S(1)}, u32[]{:S(2)}, u32[]{:S(2)}) %collective-permute-start.30) | collective-permute-done | bytes 491552 | tf_op jit(solution)/shard_map/ppermute | solution.py:30
  400.3 7.7 %add_convert_fusion = bf16[4,2,3,192,512]{4,3,2,1,0:T(8,128)(2,1)} fusion(bf16[4,2,3,192,512]{4,3,2,1,0:T(8,128)(2,1)} %collective-permute-done.29, bf16[4,2,3,192,512]{4,3,2,1,0:T(8,128)(2,1)} %get-tuple-element.95, f32[]{:T(128)} %bitcast.36), kind=kLoop, calls=%fused_computation | loop fusion | flops 11796480 | bytes 14155780 | tf_op jit(solution)/shard_map/convert_element_type | solution.py:729
  408.0 29.8 %collective-permute-done.34 = bf16[4,256,1024]{2,1,0:T(8,128)(2,1)} collective-permute-done((bf16[4,256,1024]{2,1,0:T(8,128)(2,1)}, bf16[4,256,1024]{2,1,0:T(8,128)(2,1)}, u32[]{:S(2)}, u32[]{:S(2)}) %collective-permute-start.34) | collective-permute-done | bytes 2097184 | tf_op jit(solution)/shard_map/ppermute | solution.py:30
  452.3 12.7 %collective-permute-start.37 = (bf16[256,1024]{1,0:T(8,128)(2,1)}, bf16[256,1024]{1,0:T(8,128)(2,1)}, u32[]{:S(2)}, u32[]{:S(2)}) collective-permute-start(bf16[256,1024]{1,0:T(8,128)(2,1)} %get-tuple-element.238), channel_id=1, source_target_pairs={{0,16},{4,20},{8,24},{12,28},{16,0},{20,4},{24,8},{28,12},{1,17},{... | collective-permute-start | bytes 1572872 | tf_op jit(solution)/shard_map/ppermute | solution.py:35
  467.5 21.9 %collective-permute-done.35 = bf16[256,1024]{1,0:T(8,128)(2,1)} collective-permute-done((bf16[256,1024]{1,0:T(8,128)(2,1)}, bf16[256,1024]{1,0:T(8,128)(2,1)}, u32[]{:S(2)}, u32[]{:S(2)}) %collective-permute-start.35) | collective-permute-done | bytes 524320 | tf_op jit(solution)/shard_map/ppermute | solution.py:35
  489.4 20.1 %collective-permute-done.38 = bf16[256,1024]{1,0:T(8,128)(2,1)} collective-permute-done((bf16[256,1024]{1,0:T(8,128)(2,1)}, bf16[256,1024]{1,0:T(8,128)(2,1)}, u32[]{:S(2)}, u32[]{:S(2)}) %collective-permute-start.38) | collective-permute-done | bytes 524320 | tf_op jit(solution)/shard_map/ppermute | solution.py:35
  509.5 34.4 %collective-permute-done.37 = bf16[256,1024]{1,0:T(8,128)(2,1)} collective-permute-done((bf16[256,1024]{1,0:T(8,128)(2,1)}, bf16[256,1024]{1,0:T(8,128)(2,1)}, u32[]{:S(2)}, u32[]{:S(2)}) %collective-permute-start.37) | collective-permute-done | bytes 524320 | tf_op jit(solution)/shard_map/ppermute | solution.py:35
  570.6 6.5 collective-permute-done.42
  597.5 7.7 %collective-permute-done.46 = bf16[48,1024]{0,1:T(8,128)(2,1)} collective-permute-done((bf16[48,1024]{0,1:T(8,128)(2,1)S(1)}, bf16[48,1024]{0,1:T(8,128)(2,1)}, u32[]{:S(2)}, u32[]{:S(2)}) %collective-permute-start.46) | collective-permute-done | bytes 98336 | tf_op jit(solution)/shard_map/ppermute | solution.py:35
  605.3 12.4 %collective-permute-done.45 = bf16[48,1024]{0,1:T(8,128)(2,1)} collective-permute-done((bf16[48,1024]{0,1:T(8,128)(2,1)}, bf16[48,1024]{0,1:T(8,128)(2,1)}, u32[]{:S(2)}, u32[]{:S(2)}) %collective-permute-start.45) | collective-permute-done | bytes 98336 | tf_op jit(solution)/shard_map/ppermute | solution.py:35
  647.8 8.1 %collective-permute-done.52 = bf16[3,192,512]{2,1,0:T(8,128)(2,1)} collective-permute-done((bf16[3,192,512]{2,1,0:T(8,128)(2,1)}, bf16[3,192,512]{2,1,0:T(8,128)(2,1)}, u32[]{:S(2)}, u32[]{:S(2)}) %collective-permute-start.52) | collective-permute-done | bytes 589856 | tf_op jit(solution)/shard_map/ppermute | solution.py:30
  (406 shorter events, 255.9 us)
Async XLA Ops:
  7.2 107.4 %all-gather.4.cloned.1.call-start = ((), (), s32[]{:S(2)}) async-start(), calls=%async_computation.5 | async-start | bytes 5898240 | tf_op jit(solution)/shard_map/all_gather | solution.py:621
  33.6 97.6 %all-gather.6.cloned.1.call-start = ((), (), s32[]{:S(2)}) async-start(), calls=%async_computation.9 | async-start | bytes 5898240 | tf_op jit(solution)/shard_map/all_gather | solution.py:622
  69.3 67.9 %collective-permute-start.14 = (bf16[256,1536]{1,0:T(8,128)(2,1)}, bf16[256,1536]{1,0:T(8,128)(2,1)}, u32[]{:S(2)}, u32[]{:S(2)}) collective-permute-start(bf16[256,1536]{1,0:T(8,128)(2,1)} %bitcast.17.refs_5_), channel_id=1, source_target_pairs={{0,1},{1,0},{2,3},{3,2},{4,5},{5,4},{6,7},{7,6},{8,9},{9,8},{10,11... | collective-permute-start | bytes 2359304 | tf_op jit(solution)/shard_map/ppermute | solution.py:30
  90.4 46.9 %collective-permute-start.15 = (bf16[256,1536]{1,0:T(8,128)(2,1)}, bf16[256,1536]{1,0:T(8,128)(2,1)}, u32[]{:S(2)}, u32[]{:S(2)}) collective-permute-start(bf16[256,1536]{1,0:T(8,128)(2,1)} %collective-permute-done.13.refs_6_), channel_id=1, source_target_pairs={{0,1},{1,0},{2,3},{3,2},{4,5},{5,4},{6,7},{7,6},{8,9},{9,8},{10,11... | collective-permute-start | bytes 2359304 | tf_op jit(solution)/shard_map/ppermute | solution.py:30
  90.4 47.1 %all-to-all-start = ((bf16[4,384,768]{2,1,0:T(8,128)(2,1)}), bf16[4,384,768]{2,1,0:T(8,128)(2,1)}, u32[]{:S(2)}, u32[]{:S(2)}) async-start(bf16[4,384,768]{2,1,0:T(8,128)(2,1)} %maximum_bitcast_fusion), calls=%async_computation | async-start | bytes 4718592 | tf_op jit(solution)/shard_map/all_to_all | solution.py:648
  96.4 215.5 %reduce-scatter.4.cloned.1.call-start = ((), (), s32[]{:S(2)}) async-start(), calls=%async_computation.6 | async-start | bytes 5898240 | tf_op jit(solution)/shard_map/reduce_scatter | solution.py:103
  206.0 192.4 %reduce-scatter.6.cloned.1.call-start = ((), (), s32[]{:S(2)}) async-start(), calls=%async_computation.7 | async-start | bytes 2949120 | tf_op jit(solution)/shard_map/reduce_scatter | solution.py:103
  206.1 63.4 %collective-permute-start.19 = (bf16[4,3,192,512]{3,2,1,0:T(8,128)(2,1)}, bf16[4,3,192,512]{3,2,1,0:T(8,128)(2,1)}, u32[]{:S(2)}, u32[]{:S(2)}) collective-permute-start(bf16[4,3,192,512]{3,2,1,0:T(8,128)(2,1)} %get-tuple-element.78), channel_id=1, source_target_pairs={{0,4},{4,0},{8,12},{12,8},{16,20},{20,16},{24,28},{28,24},{1,5},{5... | collective-permute-start | bytes 7077896 | tf_op jit(solution)/shard_map/ppermute | solution.py:30
  209.0 60.5 %collective-permute-start.20 = (bf16[256,1536]{1,0:T(8,128)(2,1)S(1)}, bf16[256,1536]{1,0:T(8,128)(2,1)S(1)}, u32[]{:S(2)}, u32[]{:S(2)}) collective-permute-start(bf16[256,1536]{1,0:T(8,128)(2,1)S(1)} %get-tuple-element.79), channel_id=1, source_target_pairs={{0,2},{1,3},{2,0},{3,1},{4,6},{5,7},{6,4},{7,5},{8,10},{9,11},{10,... | collective-permute-start | bytes 2359304 | tf_op jit(solution)/shard_map/ppermute | solution.py:30
  287.0 103.9 %collective-permute-start.29 = (bf16[4,2,3,192,512]{4,3,2,1,0:T(8,128)(2,1)}, bf16[4,2,3,192,512]{4,3,2,1,0:T(8,128)(2,1)}, u32[]{:S(2)}, u32[]{:S(2)}) collective-permute-start(bf16[4,2,3,192,512]{4,3,2,1,0:T(8,128)(2,1)} %get-tuple-element.91), channel_id=1, source_target_pairs={{0,4},{4,0},{8,12},{12,8},{16,20},{20,16},{24,28},{28,24},{1,5},{5... | collective-permute-start | bytes 14155784 | tf_op jit(solution)/shard_map/ppermute | solution.py:30
  318.2 319.2 %reduce-scatter.8.cloned.1.call-start = ((), (), s32[]{:S(2)}) async-start(), calls=%async_computation.8 | async-start | bytes 5898240 | tf_op jit(solution)/shard_map/reduce_scatter | solution.py:103
  341.3 49.6 %collective-permute-start.33 = (bf16[512,1536]{1,0:T(8,128)(2,1)}, bf16[512,1536]{1,0:T(8,128)(2,1)}, u32[]{:S(2)}, u32[]{:S(2)}) collective-permute-start(bf16[512,1536]{1,0:T(8,128)(2,1)} %pad_maximum_fusion.4), channel_id=1, source_target_pairs={{0,1},{1,0},{2,3},{3,2},{4,5},{5,4},{6,7},{7,6},{8,9},{9,8},{10,11... | collective-permute-start | bytes 4718600 | tf_op jit(solution)/shard_map/ppermute | solution.py:30
  355.7 35.2 %collective-permute-start.26 = (bf16[512,1536]{1,0:T(8,128)(2,1)}, bf16[512,1536]{1,0:T(8,128)(2,1)}, u32[]{:S(2)}, u32[]{:S(2)}) collective-permute-start(bf16[512,1536]{1,0:T(8,128)(2,1)} %pad_maximum_fusion.3), channel_id=1, source_target_pairs={{0,1},{1,0},{2,3},{3,2},{4,5},{5,4},{6,7},{7,6},{8,9},{9,8},{10,11... | collective-permute-start | bytes 4718600 | tf_op jit(solution)/shard_map/ppermute | solution.py:30
  390.9 46.8 %collective-permute-start.34 = (bf16[4,256,1024]{2,1,0:T(8,128)(2,1)}, bf16[4,256,1024]{2,1,0:T(8,128)(2,1)}, u32[]{:S(2)}, u32[]{:S(2)}) collective-permute-start(bf16[4,256,1024]{2,1,0:T(8,128)(2,1)} %bitcast.23), channel_id=1, source_target_pairs={{0,4},{4,0},{8,12},{12,8},{16,20},{20,16},{24,28},{28,24},{1,5},{5... | collective-permute-start | bytes 6291464 | tf_op jit(solution)/shard_map/ppermute | solution.py:30
  395.1 49.8 %collective-permute-start.27 = (bf16[512,1536]{1,0:T(8,128)(2,1)}, bf16[512,1536]{1,0:T(8,128)(2,1)}, u32[]{:S(2)}, u32[]{:S(2)}) collective-permute-start(bf16[512,1536]{1,0:T(8,128)(2,1)} %get-tuple-element.88), channel_id=1, source_target_pairs={{0,1},{1,0},{2,3},{3,2},{4,5},{5,4},{6,7},{7,6},{8,9},{9,8},{10,11... | collective-permute-start | bytes 4718600 | tf_op jit(solution)/shard_map/ppermute | solution.py:30
  444.4 45.0 %collective-permute-start.36 = (bf16[4,48,3200]{2,1,0:T(8,128)(2,1)}, bf16[4,48,3200]{2,1,0:T(8,128)(2,1)}, u32[]{:S(2)}, u32[]{:S(2)}) collective-permute-start(bf16[4,48,3200]{2,1,0:T(8,128)(2,1)} %dynamic-slice_bitcast_fusion), channel_id=1, source_target_pairs={{0,4},{4,0},{8,12},{12,8},{16,20},{20,16},{24,28},{28,24},{1,5},{5... | collective-permute-start | bytes 3686408 | tf_op jit(solution)/shard_map/ppermute | solution.py:30
  449.8 39.6 %collective-permute-start.35 = (bf16[256,1024]{1,0:T(8,128)(2,1)}, bf16[256,1024]{1,0:T(8,128)(2,1)}, u32[]{:S(2)}, u32[]{:S(2)}) collective-permute-start(bf16[256,1024]{1,0:T(8,128)(2,1)} %get-tuple-element.236), channel_id=1, source_target_pairs={{0,24},{4,28},{8,0},{12,4},{16,8},{20,12},{24,16},{28,20},{1,25},{... | collective-permute-start | bytes 1572872 | tf_op jit(solution)/shard_map/ppermute | solution.py:35
  452.1 57.4 %collective-permute-start.38 = (bf16[256,1024]{1,0:T(8,128)(2,1)}, bf16[256,1024]{1,0:T(8,128)(2,1)}, u32[]{:S(2)}, u32[]{:S(2)}) collective-permute-start(bf16[256,1024]{1,0:T(8,128)(2,1)} %get-tuple-element.237), channel_id=1, source_target_pairs={{0,8},{4,12},{8,16},{12,20},{16,24},{20,28},{24,0},{28,4},{1,9},{5... | collective-permute-start | bytes 1572872 | tf_op jit(solution)/shard_map/ppermute | solution.py:35
  452.3 91.6 %collective-permute-start.37 = (bf16[256,1024]{1,0:T(8,128)(2,1)}, bf16[256,1024]{1,0:T(8,128)(2,1)}, u32[]{:S(2)}, u32[]{:S(2)}) collective-permute-start(bf16[256,1024]{1,0:T(8,128)(2,1)} %get-tuple-element.238), channel_id=1, source_target_pairs={{0,16},{4,20},{8,24},{12,28},{16,0},{20,4},{24,8},{28,12},{1,17},{... | collective-permute-start | bytes 1572872 | tf_op jit(solution)/shard_map/ppermute | solution.py:35
  467.2 120.4 %collective-permute-start.48 = (bf16[4,3,192,256]{3,2,1,0:T(8,128)(2,1)}, bf16[4,3,192,256]{3,2,1,0:T(8,128)(2,1)}, u32[]{:S(2)}, u32[]{:S(2)}) collective-permute-start(bf16[4,3,192,256]{3,2,1,0:T(8,128)(2,1)} %get-tuple-element.105), channel_id=1, source_target_pairs={{0,4},{4,0},{8,12},{12,8},{16,20},{20,16},{24,28},{28,24},{1,5},{5... | collective-permute-start | bytes 3538952 | tf_op jit(solution)/shard_map/ppermute | solution.py:30
  582.8 34.9 %collective-permute-start.45 = (bf16[48,1024]{0,1:T(8,128)(2,1)}, bf16[48,1024]{0,1:T(8,128)(2,1)}, u32[]{:S(2)}, u32[]{:S(2)}) collective-permute-start(bf16[48,1024]{0,1:T(8,128)(2,1)} %bitcast.60), channel_id=1, source_target_pairs={{0,24},{4,28},{8,0},{12,4},{16,8},{20,12},{24,16},{28,20},{1,25},{... | collective-permute-start | bytes 294920 | tf_op jit(solution)/shard_map/ppermute | solution.py:35
  590.7 33.0 %collective-permute-start.51 = (bf16[3,192,256]{2,1,0:T(8,128)(2,1)}, bf16[3,192,256]{2,1,0:T(8,128)(2,1)}, u32[]{:S(2)}, u32[]{:S(2)}) collective-permute-start(bf16[3,192,256]{2,1,0:T(8,128)(2,1)} %get-tuple-element.257), channel_id=1, source_target_pairs={{0,8},{4,12},{8,16},{12,20},{16,24},{20,28},{24,0},{28,4},{1,9},{5... | collective-permute-start | bytes 884744 | tf_op jit(solution)/shard_map/ppermute | solution.py:35
  591.5 37.2 %collective-permute-start.50 = (bf16[3,192,256]{2,1,0:T(8,128)(2,1)}, bf16[3,192,256]{2,1,0:T(8,128)(2,1)}, u32[]{:S(2)}, u32[]{:S(2)}) collective-permute-start(bf16[3,192,256]{2,1,0:T(8,128)(2,1)} %get-tuple-element.258), channel_id=1, source_target_pairs={{0,16},{4,20},{8,24},{12,28},{16,0},{20,4},{24,8},{28,12},{1,17},{... | collective-permute-start | bytes 884744 | tf_op jit(solution)/shard_map/ppermute | solution.py:35
  597.3 32.9 %collective-permute-start.49 = (bf16[3,192,256]{2,1,0:T(8,128)(2,1)}, bf16[3,192,256]{2,1,0:T(8,128)(2,1)}, u32[]{:S(2)}, u32[]{:S(2)}) collective-permute-start(bf16[3,192,256]{2,1,0:T(8,128)(2,1)} %get-tuple-element.256), channel_id=1, source_target_pairs={{0,24},{4,28},{8,0},{12,4},{16,8},{20,12},{24,16},{28,20},{1,25},{... | collective-permute-start | bytes 884744 | tf_op jit(solution)/shard_map/ppermute | solution.py:35
  (113 other events, 1075.6 us)
Sparse Core Ops, SparseCore 0:
  33.7 38.6 all-gather.3
  74.0 53.9 all-gather.5
  206.2 91.3 reduce-scatter.3
  318.4 51.4 reduce-scatter.5
  408.1 138.9 reduce-scatter.7

commit v6 on v5

--- a/solution.py
+++ b/solution.py
@@ -358,8 +358,8 @@
     if final:
         shared_ref, out_in, dx_in, dg_in, *refs = refs
         out_hbm, dx_hbm, out_low_ref, dx_low_ref, dg_ref, *refs = refs
-        targets = tuple((refs[0].at[:, number], refs[1].at[:, number]) for number in range(2))
-        pair_target, refs = (refs[2], refs[3]), refs[4:]
+        targets = ((refs[0], refs[1]), (refs[2], refs[3]))
+        pair_target, refs = (refs[4], refs[5]), refs[6:]
         x_ref, dy_ref, he_ref, da_ref, db_ref, out_ref, dx_ref, sem = refs
     else:
         out_hbm, dx_hbm, dg_ref, line_hbm, *refs = refs
@@ -544,7 +544,7 @@
         shared = shared_w.shape[1] // 3
         pair = jax.ShapeDtypeStruct((lines, 3, per, shared), jnp.bfloat16)
         extra_specs = [whole(shared_w.shape)] + [apart] * 3
-        out_shape = (part, part, low, low, table, both, both, pair, pair)
+        out_shape = (part, part, low, low, table, term, term, term, term, pair, pair)
         outside = (0, 1)
     else:
         shared = 0
@@ -672,11 +672,11 @@
     other_one = flip(send_one, "ctx", 1)
     (
         out_keep, dx_keep, out_send, dx_send, gate_back,
-        keep_both, send_both, pair_keep, pair_send,
+        keep_two, send_two, keep_three, send_three, pair_keep, pair_send,
     ) = experts_call(
         at(2), second_pieces, grad_pieces, gates_all, weights, 2, contexts, shared_w, carried
     )
-    other_both = flip(send_both, "ctx", 1)
+    other_two = flip(send_two, "ctx", 1)
 
     def nothing(arrived):
         return 0.0 * arrived[(0,) * arrived.ndim].astype(jnp.float32)
@@ -686,7 +686,8 @@
 
     dx_near = dx_keep + flip(after(dx_send, other_one, attended_across), "wa", 1).astype(jnp.float32)
     dx_moved = flip(dx_near[rows:].astype(jnp.bfloat16), "wa", 2)
-    dx_own = dx_near[:rows] + dx_moved.astype(jnp.float32)
+    other_three = flip(after(send_three, dx_moved), "ctx", 1)
+    dx_own = dx_near[:rows] + after(dx_moved, other_two).astype(jnp.float32)
     half = 2 * rows
     gate_back = reduce_rows(gate_back[:half], gate_back[half:], jnp.float32)
 
@@ -720,15 +721,18 @@
     attended_core = flip(after(jnp.concatenate([attended, attended_across], axis=0), query_low), "wa", 1)
     query_core = flip(jnp.concatenate([query_low, query_across], axis=0), "wa", 1)
     moved = bundle[1:] + [attended_core, query_core]
-    kv_send = after(by_line(kv_send), other_both, *moved)
+    near_two = (side_sum(keep_two, after(other_two, query_low)) + nothing(sum_one)).astype(jnp.bfloat16)
+    sum_two = scatter_lines(near_two)
+    kv_send = after(by_line(kv_send), other_three, near_two, *moved)
     received = flip(kv_send, "ctx", 1)
     out_near = out_keep + flip(after(out_send, query_core), "wa", 1).astype(jnp.float32)
     out_moved = flip(out_near[rows:].astype(jnp.bfloat16), "wa", 2)
     out_own = out_near[:rows] + out_moved.astype(jnp.float32)
     block_out = (residual + out_own).astype(jnp.bfloat16).reshape(tokens.shape)
-    near_both = (side_sum(keep_both, other_both) + nothing(sum_one)).astype(jnp.bfloat16)
-    sum_both = scatter_lines(near_both)
-    received = after(received, near_both)
+    near_three = side_sum(keep_three, other_three) + 0.0 * near_two[0, 0, 0, 0].astype(jnp.float32)
+    near_three = near_three.astype(jnp.bfloat16)
+    sum_three = scatter_lines(near_three)
+    received = after(received, near_three)
     kv_near = by_line(kv_keep).astype(jnp.float32) + received.astype(jnp.float32)
     kv_parts = kv_near.astype(jnp.bfloat16)
     kv_moved = [shift(kv_parts[steps], -steps) for steps in range(1, lines)]
@@ -776,9 +780,9 @@
         + jnp.sum(mine(kv_full).astype(jnp.float32) * kv_sum, axis=1)
     ) / mine(gain_one)
 
-    line_zero = flip((line_sums[1].astype(jnp.float32) + nothing(sum_both)).astype(jnp.bfloat16), "ctx", 1)
+    line_zero = flip((line_sums[1].astype(jnp.float32) + nothing(sum_three)).astype(jnp.bfloat16), "ctx", 1)
     sum_zero = line_sums[0].astype(jnp.float32) + line_zero.astype(jnp.float32)
-    expert_sums = [sum_zero, sum_one, sum_both[0], sum_both[1]]
+    expert_sums = [sum_zero, sum_one, sum_two, sum_three]
     expert_gate_grad = jnp.stack([total[0] for total in expert_sums]).astype(jnp.float32)
     expert_up_grad = jnp.stack([total[1] for total in expert_sums]).astype(jnp.float32)
     expert_down_grad = jnp.stack([total[2].T for total in expert_sums]).astype(jnp.float32)

time: 676 us -> 675 us (level)
  starting transfers between devices: 84.1 us -> 62.9 us
  local copies, waits for them, and re-layouts: 56.4 us -> 67.1 us
    ppermute x15, waiting for transfers between devices: 124 us -> 98.9 us  [shift(): lax.ppermute(value, 'ctx', [(i, (i + 2 * steps) % count) for i in range(c...]
    ppermute x38 -> x39, waiting for transfers between devices: 153 us -> 174 us  [flip(): return lax.ppermute(value, axis, [(i, i ^ bits) for i in range(count)])]
    ppermute x15, starting transfers between devices: 31.3 us -> 19.7 us  [shift(): lax.ppermute(value, 'ctx', [(i, (i + 2 * steps) % count) for i in range(c...]
    ppermute x38 -> x39, starting transfers between devices: 41.3 us -> 32.6 us  [flip(): return lax.ppermute(value, axis, [(i, i ^ bits) for i in range(count)])]
    unnamed x168 -> x196, local copies, waits for them, and re-layouts: 20.7 us -> 22.8 us
  transfers between devices with their start and end apart: 60 -> 62, of which waited for: 33 -> 28; matrix products, arithmetic and copies ran while one was open for 21% -> 23% of each run, Pallas kernels for 13% -> 14%
where the time goes in v6:
time: 675 us; the launch traced here: 668 us
  waiting for transfers between devices  279 us (41%)
  Pallas kernels  134 us (20%)
  other arithmetic  72.6 us (11%)
  local copies, waits for them, and re-layouts  67.1 us (10%)
  starting transfers between devices  62.9 us (9%)
  matrix products  34.2 us (5%)
  between operations  18.2 us (3%)
    ppermute x39, waiting for transfers between devices, flip(): return lax.ppermute(value, axis, [(i, i ^ bits) for i in range(count)])  174 us
    pallas_call x2, Pallas kernels, experts_call(): pl.pallas_call(functools.partial(experts_kernel, final), grid_spec=pltpu....  102 us
    ppermute x15, waiting for transfers between devices, shift(): lax.ppermute(value, 'ctx', [(i, (i + 2 * steps) % count) for i in range(c...  98.9 us
    ppermute x39, starting transfers between devices, flip(): return lax.ppermute(value, axis, [(i, i ^ bits) for i in range(count)])  32.6 us
    unnamed x196, local copies, waits for them, and re-layouts  22.8 us
    ppermute x15, starting transfers between devices, shift(): lax.ppermute(value, 'ctx', [(i, (i + 2 * steps) % count) for i in range(c...  19.7 us
    pallas_call x1, Pallas kernels, attention_backward(): pl.pallas_call(attention_backward_kernel, grid_spec=pltpu.PrefetchScalarG...  18.2 us
    dot_general x9, matrix products, dot32(): lax.dot_general(left, right, (dims, ((), ())), preferred_element_type=jnp...  15.6 us
  transfers between devices with their start and end apart: 62, of which 28 were waited for; matrix products, arithmetic and copies ran while one was open for 23% of the time, Pallas kernels for 14%

profile of v6, /device:TPU:10, one launch (start us, length us, event | category | flops | bytes accessed | tf_op | source)
XLA Modules:
  0.0 668.5 jit_solution(9987758169417268503)
XLA Ops:
  12.7 20.9 %collective-permute-done.1 = bf16[384,1152]{0,1:T(8,128)(2,1)S(1)} collective-permute-done((bf16[384,1152]{0,1:T(8,128)(2,1)S(1)}, bf16[384,1152]{0,1:T(8,128)(2,1)S(1)}, u32[]{:S(2)}, u32[]{:S(2)}) %collective-permute-start.1) | collective-permute-done | bytes 884768 | tf_op jit(solution)/shard_map/ppermute | solution.py:30
  49.2 10.4 %collective-permute-done.3 = bf16[2,128,1024]{2,1,0:T(8,128)(2,1)} collective-permute-done((bf16[2,128,1024]{2,1,0:T(8,128)(2,1)}, bf16[2,128,1024]{2,1,0:T(8,128)(2,1)}, u32[]{:S(2)}, u32[]{:S(2)}) %collective-permute-start.3) | collective-permute-done | bytes 524320 | tf_op jit(solution)/shard_map/ppermute | solution.py:35
  78.4 8.6 %collective-permute-done.4 = s32[256,6]{0,1:T(8,128)S(1)} collective-permute-done((s32[256,6]{0,1:T(8,128)}, s32[256,6]{0,1:T(8,128)S(1)}, u32[]{:S(2)}, u32[]{:S(2)}) %collective-permute-start.4) | collective-permute-done | bytes 6176 | tf_op jit(solution)/shard_map/ppermute | solution.py:30
  90.5 5.9 all-to-all-start
  103.8 8.9 %collective-permute-done.12 = bf16[2,128,1024]{2,1,0:T(8,128)(2,1)} collective-permute-done((bf16[2,128,1024]{2,1,0:T(8,128)(2,1)}, bf16[2,128,1024]{2,1,0:T(8,128)(2,1)}, u32[]{:S(2)}, u32[]{:S(2)}) %collective-permute-start.12) | collective-permute-done | bytes 524320 | tf_op jit(solution)/shard_map/ppermute | solution.py:30
  118.3 14.4 %attention_forward.1 = (bf16[256,1536]{1,0:T(8,128)(2,1)S(1)}, f32[4,2,384,128]{3,2,1,0:T(8,128)S(1)}) custom-call(s32[8]{0:T(128)S(1)} %bitcast.314, s32[1]{0:T(128)} %bitcast.2.own_ref, bf16[256,1536]{1,0:T(8,128)(2,1)S(1)} %convolution_convert_fusion.q_ref, bf16[16,128,1024]{2,1,0:T(8,128)(2,1)} %constant_dynamic-update-slice_fusion.4.kv_ref), custom_call_target="tpu_custom_call" | custom-call | bytes 1048576 | tf_op jit(solution)/shard_map/attention_forward/pallas_call | solution.py:224
  145.5 16.1 %collective-permute-done.16.refs_2_ = bf16[256,1536]{1,0:T(8,128)(2,1)} collective-permute-done((bf16[256,1536]{1,0:T(8,128)(2,1)S(1)}, bf16[256,1536]{1,0:T(8,128)(2,1)}, u32[]{:S(2)}, u32[]{:S(2)}) %collective-permute-start.16) | collective-permute-done | bytes 786464 | tf_op jit(solution)/shard_map/ppermute | solution.py:30
  167.0 42.4 %experts.1 = (f32[1024,1536]{1,0:T(8,128)}, f32[1024,1536]{1,0:T(8,128)}, f32[1024,16]{1,0:T(8,128)}, bf16[4,2,3,192,512]{4,3,2,1,0:T(8,128)(2,1)}, bf16[4,3,192...) custom-call(s32[2]{0:T(128)} %pad_add_fusion.1.refs_0_, bf16[256,1536]{1,0:T(8,128)(2,1)} %copy-done.4, ...), custom_call_target="tpu_custom_call" | custom-call | bytes 1048576 | tf_op jit(solution)/shard_map/experts/pallas_call | solution.py:555
  211.9 59.4 %experts_final.1 = (f32[512,1536]{1,0:T(8,128)}, f32[512,1536]{1,0:T(8,128)}, bf16[512,1536]{1,0:T(8,128)(2,1)}, bf16[512,1536]{1,0:T(8,128)(2,1)}, f32[1024,16]...) custom-call(s32[2]{0:T(128)} %pad_add_fusion.refs_0_, ...), custom_call_target="tpu_custom_call" | custom-call | bytes 1048576 | tf_op jit(solution)/shard_map/experts_final/pallas_call | solution.py:555
  280.5 18.6 %collective-permute-done.22 = bf16[256,1536]{1,0:T(8,128)(2,1)} collective-permute-done((bf16[256,1536]{1,0:T(8,128)(2,1)S(1)}, bf16[256,1536]{1,0:T(8,128)(2,1)}, u32[]{:S(2)}, u32[]{:S(2)}) %collective-permute-start.22) | collective-permute-done | bytes 786464 | tf_op jit(solution)/shard_map/ppermute | solution.py:30
  314.7 10.8 %collective-permute-done.23 = bf16[4,3,192,512]{3,2,1,0:T(8,128)(2,1)} collective-permute-done((bf16[4,3,192,512]{3,2,1,0:T(8,128)(2,1)}, bf16[4,3,192,512]{3,2,1,0:T(8,128)(2,1)}, u32[]{:S(2)}, u32[]{:S(2)}) %collective-permute-start.23) | collective-permute-done | bytes 2359328 | tf_op jit(solution)/shard_map/ppermute | solution.py:30
  338.1 18.2 %attention_backward.1 = (bf16[256,1536]{1,0:T(8,128)(2,1)}, bf16[8,128,1024]{2,1,0:T(8,128)(2,1)}, bf16[8,128,1024]{2,1,0:T(8,128)(2,1)}) custom-call(s32[8]{0:T(128)} %bitcast.313, s32[1]{0:T(128)} %bitcast.2.own_ref, bf16[256,1536]{1,0:T(8,128)(2,1)} %copy-done, bf16[256,1536]{1,0:T(8,128)(2,1)} %fusion.19.do_ref, ...), custom_call_target="tpu_custom_call" | custom-call | bytes 1048576 | tf_op jit(solution)/shard_map/attention_backward/pallas_call | solution.py:324
  364.2 13.2 %collective-permute-done.26 = bf16[256,1536]{1,0:T(8,128)(2,1)} collective-permute-done((bf16[256,1536]{1,0:T(8,128)(2,1)}, bf16[256,1536]{1,0:T(8,128)(2,1)}, u32[]{:S(2)}, u32[]{:S(2)}) %collective-permute-start.26) | collective-permute-done | bytes 786464 | tf_op jit(solution)/shard_map/ppermute | solution.py:30
  397.8 8.7 %collective-permute-done.33 = bf16[640,384]{0,1:T(8,128)(2,1)} collective-permute-done((bf16[640,384]{0,1:T(8,128)(2,1)}, bf16[640,384]{0,1:T(8,128)(2,1)}, u32[]{:S(2)}, u32[]{:S(2)}) %collective-permute-start.33) | collective-permute-done | bytes 491552 | tf_op jit(solution)/shard_map/ppermute | solution.py:30
  417.8 37.0 %collective-permute-done.35 = bf16[4,256,1024]{2,1,0:T(8,128)(2,1)S(1)} collective-permute-done((bf16[4,256,1024]{2,1,0:T(8,128)(2,1)}, bf16[4,256,1024]{2,1,0:T(8,128)(2,1)S(1)}, u32[]{:S(2)}, u32[]{:S(2)}) %collective-permute-start.35) | collective-permute-done | bytes 2097184 | tf_op jit(solution)/shard_map/ppermute | solution.py:30
  469.8 10.6 %collective-permute-done.29 = bf16[256,1536]{1,0:T(8,128)(2,1)} collective-permute-done((bf16[256,1536]{1,0:T(8,128)(2,1)}, bf16[256,1536]{1,0:T(8,128)(2,1)}, u32[]{:S(2)}, u32[]{:S(2)}) %collective-permute-start.29) | collective-permute-done | bytes 786464 | tf_op jit(solution)/shard_map/ppermute | solution.py:30
  482.0 20.0 %collective-permute-done.36 = bf16[256,1024]{1,0:T(8,128)(2,1)} collective-permute-done((bf16[256,1024]{1,0:T(8,128)(2,1)}, bf16[256,1024]{1,0:T(8,128)(2,1)}, u32[]{:S(2)}, u32[]{:S(2)}) %collective-permute-start.36) | collective-permute-done | bytes 524320 | tf_op jit(solution)/shard_map/ppermute | solution.py:35
  502.0 4.7 collective-permute-done.39
  506.7 40.7 %collective-permute-done.38 = bf16[256,1024]{1,0:T(8,128)(2,1)} collective-permute-done((bf16[256,1024]{1,0:T(8,128)(2,1)}, bf16[256,1024]{1,0:T(8,128)(2,1)}, u32[]{:S(2)}, u32[]{:S(2)}) %collective-permute-start.38) | collective-permute-done | bytes 524320 | tf_op jit(solution)/shard_map/ppermute | solution.py:35
  557.4 5.9 collective-permute-done.41
  584.2 6.9 %collective-permute-done.43 = bf16[4,48,1024]{2,1,0:T(8,128)(2,1)S(1)} collective-permute-done((bf16[4,48,1024]{2,1,0:T(8,128)(2,1)S(1)}, bf16[4,48,1024]{2,1,0:T(8,128)(2,1)S(1)}, u32[]{:S(2)}, u32[]{:S(2)}) %collective-permute-start.43) | collective-permute-done | bytes 393248 | tf_op jit(solution)/shard_map/ppermute | solution.py:30
  625.5 6.9 %collective-permute-done.46 = bf16[48,1024]{0,1:T(8,128)(2,1)} collective-permute-done((bf16[48,1024]{0,1:T(8,128)(2,1)}, bf16[48,1024]{0,1:T(8,128)(2,1)}, u32[]{:S(2)}, u32[]{:S(2)}) %collective-permute-start.46) | collective-permute-done | bytes 98336 | tf_op jit(solution)/shard_map/ppermute | solution.py:35
  639.5 5.8 collective-permute-done.51
  653.9 5.3 all-to-all-done.1
  (443 shorter events, 250.1 us)
Async XLA Ops:
  7.2 107.4 %all-gather.4.cloned.1.call-start = ((), (), s32[]{:S(2)}) async-start(), calls=%async_computation.6 | async-start | bytes 5898240 | tf_op jit(solution)/shard_map/all_gather | solution.py:621
  33.6 100.3 %all-gather.6.cloned.1.call-start = ((), (), s32[]{:S(2)}) async-start(), calls=%async_computation.11 | async-start | bytes 5898240 | tf_op jit(solution)/shard_map/all_gather | solution.py:622
  69.4 70.6 %collective-permute-start.14 = (bf16[256,1536]{1,0:T(8,128)(2,1)}, bf16[256,1536]{1,0:T(8,128)(2,1)}, u32[]{:S(2)}, u32[]{:S(2)}) collective-permute-start(bf16[256,1536]{1,0:T(8,128)(2,1)} %bitcast.17.refs_5_), channel_id=1, source_target_pairs={{0,1},{1,0},{2,3},{3,2},{4,5},{5,4},{6,7},{7,6},{8,9},{9,8},{10,11... | collective-permute-start | bytes 2359304 | tf_op jit(solution)/shard_map/ppermute | solution.py:30
  90.5 49.5 %collective-permute-start.15 = (bf16[256,1536]{1,0:T(8,128)(2,1)}, bf16[256,1536]{1,0:T(8,128)(2,1)}, u32[]{:S(2)}, u32[]{:S(2)}) collective-permute-start(bf16[256,1536]{1,0:T(8,128)(2,1)} %collective-permute-done.13.refs_6_), channel_id=1, source_target_pairs={{0,1},{1,0},{2,3},{3,2},{4,5},{5,4},{6,7},{7,6},{8,9},{9,8},{10,11... | collective-permute-start | bytes 2359304 | tf_op jit(solution)/shard_map/ppermute | solution.py:30
  90.5 49.5 %all-to-all-start = ((bf16[4,384,768]{2,1,0:T(8,128)(2,1)}), bf16[4,384,768]{2,1,0:T(8,128)(2,1)}, u32[]{:S(2)}, u32[]{:S(2)}) async-start(bf16[4,384,768]{2,1,0:T(8,128)(2,1)} %maximum_bitcast_fusion), calls=%async_computation | async-start | bytes 4718592 | tf_op jit(solution)/shard_map/all_to_all | solution.py:648
  96.4 202.6 %reduce-scatter.5.cloned.1.call-start = ((), (), s32[]{:S(2)}) async-start(), calls=%async_computation.7 | async-start | bytes 5898240 | tf_op jit(solution)/shard_map/reduce_scatter | solution.py:103
  209.4 175.1 %reduce-scatter.7.cloned.1.call-start = ((), (), s32[]{:S(2)}) async-start(), calls=%async_computation.8 | async-start | bytes 2949120 | tf_op jit(solution)/shard_map/reduce_scatter | solution.py:103
  209.4 61.9 %collective-permute-start.19 = (bf16[4,3,192,512]{3,2,1,0:T(8,128)(2,1)}, bf16[4,3,192,512]{3,2,1,0:T(8,128)(2,1)}, u32[]{:S(2)}, u32[]{:S(2)}) collective-permute-start(bf16[4,3,192,512]{3,2,1,0:T(8,128)(2,1)} %get-tuple-element.83), channel_id=1, source_target_pairs={{0,4},{4,0},{8,12},{12,8},{16,20},{20,16},{24,28},{28,24},{1,5},{5... | collective-permute-start | bytes 7077896 | tf_op jit(solution)/shard_map/ppermute | solution.py:30
  209.7 61.6 %collective-permute-start.20 = (bf16[256,1536]{1,0:T(8,128)(2,1)S(1)}, bf16[256,1536]{1,0:T(8,128)(2,1)S(1)}, u32[]{:S(2)}, u32[]{:S(2)}) collective-permute-start(bf16[256,1536]{1,0:T(8,128)(2,1)S(1)} %get-tuple-element.84), channel_id=1, source_target_pairs={{0,2},{1,3},{2,0},{3,1},{4,6},{5,7},{6,4},{7,5},{8,10},{9,11},{10,... | collective-permute-start | bytes 2359304 | tf_op jit(solution)/shard_map/ppermute | solution.py:30
  271.6 53.9 %collective-permute-start.23 = (bf16[4,3,192,512]{3,2,1,0:T(8,128)(2,1)}, bf16[4,3,192,512]{3,2,1,0:T(8,128)(2,1)}, u32[]{:S(2)}, u32[]{:S(2)}) collective-permute-start(bf16[4,3,192,512]{3,2,1,0:T(8,128)(2,1)} %get-tuple-element.86), channel_id=1, source_target_pairs={{0,4},{4,0},{8,12},{12,8},{16,20},{20,16},{24,28},{28,24},{1,5},{5... | collective-permute-start | bytes 7077896 | tf_op jit(solution)/shard_map/ppermute | solution.py:30
  305.4 267.0 %reduce-scatter.9.cloned.1.call-start = ((), (), s32[]{:S(2)}) async-start(), calls=%async_computation.9 | async-start | bytes 2949120 | tf_op jit(solution)/shard_map/reduce_scatter | solution.py:103
  325.5 67.1 %collective-permute-start.30 = (bf16[4,3,192,512]{3,2,1,0:T(8,128)(2,1)}, bf16[4,3,192,512]{3,2,1,0:T(8,128)(2,1)}, u32[]{:S(2)}, u32[]{:S(2)}) collective-permute-start(bf16[4,3,192,512]{3,2,1,0:T(8,128)(2,1)} %get-tuple-element.99), channel_id=1, source_target_pairs={{0,4},{4,0},{8,12},{12,8},{16,20},{20,16},{24,28},{28,24},{1,5},{5... | collective-permute-start | bytes 7077896 | tf_op jit(solution)/shard_map/ppermute | solution.py:30
  364.1 42.4 %collective-permute-start.34 = (bf16[512,1536]{1,0:T(8,128)(2,1)}, bf16[512,1536]{1,0:T(8,128)(2,1)}, u32[]{:S(2)}, u32[]{:S(2)}) collective-permute-start(bf16[512,1536]{1,0:T(8,128)(2,1)} %pad_maximum_fusion.4), channel_id=1, source_target_pairs={{0,1},{1,0},{2,3},{3,2},{4,5},{5,4},{6,7},{7,6},{8,9},{9,8},{10,11... | collective-permute-start | bytes 4718600 | tf_op jit(solution)/shard_map/ppermute | solution.py:30
  397.4 183.0 %reduce-scatter.11.cloned.1.call-start = ((), (), s32[]{:S(2)}) async-start(), calls=%async_computation.10 | async-start | bytes 2949120 | tf_op jit(solution)/shard_map/reduce_scatter | solution.py:103
  406.5 48.3 %collective-permute-start.35 = (bf16[4,256,1024]{2,1,0:T(8,128)(2,1)}, bf16[4,256,1024]{2,1,0:T(8,128)(2,1)S(1)}, u32[]{:S(2)}, u32[]{:S(2)}) collective-permute-start(bf16[4,256,1024]{2,1,0:T(8,128)(2,1)} %bitcast.357), channel_id=1, source_target_pairs={{0,4},{4,0},{8,12},{12,8},{16,20},{20,16},{24,28},{28,24},{1,5},{5... | collective-permute-start | bytes 6291464 | tf_op jit(solution)/shard_map/ppermute | solution.py:30
  413.9 45.5 %collective-permute-start.28 = (bf16[512,1536]{1,0:T(8,128)(2,1)S(1)}, bf16[512,1536]{1,0:T(8,128)(2,1)S(1)}, u32[]{:S(2)}, u32[]{:S(2)}) collective-permute-start(bf16[512,1536]{1,0:T(8,128)(2,1)S(1)} %copy-done.85), channel_id=1, source_target_pairs={{0,1},{1,0},{2,3},{3,2},{4,5},{5,4},{6,7},{7,6},{8,9},{9,8},{10,11... | collective-permute-start | bytes 4718600 | tf_op jit(solution)/shard_map/ppermute | solution.py:30
  459.2 42.8 %collective-permute-start.37 = (bf16[4,48,3200]{2,1,0:T(8,128)(2,1)}, bf16[4,48,3200]{2,1,0:T(8,128)(2,1)}, u32[]{:S(2)}, u32[]{:S(2)}) collective-permute-start(bf16[4,48,3200]{2,1,0:T(8,128)(2,1)} %dynamic-slice_bitcast_fusion), channel_id=1, source_target_pairs={{0,4},{4,0},{8,12},{12,8},{16,20},{20,16},{24,28},{28,24},{1,5},{5... | collective-permute-start | bytes 3686408 | tf_op jit(solution)/shard_map/ppermute | solution.py:30
  463.9 38.1 %collective-permute-start.36 = (bf16[256,1024]{1,0:T(8,128)(2,1)}, bf16[256,1024]{1,0:T(8,128)(2,1)}, u32[]{:S(2)}, u32[]{:S(2)}) collective-permute-start(bf16[256,1024]{1,0:T(8,128)(2,1)} %get-tuple-element.246), channel_id=1, source_target_pairs={{0,24},{4,28},{8,0},{12,4},{16,8},{20,12},{24,16},{28,20},{1,25},{... | collective-permute-start | bytes 1572872 | tf_op jit(solution)/shard_map/ppermute | solution.py:35
  465.1 41.5 %collective-permute-start.39 = (bf16[256,1024]{1,0:T(8,128)(2,1)}, bf16[256,1024]{1,0:T(8,128)(2,1)}, u32[]{:S(2)}, u32[]{:S(2)}) collective-permute-start(bf16[256,1024]{1,0:T(8,128)(2,1)} %get-tuple-element.247), channel_id=1, source_target_pairs={{0,8},{4,12},{8,16},{12,20},{16,24},{20,28},{24,0},{28,4},{1,9},{5... | collective-permute-start | bytes 1572872 | tf_op jit(solution)/shard_map/ppermute | solution.py:35
  465.9 81.5 %collective-permute-start.38 = (bf16[256,1024]{1,0:T(8,128)(2,1)}, bf16[256,1024]{1,0:T(8,128)(2,1)}, u32[]{:S(2)}, u32[]{:S(2)}) collective-permute-start(bf16[256,1024]{1,0:T(8,128)(2,1)} %get-tuple-element.248), channel_id=1, source_target_pairs={{0,16},{4,20},{8,24},{12,28},{16,0},{20,4},{24,8},{28,12},{1,17},{... | collective-permute-start | bytes 1572872 | tf_op jit(solution)/shard_map/ppermute | solution.py:35
  480.4 120.0 %collective-permute-start.49 = (bf16[4,3,192,256]{3,2,1,0:T(8,128)(2,1)}, bf16[4,3,192,256]{3,2,1,0:T(8,128)(2,1)}, u32[]{:S(2)}, u32[]{:S(2)}) collective-permute-start(bf16[4,3,192,256]{3,2,1,0:T(8,128)(2,1)} %get-tuple-element.115), channel_id=1, source_target_pairs={{0,4},{4,0},{8,12},{12,8},{16,20},{20,16},{24,28},{28,24},{1,5},{5... | collective-permute-start | bytes 3538952 | tf_op jit(solution)/shard_map/ppermute | solution.py:30
  582.7 32.6 %collective-permute-start.53 = (bf16[3,192,512]{2,1,0:T(8,128)(2,1)}, bf16[3,192,512]{2,1,0:T(8,128)(2,1)}, u32[]{:S(2)}, u32[]{:S(2)}) collective-permute-start(bf16[3,192,512]{2,1,0:T(8,128)(2,1)} %fusion.69), channel_id=1, source_target_pairs={{0,4},{4,0},{8,12},{12,8},{16,20},{20,16},{24,28},{28,24},{1,5},{5... | collective-permute-start | bytes 1769480 | tf_op jit(solution)/shard_map/ppermute | solution.py:30
  598.4 33.9 %collective-permute-start.46 = (bf16[48,1024]{0,1:T(8,128)(2,1)}, bf16[48,1024]{0,1:T(8,128)(2,1)}, u32[]{:S(2)}, u32[]{:S(2)}) collective-permute-start(bf16[48,1024]{0,1:T(8,128)(2,1)} %bitcast.61), channel_id=1, source_target_pairs={{0,24},{4,28},{8,0},{12,4},{16,8},{20,12},{24,16},{28,20},{1,25},{... | collective-permute-start | bytes 294920 | tf_op jit(solution)/shard_map/ppermute | solution.py:35
  615.3 30.0 %collective-permute-start.51 = (bf16[3,192,256]{2,1,0:T(8,128)(2,1)}, bf16[3,192,256]{2,1,0:T(8,128)(2,1)}, u32[]{:S(2)}, u32[]{:S(2)}) collective-permute-start(bf16[3,192,256]{2,1,0:T(8,128)(2,1)} %get-tuple-element.262), channel_id=1, source_target_pairs={{0,16},{4,20},{8,24},{12,28},{16,0},{20,4},{24,8},{28,12},{1,17},{... | collective-permute-start | bytes 884744 | tf_op jit(solution)/shard_map/ppermute | solution.py:35
  (129 other events, 1345.9 us)
Sparse Core Ops, SparseCore 0:
  33.7 38.5 all-gather.3
  73.9 53.8 all-gather.5
  209.5 84.1 reduce-scatter.4
  305.5 46.2 reduce-scatter.6
  397.6 45.3 reduce-scatter.8
  467.6 82.4 reduce-scatter.10

commit v7 on v6

--- a/solution.py
+++ b/solution.py
@@ -723,13 +723,14 @@
     moved = bundle[1:] + [attended_core, query_core]
     near_two = (side_sum(keep_two, after(other_two, query_low)) + nothing(sum_one)).astype(jnp.bfloat16)
     sum_two = scatter_lines(near_two)
-    kv_send = after(by_line(kv_send), other_three, near_two, *moved)
+    kv_send = after(by_line(kv_send), other_three, *moved)
     received = flip(kv_send, "ctx", 1)
-    out_near = out_keep + flip(after(out_send, query_core), "wa", 1).astype(jnp.float32)
+    out_core = flip(after(out_send, query_core), "wa", 1)
+    out_near = out_keep + out_core.astype(jnp.float32)
     out_moved = flip(out_near[rows:].astype(jnp.bfloat16), "wa", 2)
     out_own = out_near[:rows] + out_moved.astype(jnp.float32)
     block_out = (residual + out_own).astype(jnp.bfloat16).reshape(tokens.shape)
-    near_three = side_sum(keep_three, other_three) + 0.0 * near_two[0, 0, 0, 0].astype(jnp.float32)
+    near_three = side_sum(keep_three, after(other_three, out_core)) + 0.0 * near_two[0, 0, 0, 0].astype(jnp.float32)
     near_three = near_three.astype(jnp.bfloat16)
     sum_three = scatter_lines(near_three)
     received = after(received, near_three)

time: 675 us -> 726 us (1.076)
  waiting for transfers between devices: 279 us -> 342 us
  local copies, waits for them, and re-layouts: 67.1 us -> 56.6 us
    ppermute x39, waiting for transfers between devices: 174 us -> 230 us  [flip(): return lax.ppermute(value, axis, [(i, i ^ bits) for i in range(count)])]
    ppermute x15, waiting for transfers between devices: 98.9 us -> 109 us  [shift(): lax.ppermute(value, 'ctx', [(i, (i + 2 * steps) % count) for i in range(c...]
    unnamed x196 -> x154, local copies, waits for them, and re-layouts: 22.8 us -> 20.4 us
  transfers between devices with their start and end apart: 62 -> 62, of which waited for: 28 -> 33; matrix products, arithmetic and copies ran while one was open for 23% -> 19% of each run, Pallas kernels for 14% -> 14%
where the time goes in v7:
time: 726 us; the launch traced here: 722 us
  waiting for transfers between devices  342 us (47%)
  Pallas kernels  140 us (19%)
  other arithmetic  68 us (9%)
  starting transfers between devices  62 us (9%)
  local copies, waits for them, and re-layouts  56.6 us (8%)
  matrix products  34 us (5%)
  between operations  18.4 us (3%)
    ppermute x39, waiting for transfers between devices, flip(): return lax.ppermute(value, axis, [(i, i ^ bits) for i in range(count)])  230 us
    ppermute x15, waiting for transfers between devices, shift(): lax.ppermute(value, 'ctx', [(i, (i + 2 * steps) % count) for i in range(c...  109 us
    pallas_call x2, Pallas kernels, experts_call(): pl.pallas_call(functools.partial(experts_kernel, final), grid_spec=pltpu....  102 us
    ppermute x39, starting transfers between devices, flip(): return lax.ppermute(value, axis, [(i, i ^ bits) for i in range(count)])  32.2 us
    pallas_call x1, Pallas kernels, attention_backward(): pl.pallas_call(attention_backward_kernel, grid_spec=pltpu.PrefetchScalarG...  21.5 us
    unnamed x154, local copies, waits for them, and re-layouts  20.4 us
    ppermute x15, starting transfers between devices, shift(): lax.ppermute(value, 'ctx', [(i, (i + 2 * steps) % count) for i in range(c...  18.1 us
    dot_general x9, matrix products, dot32(): lax.dot_general(left, right, (dims, ((), ())), preferred_element_type=jnp...  17.8 us
  transfers between devices with their start and end apart: 62, of which 33 were waited for; matrix products, arithmetic and copies ran while one was open for 19% of the time, Pallas kernels for 14%

profile of v7, /device:TPU:10, one launch (start us, length us, event | category | flops | bytes accessed | tf_op | source)
XLA Modules:
  0.0 721.6 jit_solution(14383286718029994387)
XLA Ops:
  12.7 20.9 %collective-permute-done.1 = bf16[384,1152]{0,1:T(8,128)(2,1)S(1)} collective-permute-done((bf16[384,1152]{0,1:T(8,128)(2,1)S(1)}, bf16[384,1152]{0,1:T(8,128)(2,1)S(1)}, u32[]{:S(2)}, u32[]{:S(2)}) %collective-permute-start.1) | collective-permute-done | bytes 884768 | tf_op jit(solution)/shard_map/ppermute | solution.py:30
  48.6 11.0 %collective-permute-done.3 = bf16[2,128,1024]{2,1,0:T(8,128)(2,1)} collective-permute-done((bf16[2,128,1024]{2,1,0:T(8,128)(2,1)}, bf16[2,128,1024]{2,1,0:T(8,128)(2,1)}, u32[]{:S(2)}, u32[]{:S(2)}) %collective-permute-start.3) | collective-permute-done | bytes 524320 | tf_op jit(solution)/shard_map/ppermute | solution.py:35
  77.6 9.3 %collective-permute-done.4 = s32[256,6]{0,1:T(8,128)S(1)} collective-permute-done((s32[256,6]{0,1:T(8,128)S(1)}, s32[256,6]{0,1:T(8,128)S(1)}, u32[]{:S(2)}, u32[]{:S(2)}) %collective-permute-start.4) | collective-permute-done | bytes 6176 | tf_op jit(solution)/shard_map/ppermute | solution.py:30
  91.2 5.9 all-to-all-start
  103.8 8.9 %collective-permute-done.12 = bf16[2,128,1024]{2,1,0:T(8,128)(2,1)} collective-permute-done((bf16[2,128,1024]{2,1,0:T(8,128)(2,1)}, bf16[2,128,1024]{2,1,0:T(8,128)(2,1)}, u32[]{:S(2)}, u32[]{:S(2)}) %collective-permute-start.12) | collective-permute-done | bytes 524320 | tf_op jit(solution)/shard_map/ppermute | solution.py:30
  118.3 17.0 %attention_forward.1 = (bf16[256,1536]{1,0:T(8,128)(2,1)S(1)}, f32[4,2,384,128]{3,2,1,0:T(8,128)S(1)}) custom-call(s32[8]{0:T(128)S(1)} %bitcast.314, s32[1]{0:T(128)} %bitcast.2.own_ref, bf16[256,1536]{1,0:T(8,128)(2,1)S(1)} %convolution_convert_fusion.q_ref, bf16[16,128,1024]{2,1,0:T(8,128)(2,1)} %constant_dynamic-update-slice_fusion.4.kv_ref), custom_call_target="tpu_custom_call" | custom-call | bytes 1048576 | tf_op jit(solution)/shard_map/attention_forward/pallas_call | solution.py:224
  145.4 16.4 %collective-permute-done.16.refs_2_ = bf16[256,1536]{1,0:T(8,128)(2,1)} collective-permute-done((bf16[256,1536]{1,0:T(8,128)(2,1)S(1)}, bf16[256,1536]{1,0:T(8,128)(2,1)}, u32[]{:S(2)}, u32[]{:S(2)}) %collective-permute-start.16) | collective-permute-done | bytes 786464 | tf_op jit(solution)/shard_map/ppermute | solution.py:30
  167.1 42.4 %experts.1 = (f32[1024,1536]{1,0:T(8,128)}, f32[1024,1536]{1,0:T(8,128)}, f32[1024,16]{1,0:T(8,128)}, bf16[4,2,3,192,512]{4,3,2,1,0:T(8,128)(2,1)}, bf16[4,3,192...) custom-call(s32[2]{0:T(128)} %pad_add_fusion.1.refs_0_, bf16[256,1536]{1,0:T(8,128)(2,1)} %copy-done.4, ...), custom_call_target="tpu_custom_call" | custom-call | bytes 1048576 | tf_op jit(solution)/shard_map/experts/pallas_call | solution.py:555
  212.0 59.3 %experts_final.1 = (f32[512,1536]{1,0:T(8,128)}, f32[512,1536]{1,0:T(8,128)}, bf16[512,1536]{1,0:T(8,128)(2,1)}, bf16[512,1536]{1,0:T(8,128)(2,1)}, f32[1024,16]...) custom-call(s32[2]{0:T(128)} %pad_add_fusion.refs_0_, ...), custom_call_target="tpu_custom_call" | custom-call | bytes 1048576 | tf_op jit(solution)/shard_map/experts_final/pallas_call | solution.py:555
  282.0 18.1 %collective-permute-done.25 = f32[256,16]{1,0:T(8,128)S(1)} collective-permute-done((f32[256,16]{1,0:T(8,128)S(1)}, f32[256,16]{1,0:T(8,128)S(1)}, u32[]{:S(2)}, u32[]{:S(2)}) %collective-permute-start.25) | collective-permute-done | bytes 16416 | tf_op jit(solution)/shard_map/ppermute | solution.py:30
  300.3 25.0 %collective-permute-done.23 = bf16[4,3,192,512]{3,2,1,0:T(8,128)(2,1)S(1)} collective-permute-done((bf16[4,3,192,512]{3,2,1,0:T(8,128)(2,1)}, bf16[4,3,192,512]{3,2,1,0:T(8,128)(2,1)S(1)}, u32[]{:S(2)}, u32[]{:S(2)}) %collective-permute-start.23) | collective-permute-done | bytes 2359328 | tf_op jit(solution)/shard_map/ppermute | solution.py:30
  343.0 21.5 %attention_backward.1 = (bf16[256,1536]{1,0:T(8,128)(2,1)}, bf16[8,128,1024]{2,1,0:T(8,128)(2,1)}, bf16[8,128,1024]{2,1,0:T(8,128)(2,1)}) custom-call(s32[8]{0:T(128)} %bitcast.313, s32[1]{0:T(128)} %bitcast.2.own_ref, bf16[256,1536]{1,0:T(8,128)(2,1)} %copy-done, bf16[256,1536]{1,0:T(8,128)(2,1)} %fusion.19.do_ref, ...), custom_call_target="tpu_custom_call" | custom-call | bytes 1048576 | tf_op jit(solution)/shard_map/attention_backward/pallas_call | solution.py:324
  366.2 17.8 %collective-permute-done.26 = bf16[256,1536]{1,0:T(8,128)(2,1)S(1)} collective-permute-done((bf16[256,1536]{1,0:T(8,128)(2,1)}, bf16[256,1536]{1,0:T(8,128)(2,1)S(1)}, u32[]{:S(2)}, u32[]{:S(2)}) %collective-permute-start.26) | collective-permute-done | bytes 786464 | tf_op jit(solution)/shard_map/ppermute | solution.py:30
  405.1 34.5 %collective-permute-done.30 = bf16[4,3,192,512]{3,2,1,0:T(8,128)(2,1)} collective-permute-done((bf16[4,3,192,512]{3,2,1,0:T(8,128)(2,1)}, bf16[4,3,192,512]{3,2,1,0:T(8,128)(2,1)}, u32[]{:S(2)}, u32[]{:S(2)}) %collective-permute-start.30) | collective-permute-done | bytes 2359328 | tf_op jit(solution)/shard_map/ppermute | solution.py:30
  463.9 38.3 %collective-permute-done.35 = bf16[4,256,1024]{2,1,0:T(8,128)(2,1)S(1)} collective-permute-done((bf16[4,256,1024]{2,1,0:T(8,128)(2,1)}, bf16[4,256,1024]{2,1,0:T(8,128)(2,1)S(1)}, u32[]{:S(2)}, u32[]{:S(2)}) %collective-permute-start.35) | collective-permute-done | bytes 2097184 | tf_op jit(solution)/shard_map/ppermute | solution.py:30
  517.1 12.3 %collective-permute-done.29 = bf16[256,1536]{1,0:T(8,128)(2,1)} collective-permute-done((bf16[256,1536]{1,0:T(8,128)(2,1)}, bf16[256,1536]{1,0:T(8,128)(2,1)}, u32[]{:S(2)}, u32[]{:S(2)}) %collective-permute-start.29) | collective-permute-done | bytes 786464 | tf_op jit(solution)/shard_map/ppermute | solution.py:30
  531.1 18.8 %collective-permute-done.36 = bf16[256,1024]{1,0:T(8,128)(2,1)} collective-permute-done((bf16[256,1024]{1,0:T(8,128)(2,1)}, bf16[256,1024]{1,0:T(8,128)(2,1)}, u32[]{:S(2)}, u32[]{:S(2)}) %collective-permute-start.36) | collective-permute-done | bytes 524320 | tf_op jit(solution)/shard_map/ppermute | solution.py:35
  549.9 6.4 collective-permute-done.39
  556.4 38.3 %collective-permute-done.38 = bf16[256,1024]{1,0:T(8,128)(2,1)} collective-permute-done((bf16[256,1024]{1,0:T(8,128)(2,1)}, bf16[256,1024]{1,0:T(8,128)(2,1)}, u32[]{:S(2)}, u32[]{:S(2)}) %collective-permute-start.38) | collective-permute-done | bytes 524320 | tf_op jit(solution)/shard_map/ppermute | solution.py:35
  622.0 6.5 collective-permute-done.43
  650.1 6.6 collective-permute-done.47
  656.7 12.2 %collective-permute-done.46 = bf16[48,1024]{0,1:T(8,128)(2,1)} collective-permute-done((bf16[48,1024]{0,1:T(8,128)(2,1)}, bf16[48,1024]{0,1:T(8,128)(2,1)}, u32[]{:S(2)}, u32[]{:S(2)}) %collective-permute-start.46) | collective-permute-done | bytes 98336 | tf_op jit(solution)/shard_map/ppermute | solution.py:35
  675.6 5.7 collective-permute-done.51
  701.3 7.1 collective-permute-done.53
  (400 shorter events, 242.9 us)
Async XLA Ops:
  7.2 107.4 %all-gather.4.cloned.1.call-start = ((), (), s32[]{:S(2)}) async-start(), calls=%async_computation.6 | async-start | bytes 5898240 | tf_op jit(solution)/shard_map/all_gather | solution.py:621
  33.6 102.9 %all-gather.6.cloned.1.call-start = ((), (), s32[]{:S(2)}) async-start(), calls=%async_computation.11 | async-start | bytes 5898240 | tf_op jit(solution)/shard_map/all_gather | solution.py:622
  69.4 73.1 %collective-permute-start.14 = (bf16[256,1536]{1,0:T(8,128)(2,1)}, bf16[256,1536]{1,0:T(8,128)(2,1)}, u32[]{:S(2)}, u32[]{:S(2)}) collective-permute-start(bf16[256,1536]{1,0:T(8,128)(2,1)} %bitcast.17.refs_5_), channel_id=1, source_target_pairs={{0,1},{1,0},{2,3},{3,2},{4,5},{5,4},{6,7},{7,6},{8,9},{9,8},{10,11... | collective-permute-start | bytes 2359304 | tf_op jit(solution)/shard_map/ppermute | solution.py:30
  91.2 51.3 %collective-permute-start.15 = (bf16[256,1536]{1,0:T(8,128)(2,1)}, bf16[256,1536]{1,0:T(8,128)(2,1)}, u32[]{:S(2)}, u32[]{:S(2)}) collective-permute-start(bf16[256,1536]{1,0:T(8,128)(2,1)} %collective-permute-done.13.refs_6_), channel_id=1, source_target_pairs={{0,1},{1,0},{2,3},{3,2},{4,5},{5,4},{6,7},{7,6},{8,9},{9,8},{10,11... | collective-permute-start | bytes 2359304 | tf_op jit(solution)/shard_map/ppermute | solution.py:30
  91.2 51.3 %all-to-all-start = ((bf16[4,384,768]{2,1,0:T(8,128)(2,1)}), bf16[4,384,768]{2,1,0:T(8,128)(2,1)}, u32[]{:S(2)}, u32[]{:S(2)}) async-start(bf16[4,384,768]{2,1,0:T(8,128)(2,1)} %maximum_bitcast_fusion), calls=%async_computation | async-start | bytes 4718592 | tf_op jit(solution)/shard_map/all_to_all | solution.py:648
  97.1 234.4 %reduce-scatter.5.cloned.1.call-start = ((), (), s32[]{:S(2)}) async-start(), calls=%async_computation.7 | async-start | bytes 5898240 | tf_op jit(solution)/shard_map/reduce_scatter | solution.py:103
  209.6 230.8 %reduce-scatter.7.cloned.1.call-start = ((), (), s32[]{:S(2)}) async-start(), calls=%async_computation.8 | async-start | bytes 2949120 | tf_op jit(solution)/shard_map/reduce_scatter | solution.py:103
  209.6 61.8 %collective-permute-start.19 = (bf16[4,3,192,512]{3,2,1,0:T(8,128)(2,1)}, bf16[4,3,192,512]{3,2,1,0:T(8,128)(2,1)}, u32[]{:S(2)}, u32[]{:S(2)}) collective-permute-start(bf16[4,3,192,512]{3,2,1,0:T(8,128)(2,1)} %get-tuple-element.84), channel_id=1, source_target_pairs={{0,4},{4,0},{8,12},{12,8},{16,20},{20,16},{24,28},{28,24},{1,5},{5... | collective-permute-start | bytes 7077896 | tf_op jit(solution)/shard_map/ppermute | solution.py:30
  211.1 60.2 %collective-permute-start.20 = (bf16[256,1536]{1,0:T(8,128)(2,1)S(1)}, bf16[256,1536]{1,0:T(8,128)(2,1)S(1)}, u32[]{:S(2)}, u32[]{:S(2)}) collective-permute-start(bf16[256,1536]{1,0:T(8,128)(2,1)S(1)} %get-tuple-element.85), channel_id=1, source_target_pairs={{0,2},{1,3},{2,0},{3,1},{4,6},{5,7},{6,4},{7,5},{8,10},{9,11},{10,... | collective-permute-start | bytes 2359304 | tf_op jit(solution)/shard_map/ppermute | solution.py:30
  271.5 53.9 %collective-permute-start.23 = (bf16[4,3,192,512]{3,2,1,0:T(8,128)(2,1)}, bf16[4,3,192,512]{3,2,1,0:T(8,128)(2,1)S(1)}, u32[]{:S(2)}, u32[]{:S(2)}) collective-permute-start(bf16[4,3,192,512]{3,2,1,0:T(8,128)(2,1)} %get-tuple-element.87), channel_id=1, source_target_pairs={{0,4},{4,0},{8,12},{12,8},{16,20},{20,16},{24,28},{28,24},{1,5},{5... | collective-permute-start | bytes 7077896 | tf_op jit(solution)/shard_map/ppermute | solution.py:30
  277.6 47.7 %collective-permute-start.22 = (bf16[256,1536]{1,0:T(8,128)(2,1)S(1)}, bf16[256,1536]{1,0:T(8,128)(2,1)S(1)}, u32[]{:S(2)}, u32[]{:S(2)}) collective-permute-start(bf16[256,1536]{1,0:T(8,128)(2,1)S(1)} %slice.433), channel_id=1, source_target_pairs={{0,2},{1,3},{2,0},{3,1},{4,6},{5,7},{6,4},{7,5},{8,10},{9,11},{10,... | collective-permute-start | bytes 2359304 | tf_op jit(solution)/shard_map/ppermute | solution.py:30
  337.8 352.1 %reduce-scatter.9.cloned.1.call-start = ((), (), s32[]{:S(2)}) async-start(), calls=%async_computation.9 | async-start | bytes 2949120 | tf_op jit(solution)/shard_map/reduce_scatter | solution.py:103
  385.6 54.0 %collective-permute-start.30 = (bf16[4,3,192,512]{3,2,1,0:T(8,128)(2,1)}, bf16[4,3,192,512]{3,2,1,0:T(8,128)(2,1)}, u32[]{:S(2)}, u32[]{:S(2)}) collective-permute-start(bf16[4,3,192,512]{3,2,1,0:T(8,128)(2,1)} %get-tuple-element.100), channel_id=1, source_target_pairs={{0,4},{4,0},{8,12},{12,8},{16,20},{20,16},{24,28},{28,24},{1,5},{5... | collective-permute-start | bytes 7077896 | tf_op jit(solution)/shard_map/ppermute | solution.py:30
  390.2 50.1 %collective-permute-start.28 = (bf16[512,1536]{1,0:T(8,128)(2,1)}, bf16[512,1536]{1,0:T(8,128)(2,1)}, u32[]{:S(2)}, u32[]{:S(2)}) collective-permute-start(bf16[512,1536]{1,0:T(8,128)(2,1)} %get-tuple-element.96), channel_id=1, source_target_pairs={{0,1},{1,0},{2,3},{3,2},{4,5},{5,4},{6,7},{7,6},{8,9},{9,8},{10,11... | collective-permute-start | bytes 4718600 | tf_op jit(solution)/shard_map/ppermute | solution.py:30
  400.4 53.2 %collective-permute-start.34 = (bf16[512,1536]{1,0:T(8,128)(2,1)}, bf16[512,1536]{1,0:T(8,128)(2,1)}, u32[]{:S(2)}, u32[]{:S(2)}) collective-permute-start(bf16[512,1536]{1,0:T(8,128)(2,1)} %pad_maximum_fusion.4), channel_id=1, source_target_pairs={{0,1},{1,0},{2,3},{3,2},{4,5},{5,4},{6,7},{7,6},{8,9},{9,8},{10,11... | collective-permute-start | bytes 4718600 | tf_op jit(solution)/shard_map/ppermute | solution.py:30
  403.6 50.0 %collective-permute-start.31 = (bf16[640,384]{0,1:T(8,128)(2,1)}, bf16[640,384]{0,1:T(8,128)(2,1)}, u32[]{:S(2)}, u32[]{:S(2)}) collective-permute-start(bf16[640,384]{0,1:T(8,128)(2,1)} %get-tuple-element.255), channel_id=1, source_target_pairs={{0,2},{1,3},{2,0},{3,1},{4,6},{5,7},{6,4},{7,5},{8,10},{9,11},{10,... | collective-permute-start | bytes 1474568 | tf_op jit(solution)/shard_map/ppermute | solution.py:30
  405.1 48.5 %collective-permute-start.32 = (bf16[640,384]{0,1:T(8,128)(2,1)}, bf16[640,384]{0,1:T(8,128)(2,1)}, u32[]{:S(2)}, u32[]{:S(2)}) collective-permute-start(bf16[640,384]{0,1:T(8,128)(2,1)} %get-tuple-element.254), channel_id=1, source_target_pairs={{0,1},{1,0},{2,3},{3,2},{4,5},{5,4},{6,7},{7,6},{8,9},{9,8},{10,11... | collective-permute-start | bytes 1474568 | tf_op jit(solution)/shard_map/ppermute | solution.py:30
  453.2 246.8 %reduce-scatter.11.cloned.1.call-start = ((), (), s32[]{:S(2)}) async-start(), calls=%async_computation.10 | async-start | bytes 2949120 | tf_op jit(solution)/shard_map/reduce_scatter | solution.py:103
  453.6 48.7 %collective-permute-start.35 = (bf16[4,256,1024]{2,1,0:T(8,128)(2,1)}, bf16[4,256,1024]{2,1,0:T(8,128)(2,1)S(1)}, u32[]{:S(2)}, u32[]{:S(2)}) collective-permute-start(bf16[4,256,1024]{2,1,0:T(8,128)(2,1)} %bitcast.358), channel_id=1, source_target_pairs={{0,4},{4,0},{8,12},{12,8},{16,20},{20,16},{24,28},{28,24},{1,5},{5... | collective-permute-start | bytes 6291464 | tf_op jit(solution)/shard_map/ppermute | solution.py:30
  506.6 43.4 %collective-permute-start.37 = (bf16[4,48,3200]{2,1,0:T(8,128)(2,1)}, bf16[4,48,3200]{2,1,0:T(8,128)(2,1)}, u32[]{:S(2)}, u32[]{:S(2)}) collective-permute-start(bf16[4,48,3200]{2,1,0:T(8,128)(2,1)} %dynamic-slice_bitcast_fusion), channel_id=1, source_target_pairs={{0,4},{4,0},{8,12},{12,8},{16,20},{20,16},{24,28},{28,24},{1,5},{5... | collective-permute-start | bytes 3686408 | tf_op jit(solution)/shard_map/ppermute | solution.py:30
  512.9 43.5 %collective-permute-start.39 = (bf16[256,1024]{1,0:T(8,128)(2,1)}, bf16[256,1024]{1,0:T(8,128)(2,1)}, u32[]{:S(2)}, u32[]{:S(2)}) collective-permute-start(bf16[256,1024]{1,0:T(8,128)(2,1)} %get-tuple-element.249), channel_id=1, source_target_pairs={{0,8},{4,12},{8,16},{12,20},{16,24},{20,28},{24,0},{28,4},{1,9},{5... | collective-permute-start | bytes 1572872 | tf_op jit(solution)/shard_map/ppermute | solution.py:35
  514.9 79.7 %collective-permute-start.38 = (bf16[256,1024]{1,0:T(8,128)(2,1)}, bf16[256,1024]{1,0:T(8,128)(2,1)}, u32[]{:S(2)}, u32[]{:S(2)}) collective-permute-start(bf16[256,1024]{1,0:T(8,128)(2,1)} %get-tuple-element.250), channel_id=1, source_target_pairs={{0,16},{4,20},{8,24},{12,28},{16,0},{20,4},{24,8},{28,12},{1,17},{... | collective-permute-start | bytes 1572872 | tf_op jit(solution)/shard_map/ppermute | solution.py:35
  529.4 110.0 %collective-permute-start.49 = (bf16[4,3,192,256]{3,2,1,0:T(8,128)(2,1)}, bf16[4,3,192,256]{3,2,1,0:T(8,128)(2,1)}, u32[]{:S(2)}, u32[]{:S(2)}) collective-permute-start(bf16[4,3,192,256]{3,2,1,0:T(8,128)(2,1)} %get-tuple-element.117), channel_id=1, source_target_pairs={{0,4},{4,0},{8,12},{12,8},{16,20},{20,16},{24,28},{28,24},{1,5},{5... | collective-permute-start | bytes 3538952 | tf_op jit(solution)/shard_map/ppermute | solution.py:30
  644.0 37.3 %collective-permute-start.51 = (bf16[3,192,256]{2,1,0:T(8,128)(2,1)}, bf16[3,192,256]{2,1,0:T(8,128)(2,1)}, u32[]{:S(2)}, u32[]{:S(2)}) collective-permute-start(bf16[3,192,256]{2,1,0:T(8,128)(2,1)} %get-tuple-element.264), channel_id=1, source_target_pairs={{0,16},{4,20},{8,24},{12,28},{16,0},{20,4},{24,8},{28,12},{1,17},{... | collective-permute-start | bytes 884744 | tf_op jit(solution)/shard_map/ppermute | solution.py:35
  (108 other events, 1915.6 us)
Sparse Core Ops, SparseCore 0:
  33.7 38.5 all-gather.3
  73.9 53.2 all-gather.5
  209.7 84.4 reduce-scatter.4
  338.0 46.2 reduce-scatter.6
  453.3 45.6 reduce-scatter.8
  515.0 84.0 reduce-scatter.10
